TPU v7x, 32 devices: a whole 2x2x4 slice. The times are simulated.
32 devices in a mesh: gx: 4 (over z), gy: 4 (over y, core), gz: 2 (over x).
Axes of the slice: x: 2, y: 2, z: 4, core: 2. Of those that a mesh axis runs over, the one named last changes fastest.
Arguments:
- charges: float32 [64, 64, 256], P('gx', 'gy', 'gz'), may hold values from -6 to 6
- exponents: float32 [2, 4], replicated, may hold values from 0.01 to 1
- amplitudes: float32 [2, 4], replicated, may hold values from 0.25 to 1
- top_x: float32 [4, 4], replicated, may hold values from -1.5 to 1.5
- top_y: float32 [4, 4], replicated, may hold values from -1.5 to 1.5
- top_z: float32 [16, 16], replicated, may hold values from -0.75 to 0.75
Outputs:
- potential: float32 [64, 64, 256], P('gx', 'gy', 'gz')
All inputs are finite; a program needn't handle non-finite values.
Results may differ from a plain program's by a relative error of at most 0.0003.
Values sent between devices are 32-bit elements; how exact they have to be, the bound alone decides.
No kernel may reach another device: no remote copies, remote signals or barrier semaphores. Data moves between devices by JAX's collectives and lax.ppermute only.
A program may use at most 64 MiB of HBM per device.

v0:
```python
import jax
import jax.numpy as jnp
from jax import lax
from jax.sharding import PartitionSpec as P

REACH = 8


HIGHEST = lax.Precision.HIGHEST


def with_halo(cells, sides, width):
    for axis, dim in sides:
        count = lax.axis_size(axis)
        head = lax.slice_in_dim(cells, 0, width, axis=dim)
        tail = lax.slice_in_dim(cells, cells.shape[dim] - width, cells.shape[dim], axis=dim)
        cells = jnp.concatenate(
            [
                lax.ppermute(tail, axis, [(i, (i + 1) % count) for i in range(count)]),
                cells,
                lax.ppermute(head, axis, [((i + 1) % count, i) for i in range(count)]),
            ],
            axis=dim,
        )
    return cells


def gauss_taps(exponents):
    offsets = jnp.arange(-REACH, REACH + 1).astype(jnp.float32)
    weights = jnp.exp(-exponents[..., None] * offsets * offsets)
    return weights / jnp.sum(weights, axis=-1, keepdims=True)


def spline(offsets):
    inner_weight = jnp.where((offsets == 1) | (offsets == 2), 0.75, 0.0)
    return jnp.where((offsets == 0) | (offsets == 3), 0.25, inner_weight).astype(jnp.float32)


def band_gauss(tap_table, length):
    rows = jnp.arange(length + 2 * REACH)[:, None]
    cols = jnp.arange(length)[None, :]
    offsets = rows - cols
    onehot = (offsets[:, :, None] == jnp.arange(2 * REACH + 1)[None, None, :]).astype(jnp.float32)
    return jnp.einsum("gk,pok->gpo", tap_table, onehot, precision=HIGHEST)


def band_restrict(length):
    rows = jnp.arange(length + 2)[:, None]
    cols = jnp.arange(length // 2)[None, :]
    return spline(rows - 2 * cols)


def band_prolong(length):
    rows = jnp.arange(length + 2)[:, None]
    cols = jnp.arange(2 * length)[None, :]
    return spline(cols - 2 * rows + 3)


def apply_three(field, band_x, band_y, band_z):
    field = jnp.einsum("xyz,zc->xyc", field, band_z, precision=HIGHEST)
    field = jnp.einsum("xyz,yb->xbz", field, band_y, precision=HIGHEST)
    return jnp.einsum("xyz,xa->ayz", field, band_x, precision=HIGHEST)


def rim_cells(field):
    return with_halo(field, (("gx", 0), ("gy", 1), ("gz", 2)), 1)


def restrict_local(padded):
    sizes = padded.shape
    return apply_three(
        padded,
        band_restrict(sizes[0] - 2),
        band_restrict(sizes[1] - 2),
        band_restrict(sizes[2] - 2),
    )


def prolong_local(field):
    sizes = field.shape
    return apply_three(
        rim_cells(field), band_prolong(sizes[0]), band_prolong(sizes[1]), band_prolong(sizes[2])
    )


def prolong_from_whole(whole_grid, brick):
    padded = jnp.pad(whole_grid, 1, mode="wrap")
    starts = (
        lax.axis_index("gx") * brick[0],
        lax.axis_index("gy") * brick[1],
        lax.axis_index("gz") * brick[2],
    )
    piece_cells = lax.dynamic_slice(padded, starts, (brick[0] + 2, brick[1] + 2, brick[2] + 2))
    return apply_three(
        piece_cells, band_prolong(brick[0]), band_prolong(brick[1]), band_prolong(brick[2])
    )


def assemble(gathered, brick):
    count_x = lax.axis_size("gx")
    count_y = lax.axis_size("gy")
    count_z = lax.axis_size("gz")
    blocks = gathered.reshape(count_x, count_y, count_z, brick[0], brick[1], brick[2])
    blocks = jnp.transpose(blocks, (0, 3, 1, 4, 2, 5))
    return blocks.reshape(count_x * brick[0], count_y * brick[1], count_z * brick[2])


def top_level(field, top_x, top_y, top_z):
    field = jnp.einsum("ia,abc->ibc", top_x, field, precision=HIGHEST)
    field = jnp.einsum("jb,ibc->ijc", top_y, field, precision=HIGHEST)
    return jnp.einsum("kc,ijc->ijk", top_z, field, precision=HIGHEST)


def gauss_and_restrict(field, tap_table, weights):
    size_x, size_y, size_z = field.shape
    band_z = band_gauss(tap_table, size_z)
    band_y = band_gauss(tap_table, size_y)
    band_x = band_gauss(tap_table, size_x) * weights[:, None, None]
    padded = with_halo(field, (("gx", 0), ("gy", 1), ("gz", 2)), REACH)
    along_z = jnp.einsum("xyp,gpo->xygo", padded, band_z, precision=HIGHEST)
    along_y = jnp.einsum("xpgz,gpw->xgwz", along_z, band_y, precision=HIGHEST)
    result = jnp.einsum("pgwz,gpv->vwz", along_y, band_x, precision=HIGHEST)
    inner_cells = padded[
        REACH - 1 : size_x + REACH + 1,
        REACH - 1 : size_y + REACH + 1,
        REACH - 1 : size_z + REACH + 1,
    ]
    coarse = restrict_local(inner_cells)
    return (result, coarse)


def local(charges, exponents, amplitudes, top_x, top_y, top_z):
    tap_table = gauss_taps(exponents)
    term_zero, level_one = gauss_and_restrict(charges, tap_table[0], amplitudes[0])
    term_one, level_two = gauss_and_restrict(level_one, tap_table[1], amplitudes[1])
    level_three = restrict_local(rim_cells(level_two))
    level_four = restrict_local(rim_cells(level_three))
    brick_four = level_four.shape
    gathered = lax.all_gather(level_four.reshape(1, -1), ("gx", "gy", "gz"), axis=0, tiled=True)
    phi_four = top_level(assemble(gathered, brick_four), top_x, top_y, top_z)
    phi_three = prolong_from_whole(phi_four, brick_four)
    phi_two = prolong_local(phi_three)
    phi_one = term_one + prolong_local(phi_two)
    return term_zero + prolong_local(phi_one)


def solution(mesh):
    in_specs = (P("gx", "gy", "gz"), P(), P(), P(), P(), P())
    out_specs = P("gx", "gy", "gz")
    return jax.shard_map(local, mesh=mesh, in_specs=in_specs, out_specs=out_specs, check_vma=False)
```

profile of v0, /device:TPU:0, one launch (start us, length us, event | category | flops | bytes accessed | tf_op | source)
XLA Modules:
  0.0 186.5 jit_solution(1475320691596579053)
XLA Ops:
  0.9 3.1 %collective-permute-start = (f32[8,16,128]{2,1,0:T(8,128)S(1)}, f32[8,16,128]{2,1,0:T(8,128)S(1)}, u32[]{:S(2)}, u32[]{:S(2)}) collective-permute-start(f32[8,16,128]{2,1,0:T(8,128)S(1)} %get-tuple-element.12), channel_id=1, source_target_pairs={{0,8},{8,16},{16,24},{24,0},{1,9},{9,17},{17,25},{25,1},{2,10},{10... | collective-permute-start | bytes 196616 | tf_op jit(solution)/shard_map/ppermute | solution.py:19
  4.0 2.1 %collective-permute-start.1 = (f32[8,16,128]{2,1,0:T(8,128)S(1)}, f32[8,16,128]{2,1,0:T(8,128)S(1)}, u32[]{:S(2)}, u32[]{:S(2)}) collective-permute-start(f32[8,16,128]{2,1,0:T(8,128)S(1)} %get-tuple-element.11), channel_id=1, source_target_pairs={{8,0},{16,8},{24,16},{0,24},{9,1},{17,9},{25,17},{1,25},{10,2},{18... | collective-permute-start | bytes 196616 | tf_op jit(solution)/shard_map/ppermute | solution.py:21
  9.5 1.7 collective-permute-start.3
  11.6 2.3 %collective-permute-done.2 = f32[32,8,128]{2,1,0:T(8,128)S(1)} collective-permute-done((f32[32,8,128]{2,1,0:T(8,128)S(1)}, f32[32,8,128]{2,1,0:T(8,128)S(1)}, u32[]{:S(2)}, u32[]{:S(2)}) %collective-permute-start.2) | collective-permute-done | bytes 131104 | tf_op jit(solution)/shard_map/ppermute | solution.py:19
  16.9 12.5 %collective-permute-done.4 = f32[32,32,8]{2,1,0:T(8,128)S(1)} collective-permute-done((f32[32,32,8]{2,1,0:T(8,128)S(1)}, f32[32,32,8]{2,1,0:T(8,128)S(1)}, u32[]{:S(2)}, u32[]{:S(2)}) %collective-permute-start.4) | collective-permute-done | bytes 32800 | tf_op jit(solution)/shard_map/ppermute | solution.py:19
  29.4 11.2 %collective-permute-done.5 = f32[32,32,8]{2,1,0:T(8,128)S(1)} collective-permute-done((f32[32,32,8]{2,1,0:T(8,128)S(1)}, f32[32,32,8]{2,1,0:T(8,128)S(1)}, u32[]{:S(2)}, u32[]{:S(2)}) %collective-permute-start.5) | collective-permute-done | bytes 32800 | tf_op jit(solution)/shard_map/ppermute | solution.py:21
  42.8 3.3 %collective-permute-start.7 = (f32[8,8,64]{2,0,1:T(8,128)S(1)}, f32[8,8,64]{2,0,1:T(8,128)S(1)}, u32[]{:S(2)}, u32[]{:S(2)}) collective-permute-start(f32[8,8,64]{2,0,1:T(8,128)S(1)} %fusion.18), channel_id=1, source_target_pairs={{8,0},{16,8},{24,16},{0,24},{9,1},{17,9},{25,17},{1,25},{10,2},{18... | collective-permute-start | bytes 49160 | tf_op jit(solution)/shard_map/ppermute | solution.py:21
  46.1 2.0 %collective-permute-done.6 = f32[8,8,64]{2,0,1:T(8,128)S(1)} collective-permute-done((f32[8,8,64]{2,0,1:T(8,128)S(1)}, f32[8,8,64]{2,0,1:T(8,128)S(1)}, u32[]{:S(2)}, u32[]{:S(2)}) %collective-permute-start.6) | collective-permute-done | bytes 16416 | tf_op jit(solution)/shard_map/ppermute | solution.py:19
  48.3 1.7 collective-permute-start.9
  50.0 2.3 %collective-permute-done.8 = f32[24,8,64]{2,0,1:T(8,128)S(1)} collective-permute-done((f32[24,8,64]{2,0,1:T(8,128)S(1)}, f32[24,8,64]{2,0,1:T(8,128)S(1)}, u32[]{:S(2)}, u32[]{:S(2)}) %collective-permute-start.8) | collective-permute-done | bytes 49184 | tf_op jit(solution)/shard_map/ppermute | solution.py:19
  54.6 7.3 %collective-permute-done.10 = f32[24,24,8]{2,0,1:T(8,128)S(1)} collective-permute-done((f32[24,24,8]{2,0,1:T(8,128)S(1)}, f32[24,24,8]{2,0,1:T(8,128)S(1)}, u32[]{:S(2)}, u32[]{:S(2)}) %collective-permute-start.10) | collective-permute-done | bytes 18464 | tf_op jit(solution)/shard_map/ppermute | solution.py:19
  61.9 6.3 %collective-permute-done.11 = f32[24,24,8]{2,0,1:T(8,128)S(1)} collective-permute-done((f32[24,24,8]{2,0,1:T(8,128)S(1)}, f32[24,24,8]{2,0,1:T(8,128)S(1)}, u32[]{:S(2)}, u32[]{:S(2)}) %collective-permute-start.11) | collective-permute-done | bytes 18464 | tf_op jit(solution)/shard_map/ppermute | solution.py:21
  69.4 3.8 %collective-permute-start.13 = (f32[1,4,32]{2,0,1:T(1,128)S(1)}, f32[1,4,32]{2,0,1:T(1,128)S(1)}, u32[]{:S(2)}, u32[]{:S(2)}) collective-permute-start(f32[1,4,32]{2,0,1:T(1,128)S(1)} %get-tuple-element.40), channel_id=1, source_target_pairs={{8,0},{16,8},{24,16},{0,24},{9,1},{17,9},{25,17},{1,25},{10,2},{18... | collective-permute-start | bytes 1544 | tf_op jit(solution)/shard_map/ppermute | solution.py:21
  74.8 1.7 collective-permute-start.15
  80.0 1.8 collective-permute-done.16
  85.2 2.8 %collective-permute-start.19 = (f32[1,2,16]{2,0,1:T(1,128)S(1)}, f32[1,2,16]{2,0,1:T(1,128)S(1)}, u32[]{:S(2)}, u32[]{:S(2)}) collective-permute-start(f32[1,2,16]{2,0,1:T(1,128)S(1)} %get-tuple-element.48), channel_id=1, source_target_pairs={{8,0},{16,8},{24,16},{0,24},{9,1},{17,9},{25,17},{1,25},{10,2},{18... | collective-permute-start | bytes 392 | tf_op jit(solution)/shard_map/ppermute | solution.py:21
  89.6 1.7 collective-permute-start.21
  94.8 1.6 collective-permute-done.22
  97.7 40.8 %all-reduce = f32[256]{0:T(256)S(1)} all-reduce(f32[256]{0:T(256)S(1)} %dynamic-update-slice), channel_id=2, replica_groups=mesh['gx'=4,'gy'=4,'gz'=2] {'gx','gy','gz'}, use_global_device_ids=true, to_apply=%add | all-reduce | flops 256 | bytes 2048
  139.8 1.9 %collective-permute-start.24 = (f32[1,2,16]{2,0,1:T(1,128)S(1)}, f32[1,2,16]{2,0,1:T(1,128)S(1)}, u32[]{:S(2)}, u32[]{:S(2)}) collective-permute-start(f32[1,2,16]{2,0,1:T(1,128)S(1)} %get-tuple-element.45), channel_id=1, source_target_pairs={{0,8},{8,16},{16,24},{24,0},{1,9},{9,17},{17,25},{25,1},{2,10},{10... | collective-permute-start | bytes 392 | tf_op jit(solution)/shard_map/ppermute | solution.py:19
  141.7 2.0 %collective-permute-start.25 = (f32[1,2,16]{2,0,1:T(1,128)S(1)}, f32[1,2,16]{2,0,1:T(1,128)S(1)}, u32[]{:S(2)}, u32[]{:S(2)}) collective-permute-start(f32[1,2,16]{2,0,1:T(1,128)S(1)} %get-tuple-element.46), channel_id=1, source_target_pairs={{8,0},{16,8},{24,16},{0,24},{9,1},{17,9},{25,17},{1,25},{10,2},{18... | collective-permute-start | bytes 392 | tf_op jit(solution)/shard_map/ppermute | solution.py:21
  145.3 1.7 collective-permute-start.27
  148.5 2.3 %collective-permute-start.28 = (f32[4,4,1]{2,0,1:T(4,128)S(1)}, f32[4,4,1]{2,0,1:T(4,128)S(1)}, u32[]{:S(2)}, u32[]{:S(2)}) collective-permute-start(f32[4,4,1]{2,0,1:T(4,128)S(1)} %get-tuple-element.33), channel_id=1, source_target_pairs={{0,1},{1,0},{2,3},{3,2},{4,5},{5,4},{6,7},{7,6},{8,9},{9,8},{10,11... | collective-permute-start | bytes 200 | tf_op jit(solution)/shard_map/ppermute | solution.py:19
  152.4 2.0 %collective-permute-done.29 = f32[4,4,1]{2,0,1:T(4,128)S(1)} collective-permute-done((f32[4,4,1]{2,0,1:T(4,128)S(1)}, f32[4,4,1]{2,0,1:T(4,128)S(1)}, u32[]{:S(2)}, u32[]{:S(2)}) %collective-permute-start.29) | collective-permute-done | bytes 96 | tf_op jit(solution)/shard_map/ppermute | solution.py:21
  156.5 2.4 %collective-permute-start.31 = (f32[1,4,32]{2,0,1:T(1,128)S(1)}, f32[1,4,32]{2,0,1:T(1,128)S(1)}, u32[]{:S(2)}, u32[]{:S(2)}) collective-permute-start(f32[1,4,32]{2,0,1:T(1,128)S(1)} %get-tuple-element.32), channel_id=1, source_target_pairs={{8,0},{16,8},{24,16},{0,24},{9,1},{17,9},{25,17},{1,25},{10,2},{18... | collective-permute-start | bytes 1544 | tf_op jit(solution)/shard_map/ppermute | solution.py:21
  160.6 1.7 collective-permute-start.33
  163.8 1.9 %collective-permute-start.35 = (f32[6,6,1]{2,0,1:T(8,128)S(1)}, f32[6,6,1]{2,0,1:T(8,128)S(1)}, u32[]{:S(2)}, u32[]{:S(2)}) collective-permute-start(f32[6,6,1]{2,0,1:T(8,128)S(1)} %get-tuple-element.20), channel_id=1, source_target_pairs={{1,0},{0,1},{3,2},{2,3},{5,4},{4,5},{7,6},{6,7},{9,8},{8,9},{11,10... | collective-permute-start | bytes 440 | tf_op jit(solution)/shard_map/ppermute | solution.py:21
  169.6 3.0 %collective-permute-start.37 = (f32[1,8,64]{2,0,1:T(1,128)S(1)}, f32[1,8,64]{2,0,1:T(1,128)S(1)}, u32[]{:S(2)}, u32[]{:S(2)}) collective-permute-start(f32[1,8,64]{2,0,1:T(1,128)S(1)} %get-tuple-element.18), channel_id=1, source_target_pairs={{8,0},{16,8},{24,16},{0,24},{9,1},{17,9},{25,17},{1,25},{10,2},{18... | collective-permute-start | bytes 6152 | tf_op jit(solution)/shard_map/ppermute | solution.py:21
  172.6 1.8 fusion.5
  174.7 1.6 collective-permute-start.39
  177.8 1.8 collective-permute-start.40
  182.4 2.5 %collective-permute-done.41 = f32[10,10,1]{2,0,1:T(8,128)S(1)} collective-permute-done((f32[10,10,1]{2,0,1:T(8,128)S(1)}, f32[10,10,1]{2,0,1:T(8,128)S(1)}, u32[]{:S(2)}, u32[]{:S(2)}) %collective-permute-start.41) | collective-permute-done | bytes 432 | tf_op jit(solution)/shard_map/ppermute | solution.py:21
  (170 shorter events, 48.9 us)
Async XLA Ops:
  0.9 8.4 %collective-permute-start = (f32[8,16,128]{2,1,0:T(8,128)S(1)}, f32[8,16,128]{2,1,0:T(8,128)S(1)}, u32[]{:S(2)}, u32[]{:S(2)}) collective-permute-start(f32[8,16,128]{2,1,0:T(8,128)S(1)} %get-tuple-element.12), channel_id=1, source_target_pairs={{0,8},{8,16},{16,24},{24,0},{1,9},{9,17},{17,25},{25,1},{2,10},{10... | collective-permute-start | bytes 196616 | tf_op jit(solution)/shard_map/ppermute | solution.py:19
  4.0 5.4 %collective-permute-start.1 = (f32[8,16,128]{2,1,0:T(8,128)S(1)}, f32[8,16,128]{2,1,0:T(8,128)S(1)}, u32[]{:S(2)}, u32[]{:S(2)}) collective-permute-start(f32[8,16,128]{2,1,0:T(8,128)S(1)} %get-tuple-element.11), channel_id=1, source_target_pairs={{8,0},{16,8},{24,16},{0,24},{9,1},{17,9},{25,17},{1,25},{10,2},{18... | collective-permute-start | bytes 196616 | tf_op jit(solution)/shard_map/ppermute | solution.py:21
  9.5 4.4 %collective-permute-start.2 = (f32[32,8,128]{2,1,0:T(8,128)S(1)}, f32[32,8,128]{2,1,0:T(8,128)S(1)}, u32[]{:S(2)}, u32[]{:S(2)}) collective-permute-start(f32[32,8,128]{2,1,0:T(8,128)S(1)} %get-tuple-element.9), channel_id=1, source_target_pairs={{0,2},{2,4},{4,6},{6,0},{1,3},{3,5},{5,7},{7,1},{8,10},{10,12},{12... | collective-permute-start | bytes 393224 | tf_op jit(solution)/shard_map/ppermute | solution.py:19
  9.5 5.0 %collective-permute-start.3 = (f32[32,8,128]{2,1,0:T(8,128)S(1)}, f32[32,8,128]{2,1,0:T(8,128)S(1)}, u32[]{:S(2)}, u32[]{:S(2)}) collective-permute-start(f32[32,8,128]{2,1,0:T(8,128)S(1)} %get-tuple-element.10), channel_id=1, source_target_pairs={{2,0},{4,2},{6,4},{0,6},{3,1},{5,3},{7,5},{1,7},{10,8},{12,10},{14... | collective-permute-start | bytes 393224 | tf_op jit(solution)/shard_map/ppermute | solution.py:21
  14.8 14.6 %collective-permute-start.4 = (f32[32,32,8]{2,1,0:T(8,128)S(1)}, f32[32,32,8]{2,1,0:T(8,128)S(1)}, u32[]{:S(2)}, u32[]{:S(2)}) collective-permute-start(f32[32,32,8]{2,1,0:T(8,128)S(1)} %get-tuple-element.5), channel_id=1, source_target_pairs={{0,1},{1,0},{2,3},{3,2},{4,5},{5,4},{6,7},{7,6},{8,9},{9,8},{10,11... | collective-permute-start | bytes 98312 | tf_op jit(solution)/shard_map/ppermute | solution.py:19
  16.3 24.3 %collective-permute-start.5 = (f32[32,32,8]{2,1,0:T(8,128)S(1)}, f32[32,32,8]{2,1,0:T(8,128)S(1)}, u32[]{:S(2)}, u32[]{:S(2)}) collective-permute-start(f32[32,32,8]{2,1,0:T(8,128)S(1)} %get-tuple-element.6), channel_id=1, source_target_pairs={{1,0},{0,1},{3,2},{2,3},{5,4},{4,5},{7,6},{6,7},{9,8},{8,9},{11,10... | collective-permute-start | bytes 98312 | tf_op jit(solution)/shard_map/ppermute | solution.py:21
  42.3 5.9 %collective-permute-start.6 = (f32[8,8,64]{2,0,1:T(8,128)S(1)}, f32[8,8,64]{2,0,1:T(8,128)S(1)}, u32[]{:S(2)}, u32[]{:S(2)}) collective-permute-start(f32[8,8,64]{2,0,1:T(8,128)S(1)} %fusion.18), channel_id=1, source_target_pairs={{0,8},{8,16},{16,24},{24,0},{1,9},{9,17},{17,25},{25,1},{2,10},{10... | collective-permute-start | bytes 49160 | tf_op jit(solution)/shard_map/ppermute | solution.py:19
  42.8 5.4 %collective-permute-start.7 = (f32[8,8,64]{2,0,1:T(8,128)S(1)}, f32[8,8,64]{2,0,1:T(8,128)S(1)}, u32[]{:S(2)}, u32[]{:S(2)}) collective-permute-start(f32[8,8,64]{2,0,1:T(8,128)S(1)} %fusion.18), channel_id=1, source_target_pairs={{8,0},{16,8},{24,16},{0,24},{9,1},{17,9},{25,17},{1,25},{10,2},{18... | collective-permute-start | bytes 49160 | tf_op jit(solution)/shard_map/ppermute | solution.py:21
  48.2 4.1 %collective-permute-start.8 = (f32[24,8,64]{2,0,1:T(8,128)S(1)}, f32[24,8,64]{2,0,1:T(8,128)S(1)}, u32[]{:S(2)}, u32[]{:S(2)}) collective-permute-start(f32[24,8,64]{2,0,1:T(8,128)S(1)} %pad_maximum_fusion.4), channel_id=1, source_target_pairs={{0,2},{2,4},{4,6},{6,0},{1,3},{3,5},{5,7},{7,1},{8,10},{10,12},{12... | collective-permute-start | bytes 147464 | tf_op jit(solution)/shard_map/ppermute | solution.py:19
  48.3 4.0 %collective-permute-start.9 = (f32[24,8,64]{2,0,1:T(8,128)S(1)}, f32[24,8,64]{2,0,1:T(8,128)S(1)}, u32[]{:S(2)}, u32[]{:S(2)}) collective-permute-start(f32[24,8,64]{2,0,1:T(8,128)S(1)} %pad_maximum_fusion.4), channel_id=1, source_target_pairs={{2,0},{4,2},{6,4},{0,6},{3,1},{5,3},{7,5},{1,7},{10,8},{12,10},{14... | collective-permute-start | bytes 147464 | tf_op jit(solution)/shard_map/ppermute | solution.py:21
  52.5 9.4 %collective-permute-start.10 = (f32[24,24,8]{2,0,1:T(8,128)S(1)}, f32[24,24,8]{2,0,1:T(8,128)S(1)}, u32[]{:S(2)}, u32[]{:S(2)}) collective-permute-start(f32[24,24,8]{2,0,1:T(8,128)S(1)} %get-tuple-element.7), channel_id=1, source_target_pairs={{0,1},{1,0},{2,3},{3,2},{4,5},{5,4},{6,7},{7,6},{8,9},{9,8},{10,11... | collective-permute-start | bytes 55304 | tf_op jit(solution)/shard_map/ppermute | solution.py:19
  54.1 14.2 %collective-permute-start.11 = (f32[24,24,8]{2,0,1:T(8,128)S(1)}, f32[24,24,8]{2,0,1:T(8,128)S(1)}, u32[]{:S(2)}, u32[]{:S(2)}) collective-permute-start(f32[24,24,8]{2,0,1:T(8,128)S(1)} %get-tuple-element.8), channel_id=1, source_target_pairs={{1,0},{0,1},{3,2},{2,3},{5,4},{4,5},{7,6},{6,7},{9,8},{8,9},{11,10... | collective-permute-start | bytes 55304 | tf_op jit(solution)/shard_map/ppermute | solution.py:21
  69.3 5.4 %collective-permute-start.12 = (f32[1,4,32]{2,0,1:T(1,128)S(1)}, f32[1,4,32]{2,0,1:T(1,128)S(1)}, u32[]{:S(2)}, u32[]{:S(2)}) collective-permute-start(f32[1,4,32]{2,0,1:T(1,128)S(1)} %get-tuple-element.39), channel_id=1, source_target_pairs={{0,8},{8,16},{16,24},{24,0},{1,9},{9,17},{17,25},{25,1},{2,10},{10... | collective-permute-start | bytes 1544 | tf_op jit(solution)/shard_map/ppermute | solution.py:19
  69.4 5.4 %collective-permute-start.13 = (f32[1,4,32]{2,0,1:T(1,128)S(1)}, f32[1,4,32]{2,0,1:T(1,128)S(1)}, u32[]{:S(2)}, u32[]{:S(2)}) collective-permute-start(f32[1,4,32]{2,0,1:T(1,128)S(1)} %get-tuple-element.40), channel_id=1, source_target_pairs={{8,0},{16,8},{24,16},{0,24},{9,1},{17,9},{25,17},{1,25},{10,2},{18... | collective-permute-start | bytes 1544 | tf_op jit(solution)/shard_map/ppermute | solution.py:21
  78.0 3.8 %collective-permute-start.16 = (f32[6,6,1]{2,0,1:T(8,128)S(1)}, f32[6,6,1]{2,0,1:T(8,128)S(1)}, u32[]{:S(2)}, u32[]{:S(2)}) collective-permute-start(f32[6,6,1]{2,0,1:T(8,128)S(1)} %get-tuple-element.23), channel_id=1, source_target_pairs={{0,1},{1,0},{2,3},{3,2},{4,5},{5,4},{6,7},{7,6},{8,9},{9,8},{10,11... | collective-permute-start | bytes 440 | tf_op jit(solution)/shard_map/ppermute | solution.py:19
  79.5 3.8 %collective-permute-start.17 = (f32[6,6,1]{2,0,1:T(8,128)S(1)}, f32[6,6,1]{2,0,1:T(8,128)S(1)}, u32[]{:S(2)}, u32[]{:S(2)}) collective-permute-start(f32[6,6,1]{2,0,1:T(8,128)S(1)} %get-tuple-element.24), channel_id=1, source_target_pairs={{1,0},{0,1},{3,2},{2,3},{5,4},{4,5},{7,6},{6,7},{9,8},{8,9},{11,10... | collective-permute-start | bytes 440 | tf_op jit(solution)/shard_map/ppermute | solution.py:21
  84.1 5.4 %collective-permute-start.18 = (f32[1,2,16]{2,0,1:T(1,128)S(1)}, f32[1,2,16]{2,0,1:T(1,128)S(1)}, u32[]{:S(2)}, u32[]{:S(2)}) collective-permute-start(f32[1,2,16]{2,0,1:T(1,128)S(1)} %get-tuple-element.47), channel_id=1, source_target_pairs={{0,8},{8,16},{16,24},{24,0},{1,9},{9,17},{17,25},{25,1},{2,10},{10... | collective-permute-start | bytes 392 | tf_op jit(solution)/shard_map/ppermute | solution.py:19
  85.2 4.3 %collective-permute-start.19 = (f32[1,2,16]{2,0,1:T(1,128)S(1)}, f32[1,2,16]{2,0,1:T(1,128)S(1)}, u32[]{:S(2)}, u32[]{:S(2)}) collective-permute-start(f32[1,2,16]{2,0,1:T(1,128)S(1)} %get-tuple-element.48), channel_id=1, source_target_pairs={{8,0},{16,8},{24,16},{0,24},{9,1},{17,9},{25,17},{1,25},{10,2},{18... | collective-permute-start | bytes 392 | tf_op jit(solution)/shard_map/ppermute | solution.py:21
  92.7 3.7 %collective-permute-start.22 = (f32[4,4,1]{2,0,1:T(4,128)S(1)}, f32[4,4,1]{2,0,1:T(4,128)S(1)}, u32[]{:S(2)}, u32[]{:S(2)}) collective-permute-start(f32[4,4,1]{2,0,1:T(4,128)S(1)} %get-tuple-element.37), channel_id=1, source_target_pairs={{0,1},{1,0},{2,3},{3,2},{4,5},{5,4},{6,7},{7,6},{8,9},{9,8},{10,11... | collective-permute-start | bytes 200 | tf_op jit(solution)/shard_map/ppermute | solution.py:19
  93.3 3.7 %collective-permute-start.23 = (f32[4,4,1]{2,0,1:T(4,128)S(1)}, f32[4,4,1]{2,0,1:T(4,128)S(1)}, u32[]{:S(2)}, u32[]{:S(2)}) collective-permute-start(f32[4,4,1]{2,0,1:T(4,128)S(1)} %get-tuple-element.38), channel_id=1, source_target_pairs={{1,0},{0,1},{3,2},{2,3},{5,4},{4,5},{7,6},{6,7},{9,8},{8,9},{11,10... | collective-permute-start | bytes 200 | tf_op jit(solution)/shard_map/ppermute | solution.py:21
  139.8 5.4 %collective-permute-start.24 = (f32[1,2,16]{2,0,1:T(1,128)S(1)}, f32[1,2,16]{2,0,1:T(1,128)S(1)}, u32[]{:S(2)}, u32[]{:S(2)}) collective-permute-start(f32[1,2,16]{2,0,1:T(1,128)S(1)} %get-tuple-element.45), channel_id=1, source_target_pairs={{0,8},{8,16},{16,24},{24,0},{1,9},{9,17},{17,25},{25,1},{2,10},{10... | collective-permute-start | bytes 392 | tf_op jit(solution)/shard_map/ppermute | solution.py:19
  141.7 3.6 %collective-permute-start.25 = (f32[1,2,16]{2,0,1:T(1,128)S(1)}, f32[1,2,16]{2,0,1:T(1,128)S(1)}, u32[]{:S(2)}, u32[]{:S(2)}) collective-permute-start(f32[1,2,16]{2,0,1:T(1,128)S(1)} %get-tuple-element.46), channel_id=1, source_target_pairs={{8,0},{16,8},{24,16},{0,24},{9,1},{17,9},{25,17},{1,25},{10,2},{18... | collective-permute-start | bytes 392 | tf_op jit(solution)/shard_map/ppermute | solution.py:21
  148.5 3.9 %collective-permute-start.28 = (f32[4,4,1]{2,0,1:T(4,128)S(1)}, f32[4,4,1]{2,0,1:T(4,128)S(1)}, u32[]{:S(2)}, u32[]{:S(2)}) collective-permute-start(f32[4,4,1]{2,0,1:T(4,128)S(1)} %get-tuple-element.33), channel_id=1, source_target_pairs={{0,1},{1,0},{2,3},{3,2},{4,5},{5,4},{6,7},{7,6},{8,9},{9,8},{10,11... | collective-permute-start | bytes 200 | tf_op jit(solution)/shard_map/ppermute | solution.py:19
  150.8 3.7 %collective-permute-start.29 = (f32[4,4,1]{2,0,1:T(4,128)S(1)}, f32[4,4,1]{2,0,1:T(4,128)S(1)}, u32[]{:S(2)}, u32[]{:S(2)}) collective-permute-start(f32[4,4,1]{2,0,1:T(4,128)S(1)} %get-tuple-element.34), channel_id=1, source_target_pairs={{1,0},{0,1},{3,2},{2,3},{5,4},{4,5},{7,6},{6,7},{9,8},{8,9},{11,10... | collective-permute-start | bytes 200 | tf_op jit(solution)/shard_map/ppermute | solution.py:21
  155.0 5.4 %collective-permute-start.30 = (f32[1,4,32]{2,0,1:T(1,128)S(1)}, f32[1,4,32]{2,0,1:T(1,128)S(1)}, u32[]{:S(2)}, u32[]{:S(2)}) collective-permute-start(f32[1,4,32]{2,0,1:T(1,128)S(1)} %get-tuple-element.31), channel_id=1, source_target_pairs={{0,8},{8,16},{16,24},{24,0},{1,9},{9,17},{17,25},{25,1},{2,10},{10... | collective-permute-start | bytes 1544 | tf_op jit(solution)/shard_map/ppermute | solution.py:19
  156.5 4.0 %collective-permute-start.31 = (f32[1,4,32]{2,0,1:T(1,128)S(1)}, f32[1,4,32]{2,0,1:T(1,128)S(1)}, u32[]{:S(2)}, u32[]{:S(2)}) collective-permute-start(f32[1,4,32]{2,0,1:T(1,128)S(1)} %get-tuple-element.32), channel_id=1, source_target_pairs={{8,0},{16,8},{24,16},{0,24},{9,1},{17,9},{25,17},{1,25},{10,2},{18... | collective-permute-start | bytes 1544 | tf_op jit(solution)/shard_map/ppermute | solution.py:21
  163.7 3.8 %collective-permute-start.34 = (f32[6,6,1]{2,0,1:T(8,128)S(1)}, f32[6,6,1]{2,0,1:T(8,128)S(1)}, u32[]{:S(2)}, u32[]{:S(2)}) collective-permute-start(f32[6,6,1]{2,0,1:T(8,128)S(1)} %get-tuple-element.19), channel_id=1, source_target_pairs={{0,1},{1,0},{2,3},{3,2},{4,5},{5,4},{6,7},{7,6},{8,9},{9,8},{10,11... | collective-permute-start | bytes 440 | tf_op jit(solution)/shard_map/ppermute | solution.py:19
  163.8 4.0 %collective-permute-start.35 = (f32[6,6,1]{2,0,1:T(8,128)S(1)}, f32[6,6,1]{2,0,1:T(8,128)S(1)}, u32[]{:S(2)}, u32[]{:S(2)}) collective-permute-start(f32[6,6,1]{2,0,1:T(8,128)S(1)} %get-tuple-element.20), channel_id=1, source_target_pairs={{1,0},{0,1},{3,2},{2,3},{5,4},{4,5},{7,6},{6,7},{9,8},{8,9},{11,10... | collective-permute-start | bytes 440 | tf_op jit(solution)/shard_map/ppermute | solution.py:21
  168.5 5.9 %collective-permute-start.36 = (f32[1,8,64]{2,0,1:T(1,128)S(1)}, f32[1,8,64]{2,0,1:T(1,128)S(1)}, u32[]{:S(2)}, u32[]{:S(2)}) collective-permute-start(f32[1,8,64]{2,0,1:T(1,128)S(1)} %get-tuple-element.17), channel_id=1, source_target_pairs={{0,8},{8,16},{16,24},{24,0},{1,9},{9,17},{17,25},{25,1},{2,10},{10... | collective-permute-start | bytes 6152 | tf_op jit(solution)/shard_map/ppermute | solution.py:19
  169.6 4.8 %collective-permute-start.37 = (f32[1,8,64]{2,0,1:T(1,128)S(1)}, f32[1,8,64]{2,0,1:T(1,128)S(1)}, u32[]{:S(2)}, u32[]{:S(2)}) collective-permute-start(f32[1,8,64]{2,0,1:T(1,128)S(1)} %get-tuple-element.18), channel_id=1, source_target_pairs={{8,0},{16,8},{24,16},{0,24},{9,1},{17,9},{25,17},{1,25},{10,2},{18... | collective-permute-start | bytes 6152 | tf_op jit(solution)/shard_map/ppermute | solution.py:21
  177.8 4.7 %collective-permute-start.40 = (f32[10,10,1]{2,0,1:T(8,128)S(1)}, f32[10,10,1]{2,0,1:T(8,128)S(1)}, u32[]{:S(2)}, u32[]{:S(2)}) collective-permute-start(f32[10,10,1]{2,0,1:T(8,128)S(1)} %get-tuple-element.13), channel_id=1, source_target_pairs={{0,1},{1,0},{2,3},{3,2},{4,5},{5,4},{6,7},{7,6},{8,9},{9,8},{10,11... | collective-permute-start | bytes 1208 | tf_op jit(solution)/shard_map/ppermute | solution.py:19
  179.6 5.3 %collective-permute-start.41 = (f32[10,10,1]{2,0,1:T(8,128)S(1)}, f32[10,10,1]{2,0,1:T(8,128)S(1)}, u32[]{:S(2)}, u32[]{:S(2)}) collective-permute-start(f32[10,10,1]{2,0,1:T(8,128)S(1)} %get-tuple-element.14), channel_id=1, source_target_pairs={{1,0},{0,1},{3,2},{2,3},{5,4},{4,5},{7,6},{6,7},{9,8},{8,9},{11,10... | collective-permute-start | bytes 1208 | tf_op jit(solution)/shard_map/ppermute | solution.py:21
  (14 other events, 351.2 us)
where the time goes:
time: 187 us
  waiting for transfers between devices  69 us (37%)
  starting transfers between devices  56 us (30%)
  blocking collectives  40.8 us (22%)
  matrix products  13.7 us (7%)
  local copies, waits for them, and re-layouts  3.69 us (2%)
  other arithmetic  2.81 us (2%)
    ppermute x21, waiting for transfers between devices, with_halo(): lax.ppermute(tail, axis, [(i, (i + 1) % count) for i in range(count)])  43.7 us
    unnamed x1, blocking collectives  40.8 us
    ppermute x21, starting transfers between devices, with_halo(): lax.ppermute(head, axis, [((i + 1) % count, i) for i in range(count)])  36.8 us
    ppermute x21, waiting for transfers between devices, with_halo(): lax.ppermute(head, axis, [((i + 1) % count, i) for i in range(count)])  25.2 us
    ppermute x21, starting transfers between devices, with_halo(): lax.ppermute(tail, axis, [(i, (i + 1) % count) for i in range(count)])  19.2 us
  transfers between devices with their start and end apart: 42, of which 28 were waited for; matrix products, arithmetic and copies ran while one was open for 5% of the time, Pallas kernels for 0%

commit v1 on v0

--- a/solution.py
+++ b/solution.py
@@ -1,6 +1,11 @@
+import functools
+
 import jax
 import jax.numpy as jnp
+import numpy as np
 from jax import lax
+from jax.experimental import pallas as pl
+from jax.experimental.pallas import tpu as pltpu
 from jax.sharding import PartitionSpec as P
 
 REACH = 8
@@ -129,7 +134,7 @@
     return (result, coarse)
 
 
-def local(charges, exponents, amplitudes, top_x, top_y, top_z):
+def local_any(charges, exponents, amplitudes, top_x, top_y, top_z):
     tap_table = gauss_taps(exponents)
     term_zero, level_one = gauss_and_restrict(charges, tap_table[0], amplitudes[0])
     term_one, level_two = gauss_and_restrict(level_one, tap_table[1], amplitudes[1])
@@ -144,6 +149,500 @@
     return term_zero + prolong_local(phi_one)
 
 
+F32 = jnp.float32
+BF16 = jnp.bfloat16
+LANES = 128
+FAR = 1.0e9
+GAUSSIAN_RIM = REACH + 1
+
+
+def up8(count):
+    return -(-count // 8) * 8
+
+
+def restrict_weights(fine, coarse):
+    offsets = np.asarray(fine)[None, :] - 2 * np.asarray(coarse)[:, None] + 1
+    inner = np.where((offsets == 1) | (offsets == 2), 0.75, 0.0)
+    return np.where((offsets == 0) | (offsets == 3), 0.25, inner).astype(np.float32)
+
+
+def reach_four(length):
+    total, cells = np.eye(length, dtype=np.float32), np.arange(length)
+    for level in range(1, 5):
+        coarse = np.arange(-1, length // 2**level + 1)
+        total = restrict_weights(cells, coarse) @ total
+        cells = coarse
+    return total
+
+
+def prolong_three_whole(count):
+    total = np.eye(count, dtype=np.float32)
+    for level in range(3):
+        size = count * 2**level
+        step = np.zeros((2 * size, size), np.float32)
+        for cell in range(size):
+            for offset, weight in ((-1, 0.25), (0, 0.75), (1, 0.75), (2, 0.25)):
+                step[(2 * cell + offset) % (2 * size), cell] += weight
+        total = step @ total
+    return total
+
+
+def padded(table, rows, cols):
+    out = np.zeros((rows, cols), np.float32)
+    out[: table.shape[0], : table.shape[1]] = table
+    return out
+
+
+class Plan:
+    def __init__(self, brick, counts):
+        self.brick, self.counts = brick, counts
+        bx, by, bz = brick
+        self.half = by // 2
+        self.rim = up8(2 * GAUSSIAN_RIM + 1)
+        self.fine_rows = bz + 2 * REACH
+        self.cx, self.cy = bx // 2 + 2, by // 2 + 2
+        self.window = bz // 2 + 2 * GAUSSIAN_RIM
+        self.window_rows = up8(self.window)
+        self.out_z = bz // 2 + 2
+        self.out_rows = up8(self.out_z)
+        self.top_rows = 2 * up8(bz // 16 + 2)
+        self.top_z = bz // 16 + 2
+        self.top_x, self.top_y = bx // 16 + 2, by // 16 + 2
+        self.group = 16
+        x_of, y_of = self.own_cells()
+        rz = reach_four(bz)
+        self.top_left = padded(rz, self.top_rows // 2, bz)
+        rx, ry = reach_four(bx), reach_four(by)
+        self.top_right, self.rest_right = [], []
+        sx = restrict_weights(np.arange(bx), np.arange(-1, bx // 2 + 1))
+        sy = restrict_weights(np.arange(by), np.arange(-1, by // 2 + 1))
+        for part in range(2):
+            y = y_of + part * self.half
+            table = rx[:, x_of][:, None, :] * ry[:, y][None, :, :]
+            self.top_right.append(padded(table.reshape(-1, LANES).T, LANES, LANES))
+            table = sx[:, x_of][:, None, :] * sy[:, y][None, :, :]
+            self.rest_right.append(padded(table.reshape(-1, LANES).T, LANES, LANES))
+        z_in = np.concatenate([np.arange(bz), bz + np.arange(self.rim), np.arange(-self.rim, 0)])
+        z_out = np.arange(-GAUSSIAN_RIM, bz // 2 + GAUSSIAN_RIM)
+        self.rest_left = padded(restrict_weights(z_in, z_out), self.window_rows, z_in.size)
+        spread = restrict_weights(np.arange(bz), np.arange(-1, bz // 2 + 1)).T
+        self.back_left = padded(spread, bz, self.out_rows)
+        cols = []
+        for part in range(2):
+            y = y_of + part * self.half
+            table = sx[:, x_of][:, None, :] * sy[:, y][None, :, :]
+            cols.append(padded(table.reshape(-1, LANES), LANES, LANES))
+        self.back_right = np.concatenate(cols, axis=1)
+        self.message = self.fine_rows + self.window_rows + self.top_rows
+
+    def own_cells(self):
+        lane = np.arange(LANES)
+        return lane // self.half, lane % self.half
+
+
+def fits(brick, counts):
+    bx, by, bz = brick
+    return (
+        counts == (4, 4, 2)
+        and bx * (by // 2) == LANES
+        and by % 16 == 0
+        and bx % 16 == 0
+        and bz == LANES
+        and bx // 2 >= REACH
+        and (bx // 2 + 4) * (by // 2 + 2) <= LANES
+        and (bx // 16 + 2) * (by // 16 + 2) <= 16
+    )
+
+
+def split(value):
+    high = value.astype(BF16)
+    return high, (value - high.astype(F32)).astype(BF16)
+
+
+def split_wide(value):
+    high = lax.reduce_precision(value, 8, 7)
+    return high.astype(BF16), (value - high).astype(BF16)
+
+
+def dot(left, right):
+    return jnp.dot(left, right, preferred_element_type=F32)
+
+
+def dot_left(exact, value):
+    high, low = split(value)
+    return dot(exact, high) + dot(exact, low)
+
+
+def dot_right(value, exact):
+    high, low = split(value)
+    return dot(high, exact) + dot(low, exact)
+
+
+def dot_split(left, right):
+    return dot(left[0], right[0]) + dot(left[1], right[0]) + dot(left[0], right[1])
+
+
+def lanes_of(rows):
+    return lax.broadcasted_iota(jnp.int32, (rows, LANES), 1)
+
+
+def halves(first, second):
+    low = lanes_of(first.shape[0]) < LANES // 2
+    return (
+        jnp.where(low, first, pltpu.roll(second, LANES // 2, 1)),
+        jnp.where(low, pltpu.roll(first, LANES // 2, 1), second),
+    )
+
+
+def start_kernel(plan, charges_ref, left_ref, left_low_ref, right_ref, right_low_ref, own_ref, out_ref):
+    bx, by, bz = plan.brick
+    rim, half = plan.rim, plan.half
+    top = None
+    for part in range(2):
+        cells = charges_ref[:, part * half : (part + 1) * half, :].reshape(LANES, bz).T
+        own_ref[part] = cells
+        out_ref[2 * rim * part : 2 * rim * part + rim] = cells[:rim]
+        out_ref[2 * rim * part + rim : 2 * rim * (part + 1)] = cells[bz - rim :]
+        rows = dot_split((left_ref[...], left_low_ref[...]), split(cells))
+        rows = dot_split(split(rows), (right_ref[part], right_low_ref[part]))
+        top = rows if top is None else top + rows
+    out_ref[4 * rim :] = top
+
+
+def spread_kernel(plan, place_ref, own_ref, sent_ref, got_ref, left_ref, right_ref, fine_ref, out_ref):
+    bx, by, bz = plan.brick
+    rim, rows = plan.rim, plan.fine_rows
+    coarse = None
+    for part in range(2):
+        cells = own_ref[part]
+        far = got_ref[2 * rim * part : 2 * rim * (part + 1)]
+        fine_ref[part, :bz] = cells
+        fine_ref[part, bz : bz + REACH] = far[2 * rim - REACH :]
+        fine_ref[part, bz + REACH :] = far[:REACH]
+        summed = dot_left(left_ref[...], jnp.concatenate([cells, far], axis=0))
+        summed = dot_right(summed, right_ref[part])
+        coarse = summed if coarse is None else coarse + summed
+    low, high = halves(fine_ref[0], fine_ref[1])
+    even = place_ref[0] % 2 == 0
+    out_ref[:rows] = jnp.where(even, high, low)
+    out_ref[rows : rows + plan.window_rows] = coarse
+    top = rows + plan.window_rows
+    out_ref[top : top + plan.top_rows // 2] = sent_ref[4 * rim :]
+    out_ref[top + plan.top_rows // 2 :] = got_ref[4 * rim :]
+
+
+def pass_kernel(plan, place_ref, fine_ref, sent_ref, got_ref, out_ref):
+    rows = plan.fine_rows
+    even = place_ref[0] % 2 == 0
+    low, high = halves(fine_ref[0], fine_ref[1])
+    out_ref[:rows] = jnp.where(even, low, high)
+    own = sent_ref[rows : rows + plan.window_rows]
+    far = got_ref[rows : rows + plan.window_rows]
+    lane = lanes_of(plan.window_rows)
+    edge, all_lanes = 2 * plan.cy, plan.cx * plan.cy
+    last = all_lanes - edge
+    right = own + jnp.where((lane >= last) & (lane < all_lanes), pltpu.roll(far, last, 1), 0.0)
+    right = right + jnp.where((lane >= all_lanes) & (lane < all_lanes + edge), pltpu.roll(far, edge, 1), 0.0)
+    left = own + jnp.where(lane < edge, pltpu.roll(far, LANES - last, 1), 0.0)
+    left = left + jnp.where((lane >= all_lanes) & (lane < all_lanes + edge), pltpu.roll(far, all_lanes, 1), 0.0)
+    out_ref[rows : rows + plan.window_rows] = jnp.where(even, right, left)
+    top = rows + plan.window_rows
+    out_ref[top:] = sent_ref[top:] + pltpu.roll(got_ref[top:], plan.group, 1)
+
+
+def stack_kernel(plan, place_ref, fine_ref, first_sent_ref, sent_ref, first_ref, second_ref, cells_ref, out_ref):
+    rows, window = plan.fine_rows, plan.window_rows
+    low, high = halves(first_ref[:rows], second_ref[:rows])
+    for part, other in ((0, low), (1, high)):
+        cells_ref[part, :rows] = fine_ref[part]
+        cells_ref[part, rows:] = other
+    even = place_ref[1] % 2 == 0
+    out_ref[: 2 * rows] = jnp.where(even, cells_ref[0], cells_ref[1])
+    at = 2 * rows
+    for source in (first_sent_ref, first_ref, second_ref):
+        out_ref[at : at + window] = source[rows : rows + window]
+        at = at + window
+    out_ref[at:] = sent_ref[rows + window :] + pltpu.roll(second_ref[rows + window :], 2 * plan.group, 1)
+
+
+def share_kernel(plan, place_ref, cells_ref, sent_ref, got_ref, out_ref):
+    rows, window = plan.fine_rows, plan.window_rows
+    even = place_ref[1] % 2 == 0
+    out_ref[: 2 * rows] = jnp.where(even, cells_ref[1], cells_ref[0])
+    at, size = 2 * rows, 3 * window
+    out_ref[at : at + size] = sent_ref[at : at + size]
+    out_ref[at + size : at + 2 * size] = got_ref[at : at + size]
+    out_ref[at + 2 * size :] = sent_ref[at + size :] + pltpu.roll(got_ref[at + size :], 4 * plan.group, 1)
+
+
+def add_fine(plan, total, cells, left, right_refs, at, terms):
+    bz = plan.brick[2]
+    for block in range(2):
+        along_z = dot_split(left, split(cells[block]))
+        for term in range(terms):
+            piece = split(along_z[term * bz : (term + 1) * bz])
+            rows = pl.ds((2 * at + block) * LANES, LANES)
+            total = total + dot_split(piece, (right_refs[0][term, rows], right_refs[1][term, rows]))
+    return total
+
+
+def add_coarse(plan, total, cells, left, right_refs, at, terms):
+    along_z = dot_split(left, split(cells))
+    rows = pl.ds(at * LANES, LANES)
+    for term in range(terms):
+        piece = split(along_z[term * plan.out_rows : (term + 1) * plan.out_rows])
+        total = total + dot_split(piece, (right_refs[0][term, rows], right_refs[1][term, rows]))
+    return total
+
+
+def near_kernel(plan, terms, cells_ref, sent_ref, zl_ref, zl_low_ref, kl_ref, kl_low_ref, z1_ref, z1_low_ref,
+                k1_ref, k1_low_ref, fine_ref, coarse_ref):
+    rows, window = plan.fine_rows, plan.window_rows
+    total = jnp.zeros((plan.brick[2], 2 * LANES), F32)
+    left = (zl_ref[...], zl_low_ref[...])
+    for part in range(2):
+        blocks = (cells_ref[part, :rows], cells_ref[part, rows:])
+        total = add_fine(plan, total, blocks, left, (kl_ref, kl_low_ref), part, terms)
+    fine_ref[...] = total
+    coarse = jnp.zeros((plan.out_rows, LANES), F32)
+    left = (z1_ref[...], z1_low_ref[...])
+    for part in range(3):
+        at = 2 * rows + part * window
+        coarse = add_coarse(plan, coarse, sent_ref[at : at + window], left, (k1_ref, k1_low_ref), part, terms)
+    coarse_ref[...] = coarse
+
+
+def far_kernel(plan, terms, fine_ref, coarse_ref, first_ref, sent_ref, second_ref, zl_ref, zl_low_ref, kl_ref,
+               kl_low_ref, z1_ref, z1_low_ref, k1_ref, k1_low_ref, zc_ref, zc_low_ref, kc_ref, kc_low_ref, back_ref,
+               back_right_ref, out_ref):
+    rows, window, bz = plan.fine_rows, plan.window_rows, plan.brick[2]
+    total = fine_ref[...]
+    left = (zl_ref[...], zl_low_ref[...])
+    for part, source in ((2, first_ref), (3, second_ref)):
+        blocks = (source[:rows], source[rows : 2 * rows])
+        total = add_fine(plan, total, blocks, left, (kl_ref, kl_low_ref), part, terms)
+    coarse = coarse_ref[...]
+    left = (z1_ref[...], z1_low_ref[...])
+    for part in range(9):
+        source, place = (first_ref, part) if part < 3 else (second_ref, part - 3)
+        at = 2 * rows + place * window
+        coarse = add_coarse(plan, coarse, source[at : at + window], left, (k1_ref, k1_low_ref), part + 3, terms)
+    at = 2 * rows + 6 * window
+    for part, source in ((0, sent_ref), (1, second_ref)):
+        along_z = dot_split((zc_ref[...], zc_low_ref[...]), split(source[at : at + plan.top_rows]))
+        place = pl.ds(part * LANES, LANES)
+        coarse = coarse + dot_split(split(along_z), (kc_ref[place], kc_low_ref[place]))
+    total = total + dot_right(dot_left(back_ref[...], coarse), back_right_ref[...])
+    half = plan.half
+    for part in range(2):
+        cells = total[:, part * LANES : (part + 1) * LANES].T
+        out_ref[:, part * half : (part + 1) * half, :] = cells.reshape(plan.brick[0], half, bz)
+
+
+def norms(exponents):
+    offsets = jnp.arange(-REACH, REACH + 1).astype(F32)
+    return 1.0 / jnp.sum(jnp.exp(-exponents[..., None] * offsets * offsets), axis=-1)
+
+
+def gauss_of(exponents, scales, squared):
+    return scales[:, None, None] * jnp.exp(-exponents[:, None, None] * squared[None])
+
+
+def squares(difference):
+    return jnp.where(jnp.abs(difference) <= REACH, (difference * difference).astype(F32), FAR)
+
+
+def wrapped(difference, count):
+    return (difference + count // 2 + 2 * count) % count - count // 2
+
+
+def fine_weights(plan, exponents, amplitudes, even_x, even_y):
+    bx, by, bz = plan.brick
+    half = plan.half
+    scale = norms(exponents)
+    z_in = np.concatenate([np.arange(bz), np.arange(-REACH, 0), bz + np.arange(REACH)])
+    left = gauss_of(exponents, scale, squares(jnp.asarray(z_in[None, :] - np.arange(bz)[:, None])))
+    row = jnp.arange(8 * LANES)[:, None]
+    col = jnp.arange(2 * LANES)[None, :]
+    lane, block, group = row % LANES, (row // LANES) % 2, row // (2 * LANES)
+    strip = lane // (LANES // 2)
+    to_right = (strip == 0) == even_x
+    x_far = jnp.where(to_right, bx, -REACH) + (lane % (LANES // 2)) // half
+    x_in = jnp.where(block == 0, lane // half, x_far)
+    y_far = jnp.where((group == 3) == even_y, by, -half)
+    y_in = jnp.where(group < 2, group * half, y_far) + lane % half
+    x_out, y_out = (col % LANES) // half, (col // LANES) * half + col % half
+    right = gauss_of(exponents, amplitudes * scale * scale, squares(x_in - x_out) + squares(y_in - y_out))
+    return split_wide(left.reshape(-1, plan.fine_rows)), split_wide(right)
+
+
+def coarse_weights(plan, exponents, amplitudes, even_x, even_y):
+    bx, by, bz = (size // 2 for size in plan.brick)
+    scale = norms(exponents)
+    z_in = np.arange(plan.window_rows) - GAUSSIAN_RIM
+    z_out = np.arange(plan.out_rows) - 1
+    distance = np.where((np.arange(plan.window_rows) < plan.window)[None, :], z_in[None, :] - z_out[:, None], 2 * REACH)
+    distance = np.where((np.arange(plan.out_rows) < plan.out_z)[:, None], distance, 2 * REACH)
+    left = gauss_of(exponents, scale, squares(jnp.asarray(distance)))
+    row = jnp.arange(12 * LANES)[:, None]
+    col = jnp.arange(LANES)[None, :]
+    lane, slot, group = row % LANES, (row // LANES) % 3, row // (3 * LANES)
+    cell = lane // plan.cy
+    to_right = (slot == 1) == even_x
+    toward = jnp.where(to_right, bx, -bx)
+    x_in = jnp.where(slot == 0, 0, toward) + cell - 1
+    extra = jnp.where(to_right, 2 * bx + bx - 1, -2 * bx - 1) + cell - plan.cx
+    x_in = jnp.where(cell >= plan.cx, extra, x_in)
+    used = cell < jnp.where(slot == 2, plan.cx + 2, plan.cx)
+    toward = jnp.where((group == 2) == even_y, by, -by)
+    y_in = jnp.where(group == 0, 0, jnp.where(group == 3, 2 * by, toward)) + lane % plan.cy - 1
+    x_out, y_out = col // plan.cy - 1, col % plan.cy - 1
+    squared = squares(wrapped(x_in - x_out, bx * plan.counts[0])) + squares(wrapped(y_in - y_out, by * plan.counts[1]))
+    squared = jnp.where(used & (col < plan.cx * plan.cy), squared, FAR)
+    right = gauss_of(exponents, amplitudes * scale * scale, squared)
+    return split_wide(left.reshape(-1, plan.window_rows)), split_wide(right)
+
+
+def top_weights(plan, place, top_x, top_y, top_z):
+    bx, by, bz = plan.brick
+    nx, ny, nz = plan.counts
+    four = (bx // 16, by // 16, bz // 16)
+
+    def spread(kernel, axis, rows):
+        whole = prolong_three_whole(kernel.shape[0])
+        size = plan.brick[axis] // 2
+        wide = np.concatenate([whole[-1:], whole, whole[: size + 8]], axis=0)
+        mine = lax.dynamic_slice(jnp.asarray(wide), (place[axis] * size, 0), (rows, kernel.shape[0]))
+        return jnp.dot(mine, kernel, precision=HIGHEST)
+
+    def pick(index, used, count):
+        return jnp.where((index[:, None] % count == jnp.arange(count)[None, :]) & used[:, None], 1.0, 0.0)
+
+    row = jnp.arange(plan.top_rows)
+    side, cell = row // (plan.top_rows // 2), row % (plan.top_rows // 2)
+    z_in = jnp.where(side == 0, place[2], nz - 1 - place[2]) * four[2] + cell - 1 + nz * four[2]
+    left = jnp.dot(
+        spread(top_z, 2, plan.out_rows), pick(z_in, cell < plan.top_z, nz * four[2]).T, precision=HIGHEST
+    )
+    row = jnp.arange(2 * LANES)
+    lane, partner = row % LANES, row // LANES
+    group, cell = lane // plan.group, lane % plan.group
+    used = cell < plan.top_x * plan.top_y
+    x_dev = place[0] ^ (group % 2) ^ (3 * ((group // 2) % 2))
+    y_dev = place[1] ^ partner ^ (3 * (group // 4))
+    x_in = x_dev * four[0] + cell // plan.top_y - 1 + nx * four[0]
+    y_in = y_dev * four[1] + cell % plan.top_y - 1 + ny * four[1]
+    along_x = jnp.dot(pick(x_in, used, nx * four[0]), spread(top_x, 0, plan.cx).T, precision=HIGHEST)
+    along_y = jnp.dot(pick(y_in, used, ny * four[1]), spread(top_y, 1, plan.cy).T, precision=HIGHEST)
+    col = np.arange(LANES)
+    cols_x = (np.arange(plan.cx)[:, None] == col[None, :] // plan.cy).astype(np.float32)
+    cols_y = (np.arange(plan.cy)[:, None] == col[None, :] % plan.cy).astype(np.float32)
+    right = jnp.dot(along_x, cols_x, precision=HIGHEST) * jnp.dot(along_y, cols_y, precision=HIGHEST)
+    return split_wide(left), split_wide(right)
+
+
+def call(body, shapes, *operands, scalars=0):
+    specs = [pl.BlockSpec(memory_space=pltpu.SMEM)] * scalars
+    specs += [pl.BlockSpec(memory_space=pltpu.VMEM)] * (len(operands) - scalars)
+    out = pl.pallas_call(
+        body,
+        out_shape=[jax.ShapeDtypeStruct(shape, F32) for shape in shapes],
+        in_specs=specs,
+        out_specs=[pl.BlockSpec(memory_space=pltpu.VMEM)] * len(shapes),
+    )(*operands)
+    return out
+
+
+def pair(value, axis, bits):
+    count = lax.axis_size(axis)
+    return lax.ppermute(value, axis, [(i, i ^ bits) for i in range(count)])
+
+
+def local_short(plan, charges, exponents, amplitudes, top_x, top_y, top_z):
+    place = [lax.axis_index(axis) for axis in ("gx", "gy", "gz")]
+    where = jnp.stack(place).astype(jnp.int32)
+    even_x, even_y = place[0] % 2 == 0, place[1] % 2 == 0
+    terms = exponents.shape[1]
+    bx, by, bz = plan.brick
+    bind = functools.partial
+
+    own, sent_z = call(
+        bind(start_kernel, plan),
+        [(2, bz, LANES), (4 * plan.rim + plan.top_rows // 2, LANES)],
+        charges,
+        *np_split(plan.top_left),
+        *np_split(np.stack(plan.top_right)),
+    )
+    got_z = pair(sent_z, "gz", 1)
+    fine_left, fine_right = fine_weights(plan, exponents[0], amplitudes[0], even_x, even_y)
+    coarse_left, coarse_right = coarse_weights(plan, exponents[1], amplitudes[1], even_x, even_y)
+    top_left, top_right = top_weights(plan, place, top_x, top_y, top_z)
+
+    fine, sent_a = call(
+        bind(spread_kernel, plan),
+        [(2, plan.fine_rows, LANES), (plan.message, LANES)],
+        where,
+        own,
+        sent_z,
+        got_z,
+        jnp.asarray(plan.rest_left, BF16),
+        jnp.asarray(np.stack(plan.rest_right), BF16),
+        scalars=1,
+    )
+    got_a = pair(sent_a, "gx", 1)
+    (sent_b,) = call(bind(pass_kernel, plan), [(plan.message, LANES)], where, fine, sent_a, got_a, scalars=1)
+    got_b = pair(sent_b, "gx", 3)
+    size = 2 * plan.fine_rows + 3 * plan.window_rows + plan.top_rows
+    cells, sent_c = call(
+        bind(stack_kernel, plan),
+        [(2, 2 * plan.fine_rows, LANES), (size, LANES)],
+        where,
+        fine,
+        sent_a,
+        sent_b,
+        got_a,
+        got_b,
+        scalars=1,
+    )
+    got_c = pair(sent_c, "gy", 3)
+    weights = (*fine_left, *fine_right, *coarse_left, *coarse_right)
+    near_fine, near_coarse = call(
+        bind(near_kernel, plan, terms), [(bz, 2 * LANES), (plan.out_rows, LANES)], cells, sent_c, *weights
+    )
+    (sent_d,) = call(
+        bind(share_kernel, plan), [(size + 3 * plan.window_rows, LANES)], where, cells, sent_c, got_c, scalars=1
+    )
+    got_d = pair(sent_d, "gy", 1)
+    (out,) = call(
+        bind(far_kernel, plan, terms),
+        [(bx, by, bz)],
+        near_fine,
+        near_coarse,
+        got_c,
+        sent_d,
+        got_d,
+        *weights,
+        *top_left,
+        *top_right,
+        jnp.asarray(plan.back_left, BF16),
+        jnp.asarray(plan.back_right, BF16),
+    )
+    return out
+
+
+def np_split(table):
+    high = table.astype(BF16)
+    return jnp.asarray(high), jnp.asarray((table - high.astype(np.float32)).astype(BF16))
+
+
+def local(*arguments):
+    counts = tuple(lax.axis_size(axis) for axis in ("gx", "gy", "gz"))
+    brick = arguments[0].shape
+    if fits(brick, counts):
+        return local_short(Plan(brick, counts), *arguments)
+    return local_any(*arguments)
+
+
 def solution(mesh):
     in_specs = (P("gx", "gy", "gz"), P(), P(), P(), P(), P())
     out_specs = P("gx", "gy", "gz")

time: 187 us -> 71.1 us (0.38)
  waiting for transfers between devices: 69 us -> 14.4 us
  starting transfers between devices: 56 us -> 8.26 us
  blocking collectives: 40.8 us -> 0 us
  Pallas kernels: 0 us -> 27.2 us
  matrix products: 13.7 us -> 3.7 us
  other arithmetic: 2.81 us -> 12.5 us
    ppermute x42 -> x5, waiting for transfers between devices: 69 us -> 14.4 us  [pair(): return lax.ppermute(value, axis, [(i, i ^ bits) for i in range(count)])]
    ppermute x42 -> x5, starting transfers between devices: 56 us -> 8.26 us  [pair(): return lax.ppermute(value, axis, [(i, i ^ bits) for i in range(count)])]
    unnamed x1 -> x0, blocking collectives: 40.8 us -> none
    pallas_call x0 -> x7, Pallas kernels: none -> 27.2 us  [call(): pl.pallas_call(body, out_shape=[jax.ShapeDtypeStruct(shape, F32) for shap...]
    dot_general x37 -> x8, matrix products: 13.7 us -> 3.7 us  [the longest x3 1.36 us: spread(): return jnp.dot(mine, kernel, precision=HIGHEST)]
    convert_element_type x1 -> x6, other arithmetic: 0.01 us -> 8.13 us  [the longest x5 8.13 us: split_wide(): return (high.astype(BF16), (value - high).astype(BF16))]
    unnamed x12 -> x26, local copies, waits for them, and re-layouts: 0.24 us -> 3.47 us
    slice x19 -> x0, local copies, waits for them, and re-layouts: 1.9 us -> none  [the longest x1 0.92 us: with_halo(): head = lax.slice_in_dim(cells, 0, width, axis=dim)]
  transfers between devices with their start and end apart: 42 -> 5, of which waited for: 28 -> 3; matrix products, arithmetic and copies ran while one was open for 5% -> 24% of each run, Pallas kernels for 0% -> 11%
where the time goes in v1:
time: 71.1 us; the launch traced here: 70.8 us
  Pallas kernels  27.2 us (38%)
  waiting for transfers between devices  14.4 us (20%)
  other arithmetic  12.5 us (18%)
  starting transfers between devices  8.26 us (12%)
  local copies, waits for them, and re-layouts  4.6 us (6%)
  matrix products  3.7 us (5%)
    pallas_call x7, Pallas kernels, call(): pl.pallas_call(body, out_shape=[jax.ShapeDtypeStruct(shape, F32) for shap...  27.2 us
    ppermute x5, waiting for transfers between devices, pair(): return lax.ppermute(value, axis, [(i, i ^ bits) for i in range(count)])  14.4 us
    ppermute x5, starting transfers between devices, pair(): return lax.ppermute(value, axis, [(i, i ^ bits) for i in range(count)])  8.26 us
    convert_element_type x5, other arithmetic, split_wide(): return (high.astype(BF16), (value - high).astype(BF16))  8.13 us
    unnamed x26, local copies, waits for them, and re-layouts  3.47 us
  transfers between devices with their start and end apart: 5, of which 3 were waited for; matrix products, arithmetic and copies ran while one was open for 24% of the time, Pallas kernels for 11%

profile of v1, /device:TPU:0, one launch (start us, length us, event | category | flops | bytes accessed | tf_op | source)
XLA Modules:
  0.0 70.8 jit_solution(3124999932868275447)
XLA Ops:
  0.0 0.6 jit_solution_.3.left_low_ref
  0.6 2.0 %shard_map.199 = (f32[2,128,128]{2,1,0:T(8,128)}, f32[112,128]{1,0:T(8,128)}) custom-call(f32[16,16,128]{2,1,0:T(8,128)} %charges_ref.1, bf16[16,128]{1,0:T(8,128)(2,1)} %constant.445.clone.left_ref, bf16[16,128]{1,0:T(8,128)(2,1)} %jit_solution_.3.left_low_ref, bf16[2,128,128]{2,1,0:T(8,128)(2,1)} %constant.447.clone.right_ref, ...), custom_call_target="tpu_custom_call" | custom-call | tf_op jit(solution)/shard_map/pallas_call | solution.py:547
  2.6 3.0 %collective-permute-start = (f32[112,128]{1,0:T(8,128)}, f32[112,128]{1,0:T(8,128)S(1)}, u32[]{:S(2)}, u32[]{:S(2)}) collective-permute-start(f32[112,128]{1,0:T(8,128)} %get-tuple-element.14.sent_ref), channel_id=1, source_target_pairs={{0,1},{1,0},{2,3},{3,2},{4,5},{5,4},{6,7},{7,6},{8,9},{9,8},{10,11... | collective-permute-start | bytes 172040 | tf_op jit(solution)/shard_map/ppermute | solution.py:558
  5.7 0.8 %negate_bitcast_fusion = (f32[4]{0:T(128)S(1)}, f32[4]{0:T(128)S(1)}) fusion(f32[2,4]{1,0:T(2,128)} %param.22), kind=kLoop, calls=%fused_computation.244 | loop fusion | flops 8 | bytes 64 | tf_op jit(solution)/shard_map/neg | solution.py:444
  6.5 1.0 %fusion.36 = f32[72,16]{0,1:T(8,128)S(1)} fusion(f32[16,16]{1,0:T(8,128)S(1)} %copy-done, f32[201,16]{1,0:T(8,128)} %constant.451.clone, s32[]{:T(128)S(6)} %select_n.665), kind=kOutput, calls=%fused_computation.65 | convolution fusion | flops 221184 | bytes 42500 | tf_op jit(solution)/shard_map/dot_general | solution.py:516
  8.2 0.8 %multiply_multiply_fusion = (f32[4]{0:T(128)S(1)}, f32[4]{0:T(128)S(1)}, f32[4]{0:T(128)S(1)}, f32[4]{0:T(128)S(1)}) fusion(f32[2,4]{1,0:T(2,128)} %param.23, f32[4]{0:T(128)S(1)} %get-tuple-element.21, f32[4]{0:T(128)S(1)} %get-tuple-element.22), kind=kLoop, calls=%fused_computation.230 | loop fusion | flops 24 | bytes 128 | tf_op jit(solution)/shard_map/mul | solution.py:502
  8.9 1.2 %add_select_fusion.2 = f32[1536,128]{1,0:T(8,128)S(1)} fusion(s32[128]{0:T(128)S(1)} %get-tuple-element.49, s32[1536]{0:T(1024)S(1)} %get-tuple-element.55, s32[128]{0:T(128)S(1)} %get-tuple-element.50, s32[1536]{0:T(1024)S(1)} %get-tuple-element.56, pred[128]{0:T(512)(128)(4,1)S(1)} %iota_compare_fusion.3, pred[1536]{0:T(1024)(128)(4,1)S(1)} %select_compare_fusion), kind=kLoop, calls=%fused_computation.30 | loop fusion | flops 8060928 | bytes 801408 | tf_op jit(solution)/shard_map/jit(_where)/select_n | solution.py:501
  10.2 2.5 %fusion.1 = (bf16[4,1536,128]{2,1,0:T(8,128)(2,1)}, bf16[4,1536,128]{2,1,0:T(8,128)(2,1)}) fusion(f32[1536,128]{1,0:T(8,128)S(1)} %add_select_fusion.2, f32[4]{0:T(128)S(1)} %get-tuple-element.41, f32[4]{0:T(128)S(1)} %get-tuple-element.23), kind=kLoop, calls=%fused_computation.6 | loop fusion | flops 4718592 | bytes 3932192 | tf_op jit(solution)/shard_map/convert_element_type | solution.py:264
  13.3 0.4 fusion.126
  14.3 0.6 pad_add_fusion.place_ref
  14.9 0.6 copy-done.6
  15.5 2.1 %shard_map.200 = (f32[2,144,128]{2,1,0:T(8,128)}, f32[264,128]{1,0:T(8,128)}) custom-call(s32[3]{0:T(128)} %pad_add_fusion.place_ref, f32[2,128,128]{2,1,0:T(8,128)} %get-tuple-element.13.own_ref, f32[112,128]{1,0:T(8,128)} %get-tuple-element.14.sent_ref, f32[112,128]{1,0:T(8,128)} %copy-done.6, bf16[88,176]{1,0:T(8,128)(2,1)} %constant.455.clone.left_ref, ...), custom_call_target="tpu_custom_call" | custom-call | tf_op jit(solution)/shard_map/pallas_call | solution.py:547
  17.6 1.6 %collective-permute-start.1 = (f32[264,128]{1,0:T(8,128)}, f32[264,128]{1,0:T(8,128)S(1)}, u32[]{:S(2)}, u32[]{:S(2)}) collective-permute-start(f32[264,128]{1,0:T(8,128)} %get-tuple-element.16.sent_ref.first_sent_ref), channel_id=1, source_target_pairs={{0,8},{8,0},{16,24},{24,16},{1,9},{9,1},{17,25},{25,17},{2,10},{10... | collective-permute-start | bytes 405512 | tf_op jit(solution)/shard_map/ppermute | solution.py:558
  19.2 1.1 %fusion.19 = (bf16[256,128]{1,0:T(8,128)(2,1)}, bf16[256,128]{1,0:T(8,128)(2,1)}) fusion(f32[256,128]{1,0:T(8,128)S(1)} %fusion.126, f32[256,10]{0,1:T(8,128)S(1)} %fusion.20, f32[10,128]{1,0:T(8,128)S(1)} %copy-done.9), kind=kOutput, calls=%fused_computation.47 | convolution fusion | flops 4096000 | bytes 277504 | tf_op jit(solution)/shard_map/dot_general | solution.py:540
  20.3 2.6 %collective-permute-done.1.got_ref.first_ref = f32[264,128]{1,0:T(8,128)S(1)} collective-permute-done((f32[264,128]{1,0:T(8,128)}, f32[264,128]{1,0:T(8,128)S(1)}, u32[]{:S(2)}, u32[]{:S(2)}) %collective-permute-start.1) | collective-permute-done | bytes 135200 | tf_op jit(solution)/shard_map/ppermute | solution.py:558
  22.9 0.6 copy-done.2
  23.5 1.9 %shard_map.201.sent_ref = f32[264,128]{1,0:T(8,128)} custom-call(s32[3]{0:T(128)} %pad_add_fusion.place_ref, f32[2,144,128]{2,1,0:T(8,128)} %get-tuple-element.15.fine_ref, f32[264,128]{1,0:T(8,128)} %get-tuple-element.16.sent_ref.first_sent_ref, f32[264,128]{1,0:T(8,128)} %copy-done.2), custom_call_target="tpu_custom_call" | custom-call | tf_op jit(solution)/shard_map/pallas_call | solution.py:547
  25.4 3.6 %collective-permute-start.2 = (f32[264,128]{1,0:T(8,128)}, f32[264,128]{1,0:T(8,128)S(1)}, u32[]{:S(2)}, u32[]{:S(2)}) collective-permute-start(f32[264,128]{1,0:T(8,128)} %shard_map.201.sent_ref), channel_id=1, source_target_pairs={{0,24},{8,16},{16,8},{24,0},{1,25},{9,17},{17,9},{25,1},{2,26},{10... | collective-permute-start | bytes 405512 | tf_op jit(solution)/shard_map/ppermute | solution.py:558
  29.0 0.6 subtract_convert_fusion
  29.6 2.9 %collective-permute-done.2.second_ref = f32[264,128]{1,0:T(8,128)S(1)} collective-permute-done((f32[264,128]{1,0:T(8,128)}, f32[264,128]{1,0:T(8,128)S(1)}, u32[]{:S(2)}, u32[]{:S(2)}) %collective-permute-start.2) | collective-permute-done | bytes 135200 | tf_op jit(solution)/shard_map/ppermute | solution.py:558
  32.5 0.7 copy-done.4
  33.2 2.1 %shard_map.202 = (f32[2,288,128]{2,1,0:T(8,128)}, f32[584,128]{1,0:T(8,128)}) custom-call(s32[3]{0:T(128)} %pad_add_fusion.place_ref, f32[2,144,128]{2,1,0:T(8,128)} %get-tuple-element.15.fine_ref, f32[264,128]{1,0:T(8,128)} %get-tuple-element.16.sent_ref.first_sent_ref, f32[264,128]{1,0:T(8,128)} %shard_map.201.sent_ref, f32[264,128]{1,0:T(8,128)} %copy-done.2, ...), custom_call_target="tpu_custom_call" | custom-call | tf_op jit(solution)/shard_map/pallas_call | solution.py:547
  35.3 0.6 fusion.5
  35.9 8.9 %collective-permute-done.3.got_ref.first_ref = f32[584,128]{1,0:T(8,128)S(1)} collective-permute-done((f32[584,128]{1,0:T(8,128)}, f32[584,128]{1,0:T(8,128)S(1)}, u32[]{:S(2)}, u32[]{:S(2)}) %collective-permute-start.3) | collective-permute-done | bytes 299040 | tf_op jit(solution)/shard_map/ppermute | solution.py:558
  44.8 0.7 %copy-done.1 = f32[584,128]{1,0:T(8,128)} copy-done((f32[584,128]{1,0:T(8,128)}, f32[584,128]{1,0:T(8,128)S(1)}, u32[]{:S(2)}) %copy-start.1) | copy-done | bytes 299032
  45.5 2.0 %shard_map.204.sent_ref = f32[848,128]{1,0:T(8,128)} custom-call(s32[3]{0:T(128)} %pad_add_fusion.place_ref, f32[2,288,128]{2,1,0:T(8,128)} %get-tuple-element.17.cells_ref, f32[584,128]{1,0:T(8,128)} %get-tuple-element.18.sent_ref, f32[584,128]{1,0:T(8,128)} %copy-done.1), custom_call_target="tpu_custom_call" | custom-call | tf_op jit(solution)/shard_map/pallas_call | solution.py:547
  48.0 1.1 %fusion.13 = (bf16[512,144]{1,0:T(8,128)(2,1)}, bf16[512,144]{1,0:T(8,128)(2,1)}) fusion(f32[128,144]{1,0:T(8,128)S(1)} %copy-done.5, f32[512]{0:T(512)S(1)} %get-tuple-element.51, f32[512]{0:T(512)S(1)} %get-tuple-element.52), kind=kLoop, calls=%fused_computation.35 | loop fusion | flops 442368 | bytes 372736 | tf_op jit(solution)/shard_map/convert_element_type | solution.py:264
  49.1 0.8 %fusion.16 = (bf16[288,88]{1,0:T(8,128)(2,1)}, bf16[288,88]{1,0:T(8,128)(2,1)}) fusion(f32[72,88]{1,0:T(8,128)S(1)} %copy-done.7, f32[288]{0:T(512)S(1)} %mul.299, f32[288]{0:T(512)S(1)} %mul.296), kind=kLoop, calls=%fused_computation.43 | loop fusion | flops 152064 | bytes 129024 | tf_op jit(solution)/shard_map/convert_element_type | solution.py:264
  49.9 3.1 %fusion = (bf16[4,1024,256]{2,1,0:T(8,128)(2,1)}, bf16[4,1024,256]{2,1,0:T(8,128)(2,1)}) fusion(f32[1024,256]{1,0:T(8,128)S(1)} %fusion.5, f32[4]{0:T(128)S(1)} %get-tuple-element.42, f32[4]{0:T(128)S(1)} %get-tuple-element.39), kind=kLoop, calls=%fused_computation.4 | loop fusion | flops 6291456 | bytes 5242912 | tf_op jit(solution)/shard_map/convert_element_type | solution.py:264
  53.0 7.6 %shard_map.203 = (f32[128,256]{1,0:T(8,128)}, f32[72,128]{1,0:T(8,128)}) custom-call(f32[2,288,128]{2,1,0:T(8,128)} %get-tuple-element.17.cells_ref, f32[584,128]{1,0:T(8,128)} %get-tuple-element.18.sent_ref, bf16[512,144]{1,0:T(8,128)(2,1)} %get-tuple-element.32.zl_ref, bf16[512,144]{1,0:T(8,128)(2,1)} %get-tuple-element.31.zl_low_ref, ...), custom_call_target="tpu_custom_call" | custom-call | tf_op jit(solution)/shard_map/pallas_call | solution.py:547
  60.6 0.8 %copy-done.3 = f32[848,128]{1,0:T(8,128)} copy-done((f32[848,128]{1,0:T(8,128)}, f32[848,128]{1,0:T(8,128)S(1)}, u32[]{:S(2)}) %copy-start.3) | copy-done | bytes 434200
  61.4 9.4 %shard_map.205 = f32[16,16,128]{2,1,0:T(8,128)} custom-call(f32[128,256]{1,0:T(8,128)} %get-tuple-element.19.fine_ref, f32[72,128]{1,0:T(8,128)} %get-tuple-element.20.coarse_ref, f32[584,128]{1,0:T(8,128)} %copy-done.1, f32[848,128]{1,0:T(8,128)} %shard_map.204.sent_ref, f32[848,128]{1,0:T(8,128)} %copy-done.3, bf16[512,144]{1,0:T(8,128)(2,1)} %get-tuple-element.32.zl_ref, ...), custom_call_target="tpu_custom_call" | custom-call | tf_op jit(solution)/shard_map/pallas_call | solution.py:547
  (49 shorter events, 2.4 us)
Async XLA Ops:
  0.0 6.5 %copy-start = (f32[16,16]{1,0:T(8,128)S(1)}, f32[16,16]{1,0:T(8,128)}, u32[]{:S(2)}) copy-start(f32[16,16]{1,0:T(8,128)} %param.26) | copy-start | bytes 3076
  2.6 12.2 %collective-permute-start = (f32[112,128]{1,0:T(8,128)}, f32[112,128]{1,0:T(8,128)S(1)}, u32[]{:S(2)}, u32[]{:S(2)}) collective-permute-start(f32[112,128]{1,0:T(8,128)} %get-tuple-element.14.sent_ref), channel_id=1, source_target_pairs={{0,1},{1,0},{2,3},{3,2},{4,5},{5,4},{6,7},{7,6},{8,9},{9,8},{10,11... | collective-permute-start | bytes 172040 | tf_op jit(solution)/shard_map/ppermute | solution.py:558
  10.2 2.6 %copy-start.8 = (f32[49,4]{1,0:T(8,128)S(1)}, f32[49,4]{1,0:T(8,128)}, u32[]{:S(2)}) copy-start(f32[49,4]{1,0:T(8,128)} %constant.452.clone) | copy-start | bytes 2356
  10.2 2.6 %copy-start.11 = (f32[4,4]{1,0:T(4,128)S(1)}, f32[4,4]{1,0:T(4,128)}, u32[]{:S(2)}) copy-start(f32[4,4]{1,0:T(4,128)} %param.24) | copy-start | bytes 196
  10.2 3.1 %copy-start.10 = (f32[10,128]{1,0:T(8,128)S(1)}, f32[10,128]{1,0:T(8,128)}, u32[]{:S(2)}) copy-start(f32[10,128]{1,0:T(8,128)} %constant.453.clone) | copy-start | bytes 15364
  10.2 3.5 %copy-start.12 = (f32[4,4]{1,0:T(4,128)S(1)}, f32[4,4]{1,0:T(4,128)}, u32[]{:S(2)}) copy-start(f32[4,4]{1,0:T(4,128)} %param.25) | copy-start | bytes 196
  10.2 9.0 %copy-start.9 = (f32[10,128]{1,0:T(8,128)S(1)}, f32[10,128]{1,0:T(8,128)}, u32[]{:S(2)}) copy-start(f32[10,128]{1,0:T(8,128)} %constant.454.clone) | copy-start | bytes 15364
  14.9 0.6 copy-start.6
  17.6 30.4 %copy-start.5 = (f32[128,144]{1,0:T(8,128)S(1)}, f32[128,144]{1,0:T(8,128)}, u32[]{:S(2)}) copy-start(f32[128,144]{1,0:T(8,128)} %constant.463) | copy-start | bytes 221188
  17.6 5.3 %collective-permute-start.1 = (f32[264,128]{1,0:T(8,128)}, f32[264,128]{1,0:T(8,128)S(1)}, u32[]{:S(2)}, u32[]{:S(2)}) collective-permute-start(f32[264,128]{1,0:T(8,128)} %get-tuple-element.16.sent_ref.first_sent_ref), channel_id=1, source_target_pairs={{0,8},{8,0},{16,24},{24,16},{1,9},{9,1},{17,25},{25,17},{2,10},{10... | collective-permute-start | bytes 405512 | tf_op jit(solution)/shard_map/ppermute | solution.py:558
  22.9 0.6 copy-start.2
  23.5 25.6 %copy-start.7 = (f32[72,88]{1,0:T(8,128)S(1)}, f32[72,88]{1,0:T(8,128)}, u32[]{:S(2)}) copy-start(f32[72,88]{1,0:T(8,128)} %constant.468) | copy-start | bytes 76036
  25.4 7.1 %collective-permute-start.2 = (f32[264,128]{1,0:T(8,128)}, f32[264,128]{1,0:T(8,128)S(1)}, u32[]{:S(2)}, u32[]{:S(2)}) collective-permute-start(f32[264,128]{1,0:T(8,128)} %shard_map.201.sent_ref), channel_id=1, source_target_pairs={{0,24},{8,16},{16,8},{24,0},{1,25},{9,17},{17,9},{25,1},{2,26},{10... | collective-permute-start | bytes 405512 | tf_op jit(solution)/shard_map/ppermute | solution.py:558
  32.5 0.7 copy-start.4
  35.3 9.5 %collective-permute-start.3 = (f32[584,128]{1,0:T(8,128)}, f32[584,128]{1,0:T(8,128)S(1)}, u32[]{:S(2)}, u32[]{:S(2)}) collective-permute-start(f32[584,128]{1,0:T(8,128)} %get-tuple-element.18.sent_ref), channel_id=1, source_target_pairs={{0,6},{2,4},{4,2},{6,0},{1,7},{3,5},{5,3},{7,1},{8,14},{10,12},{12... | collective-permute-start | bytes 897032 | tf_op jit(solution)/shard_map/ppermute | solution.py:558
  44.8 0.7 %copy-start.1 = (f32[584,128]{1,0:T(8,128)}, f32[584,128]{1,0:T(8,128)S(1)}, u32[]{:S(2)}) copy-start(f32[584,128]{1,0:T(8,128)S(1)} %collective-permute-done.3.got_ref.first_ref) | copy-start | bytes 897028
  47.5 13.1 %collective-permute-start.4 = (f32[848,128]{1,0:T(8,128)}, f32[848,128]{1,0:T(8,128)S(1)}, u32[]{:S(2)}, u32[]{:S(2)}) collective-permute-start(f32[848,128]{1,0:T(8,128)} %shard_map.204.sent_ref), channel_id=1, source_target_pairs={{0,2},{2,0},{4,6},{6,4},{1,3},{3,1},{5,7},{7,5},{8,10},{10,8},{12,... | collective-permute-start | bytes 1302536 | tf_op jit(solution)/shard_map/ppermute | solution.py:558
  60.6 0.8 %copy-start.3 = (f32[848,128]{1,0:T(8,128)}, f32[848,128]{1,0:T(8,128)S(1)}, u32[]{:S(2)}) copy-start(f32[848,128]{1,0:T(8,128)S(1)} %collective-permute-done.4.second_ref) | copy-start | bytes 1302532

commit v2 on v1

--- a/solution.py
+++ b/solution.py
@@ -226,21 +226,120 @@
         z_out = np.arange(-GAUSSIAN_RIM, bz // 2 + GAUSSIAN_RIM)
         self.rest_left = padded(restrict_weights(z_in, z_out), self.window_rows, z_in.size)
         spread = restrict_weights(np.arange(bz), np.arange(-1, bz // 2 + 1)).T
-        self.back_left = padded(spread, bz, self.out_rows)
+        self.back_left = padded(spread.T, LANES, bz)
         cols = []
         for part in range(2):
             y = y_of + part * self.half
             table = sx[:, x_of][:, None, :] * sy[:, y][None, :, :]
             cols.append(padded(table.reshape(-1, LANES), LANES, LANES))
-        self.back_right = np.concatenate(cols, axis=1)
+        self.out_cells = -(-self.cx * self.cy // 16) * 16
+        self.back_right = np.concatenate(cols, axis=1).T[:, : self.out_cells]
         self.message = self.fine_rows + self.window_rows + self.top_rows
+
+    def constants(self, kernels):
+        rest = self.rest_left
+        fine_cells, fine_dz = self.fine_tables()
+        coarse_cells, out_cells, coarse_dz = self.coarse_tables()
+        spread_x, pick_x, spread_y, pick_y, spread_z, pick_z, lift_x, lift_y = self.top_tables(kernels)
+        named = {
+            "rest_left": rest[:, :LANES],
+            "rest_far": rest[:, LANES:],
+            "rest_right": np.concatenate(self.rest_right),
+            "fine_cells": fine_cells,
+            "fine_dz": fine_dz,
+            "coarse_cells": coarse_cells,
+            "out_cells": out_cells.reshape(-1, LANES),
+            "coarse_dz": coarse_dz,
+            "back": self.back_left,
+            "back_right": self.back_right,
+            "spread_x": spread_x.reshape(-1, 16),
+            "pick_x": pick_x.transpose(0, 2, 1, 3).reshape(-1, LANES),
+            "spread_y": spread_y.reshape(-1, 16),
+            "pick_y": pick_y.transpose(0, 2, 1, 3).reshape(-1, LANES),
+            "spread_z": spread_z.reshape(-1, 16),
+            "pick_z": pick_z.reshape(-1, self.top_rows),
+            "lift_x": lift_x,
+            "lift_y": lift_y,
+        }
+        at, starts, pieces = 0, {}, []
+        for name, table in named.items():
+            rows = -(-table.shape[0] // 16) * 16
+            starts[name] = at
+            pieces.append(padded(table, rows, LANES))
+            at += rows
+        self.starts = starts
+        return np.concatenate(pieces)
+
+    def fine_tables(self):
+        bx, by, bz = self.brick
+        x_of, y_of = self.own_cells()
+        strip, x_far = np.arange(LANES) // (LANES // 2), x_of % (LANES // 2 // self.half)
+        right, left = bx + x_far, x_far - REACH
+        cells = np.stack([x_of, y_of, np.where(strip == 0, right, left), np.where(strip == 0, left, right)])
+        z_in = np.concatenate([np.arange(bz), np.arange(-REACH, 0), bz + np.arange(REACH)])
+        distance = z_in[:, None] - np.arange(bz)[None, :]
+        squared = np.where(np.abs(distance) <= REACH, distance * distance, FAR)
+        return padded(cells, 8, LANES), squared.astype(np.float32)
+
+    def coarse_tables(self):
+        bx, by, bz = (size // 2 for size in self.brick)
+        lane = np.arange(LANES)
+        cell, count = lane // self.cy, self.cx * self.cy
+        own = cell - 1
+        extra = cell >= self.cx
+        far_right = np.where(extra, 3 * bx - 1 + cell - self.cx, bx + own)
+        far_left = np.where(extra, -2 * bx - 1 + cell - self.cx, own - bx)
+        cells = [own, own, own + bx, own - bx, far_left, far_right, lane % self.cy - 1]
+        cells += [np.where(lane < count, 0.0, FAR), np.where(cell < self.cx + 2, 0.0, FAR)]
+        row = np.arange(self.out_cells)[:, None] + np.zeros((1, LANES))
+        outs = np.stack([row // self.cy - 1, row % self.cy - 1, np.where(row < count, 0.0, FAR)])
+        z_in, z_out = np.arange(self.window_rows) - GAUSSIAN_RIM, np.arange(LANES) - 1
+        distance = z_in[:, None] - z_out[None, :]
+        near = (np.abs(distance) <= REACH) & (np.arange(LANES) < self.out_z)[None, :]
+        near = near & (np.arange(self.window_rows) < self.window)[:, None]
+        squared = np.where(near, distance * distance, FAR)
+        return padded(np.stack(cells), 16, LANES), outs.astype(np.float32), squared.astype(np.float32)
+
+    def top_tables(self, kernels):
+        four = [size // 16 for size in self.brick]
+        lane = np.arange(2 * LANES)
+        group, cell, partner = (lane % LANES) // self.group, lane % self.group, lane // LANES
+        used = cell < self.top_x * self.top_y
+        tables = []
+        for axis in range(3):
+            count, size = kernels[axis].shape[0], self.brick[axis] // 2
+            whole = prolong_three_whole(count)
+            outs = (self.cx, self.cy, self.out_z)[axis]
+            spread, pick = [], []
+            for place in range(self.counts[axis]):
+                index = (place * size - 1 + np.arange(outs)) % (8 * count)
+                spread.append(padded(whole[index], 16 if axis < 2 else LANES, 16))
+                if axis == 0:
+                    cells = (place ^ (group % 2) ^ (3 * ((group // 2) % 2))) * four[0] + cell // self.top_y - 1
+                    valid = used
+                elif axis == 1:
+                    cells = (place ^ partner ^ (3 * (group // 4))) * four[1] + cell % self.top_y - 1
+                    valid = used
+                else:
+                    row = np.arange(self.top_rows)
+                    side, at = row // (self.top_rows // 2), row % (self.top_rows // 2)
+                    cells = (place ^ side) * four[2] + at - 1
+                    valid = at < self.top_z
+                hot = (np.arange(count)[:, None] == (cells % count)[None, :]) & valid[None, :]
+                hot = padded(hot, 16, cells.size)
+                pick.append(hot if axis == 2 else hot.reshape(16, 2, LANES))
+            tables += [np.stack(spread), np.stack(pick)]
+        out = np.arange(self.out_cells)
+        tables.append((out[:, None] // self.cy == np.arange(16)[None, :]).astype(np.float32))
+        tables.append((out[:, None] % self.cy == np.arange(16)[None, :]).astype(np.float32))
+        return tables
 
     def own_cells(self):
         lane = np.arange(LANES)
         return lane // self.half, lane % self.half
 
 
-def fits(brick, counts):
+def fits(brick, counts, tops):
     bx, by, bz = brick
     return (
         counts == (4, 4, 2)
@@ -248,9 +347,11 @@
         and by % 16 == 0
         and bx % 16 == 0
         and bz == LANES
-        and bx // 2 >= REACH
+        and bx // 2 == REACH
+        and by // 2 == REACH
         and (bx // 2 + 4) * (by // 2 + 2) <= LANES
         and (bx // 16 + 2) * (by // 16 + 2) <= 16
+        and max(top.shape[0] for top in tops) <= 16
     )
 
 
@@ -259,11 +360,6 @@
     return high, (value - high.astype(F32)).astype(BF16)
 
 
-def split_wide(value):
-    high = lax.reduce_precision(value, 8, 7)
-    return high.astype(BF16), (value - high).astype(BF16)
-
-
 def dot(left, right):
     return jnp.dot(left, right, preferred_element_type=F32)
 
@@ -280,6 +376,14 @@
 
 def dot_split(left, right):
     return dot(left[0], right[0]) + dot(left[1], right[0]) + dot(left[0], right[1])
+
+
+def exact_tables(plan, ref):
+    def read(name, rows, at=0):
+        start = plan.starts[name] + at * rows
+        return ref[start : start + rows].astype(BF16)
+
+    return read
 
 
 def lanes_of(rows):
@@ -309,9 +413,34 @@
     out_ref[4 * rim :] = top
 
 
-def spread_kernel(plan, place_ref, own_ref, sent_ref, got_ref, left_ref, right_ref, fine_ref, out_ref):
+def setup_kernel(plan, terms, exponents_ref, amplitudes_ref, tops_x_ref, tops_y_ref, tops_z_ref, table_ref, kept_ref,
+                 params_ref, semaphore):
+    copy = pltpu.make_async_copy(table_ref, kept_ref, semaphore)
+    copy.start()
+    offsets = lax.broadcasted_iota(jnp.int32, (1, LANES), 1).astype(F32) - REACH
+    squared = jnp.where(offsets <= REACH, offsets * offsets, FAR)
+    for level in range(2):
+        for term in range(terms):
+            exponent = exponents_ref[level, term]
+            scale = 1.0 / jnp.sum(jnp.exp(squared * -exponent), axis=1, keepdims=True)
+            scale = jnp.broadcast_to(scale, (1, LANES))
+            row = 3 * terms * level + term
+            params_ref[row : row + 1] = jnp.zeros((1, LANES), F32) + exponent
+            row = row + terms
+            params_ref[row : row + 1] = scale * scale * amplitudes_ref[level, term]
+            row = row + terms
+            params_ref[row : row + 1] = scale
+    params_ref[6 * terms :] = jnp.zeros((3 * 16, LANES), F32)
+    for axis, source in enumerate((tops_x_ref, tops_y_ref, tops_z_ref)):
+        at, count = 6 * terms + 16 * axis, source.shape[0]
+        params_ref[at : at + count, :count] = source[...]
+    copy.wait()
+
+
+def spread_kernel(plan, place_ref, own_ref, sent_ref, got_ref, table_ref, fine_ref, out_ref):
     bx, by, bz = plan.brick
     rim, rows = plan.rim, plan.fine_rows
+    table = exact_tables(plan, table_ref)
     coarse = None
     for part in range(2):
         cells = own_ref[part]
@@ -319,8 +448,9 @@
         fine_ref[part, :bz] = cells
         fine_ref[part, bz : bz + REACH] = far[2 * rim - REACH :]
         fine_ref[part, bz + REACH :] = far[:REACH]
-        summed = dot_left(left_ref[...], jnp.concatenate([cells, far], axis=0))
-        summed = dot_right(summed, right_ref[part])
+        summed = dot_left(table("rest_left", plan.window_rows), cells)
+        summed = summed + dot_left(table("rest_far", plan.window_rows)[:, : 2 * rim], far)
+        summed = dot_right(summed, table("rest_right", LANES, part))
         coarse = summed if coarse is None else coarse + summed
     low, high = halves(fine_ref[0], fine_ref[1])
     even = place_ref[0] % 2 == 0
@@ -375,182 +505,207 @@
     out_ref[at + 2 * size :] = sent_ref[at + size :] + pltpu.roll(got_ref[at + size :], 4 * plan.group, 1)
 
 
-def add_fine(plan, total, cells, left, right_refs, at, terms):
-    bz = plan.brick[2]
-    for block in range(2):
-        along_z = dot_split(left, split(cells[block]))
-        for term in range(terms):
-            piece = split(along_z[term * bz : (term + 1) * bz])
-            rows = pl.ds((2 * at + block) * LANES, LANES)
-            total = total + dot_split(piece, (right_refs[0][term, rows], right_refs[1][term, rows]))
-    return total
-
-
-def add_coarse(plan, total, cells, left, right_refs, at, terms):
-    along_z = dot_split(left, split(cells))
-    rows = pl.ds(at * LANES, LANES)
+def dot_turned(left, right):
+    def product(first, second):
+        return lax.dot_general(first, second, (((1,), (1,)), ((), ())), preferred_element_type=F32)
+
+    return product(left[0], right[0]) + product(left[1], right[0]) + product(left[0], right[1])
+
+
+def fine_weights_kernel(plan, terms, place_ref, params_ref, table_ref, kf_ref, kf_low_ref, zf_ref, zf_low_ref):
+    bx, by, bz = plan.brick
+    cells_ref = table_ref.at[pl.ds(plan.starts["fine_cells"], 8)]
+    dz_ref = table_ref.at[pl.ds(plan.starts["fine_dz"], plan.fine_rows)]
+    half = plan.half
+    even_x, even_y = place_ref[0] % 2 == 0, place_ref[1] % 2 == 0
+    own_x, own_y = cells_ref[0:1], cells_ref[1:2]
+    far_x = jnp.where(even_x, cells_ref[2:3], cells_ref[3:4])
+    x_out = lax.broadcasted_iota(jnp.int32, (bx, LANES), 0).astype(F32)
+    y_out = lax.broadcasted_iota(jnp.int32, (half, LANES), 0).astype(F32)
+    y_low, y_high = F32(-half), F32(by)
+    y_far = jnp.where(even_y, y_low, y_high), jnp.where(even_y, y_high, y_low)
+
+    def decay(exponent, distance):
+        return jnp.where(jnp.abs(distance) <= REACH, jnp.exp(-exponent * distance * distance), 0.0)
+
     for term in range(terms):
-        piece = split(along_z[term * plan.out_rows : (term + 1) * plan.out_rows])
-        total = total + dot_split(piece, (right_refs[0][term, rows], right_refs[1][term, rows]))
-    return total
-
-
-def near_kernel(plan, terms, cells_ref, sent_ref, zl_ref, zl_low_ref, kl_ref, kl_low_ref, z1_ref, z1_low_ref,
-                k1_ref, k1_low_ref, fine_ref, coarse_ref):
+        exponent = params_ref[term : term + 1]
+        scale = params_ref[terms + term : terms + term + 1]
+        along_x = [decay(exponent, x_in - x_out)[:, None, :] for x_in in (own_x, far_x)]
+        for group in range(4):
+            y_in = own_y + (F32(group * half) if group < 2 else y_far[group - 2])
+            for part in range(2):
+                along_y = decay(exponent, y_in - (y_out + part * half)) * scale
+                for block in range(2):
+                    high, low = split((along_x[block] * along_y[None]).reshape(bx * half, LANES))
+                    rows, cols = pl.ds(part * LANES, LANES), pl.ds((2 * group + block) * LANES, LANES)
+                    kf_ref[term, rows, cols] = high
+                    kf_low_ref[term, rows, cols] = low
+        zf_ref[term], zf_low_ref[term] = split(
+            jnp.exp(-exponent * dz_ref[...]) * params_ref[2 * terms + term : 2 * terms + term + 1]
+        )
+
+
+def coarse_weights_kernel(plan, terms, place_ref, params_ref, table_ref, k1_ref, k1_low_ref, z1_ref, z1_low_ref,
+                          zc_ref, kc_ref):
+    cells_ref = table_ref.at[pl.ds(plan.starts["coarse_cells"], 16)]
+    at, count = plan.starts["out_cells"], plan.out_cells
+    out_cells_ref = [table_ref[at + count * part : at + count * (part + 1)] for part in range(3)]
+    dz_ref = table_ref.at[pl.ds(plan.starts["coarse_dz"], plan.window_rows)]
+    zc_ref[...], kc_ref[...] = top_weights(plan, terms, place_ref, params_ref, table_ref)
+    bx, by = plan.brick[0] // 2, plan.brick[1] // 2
+    even_x, even_y = place_ref[0] % 2 == 0, place_ref[1] % 2 == 0
+    base = 3 * terms
+
+    def squared(distance, count):
+        distance = distance - count * jnp.floor((distance + count // 2) * (1.0 / count))
+        return jnp.where(jnp.abs(distance) <= REACH, distance * distance, FAR)
+
+    x_out, y_out = out_cells_ref[0], out_cells_ref[1]
+    squares_x = []
+    for slot in range(3):
+        x_in = jnp.where(even_x, cells_ref[2 * slot : 2 * slot + 1], cells_ref[2 * slot + 1 : 2 * slot + 2])
+        used = cells_ref[7:8] if slot < 2 else cells_ref[8:9]
+        squares_x.append(squared(x_in - x_out, bx * plan.counts[0]) + used)
+    toward = jnp.where(even_y, F32(by), F32(-by))
+    for group, offset in enumerate((F32(0), -toward, toward, F32(2 * by))):
+        square_y = squared(cells_ref[6:7] + offset - y_out, by * plan.counts[1]) + out_cells_ref[2]
+        for slot in range(3):
+            total = squares_x[slot] + square_y
+            cols = pl.ds((3 * group + slot) * LANES, LANES)
+            for term in range(terms):
+                exponent = params_ref[base + term : base + term + 1]
+                scale = params_ref[base + terms + term : base + terms + term + 1]
+                high, low = split(jnp.exp(-exponent * total) * scale)
+                rows = pl.ds(term * plan.out_cells, plan.out_cells)
+                k1_ref[rows, cols] = high
+                k1_low_ref[rows, cols] = low
+    for term in range(terms):
+        exponent = params_ref[base + term : base + term + 1]
+        scale = params_ref[base + 2 * terms + term : base + 2 * terms + term + 1]
+        z1_ref[term], z1_low_ref[term] = split(jnp.exp(-exponent * dz_ref[...]) * scale)
+
+
+def top_weights(plan, terms, place_ref, params_ref, table_ref):
+    def chain(*factors):
+        value = factors[0]
+        for factor in factors[1:]:
+            value = dot_split(split(value), split(factor))
+        return value
+
+    def read(name, rows, at=0):
+        return table_ref[pl.ds(pl.multiple_of(plan.starts[name] + at * rows, 8), rows)]
+
+    size = 16
+    along = []
+    for axis, (spread, pick) in enumerate((("spread_x", "pick_x"), ("spread_y", "pick_y"))):
+        top = params_ref[6 * terms + size * axis : 6 * terms + size * (axis + 1)]
+        picked = read(pick, 2 * size, place_ref[axis])
+        picked = jnp.concatenate([picked[:size], picked[size:]], axis=1)
+        value = chain(read(spread, size, place_ref[axis])[:, :size], top)[:, :size]
+        along.append(chain(value, picked))
+    top = params_ref[6 * terms + 2 * size : 6 * terms + 3 * size]
+    value = chain(read("spread_z", LANES, place_ref[2])[:, :size], top)[:, :size]
+    left = chain(value, read("pick_z", size, place_ref[2])[:, : plan.top_rows])
+    lift_x, lift_y = (read(name, plan.out_cells)[:, :size] for name in ("lift_x", "lift_y"))
+    return left, chain(lift_x, along[0]) * chain(lift_y, along[1])
+
+
+def side_by_side(source, start, rows, count):
+    return jnp.concatenate([source[start + rows * at : start + rows * (at + 1)] for at in range(count)], axis=1)
+
+
+def gather_part(plan, terms, blocks, near, kf_refs, k1_refs, fine_at, coarse_at, before):
+    cells, near = split(blocks), split(near)
+    fine_cols = pl.ds(fine_at * LANES, blocks.shape[1])
+    fine = []
+    for term in range(terms):
+        value = dot_turned((kf_refs[0][term, :, fine_cols], kf_refs[1][term, :, fine_cols]), cells)
+        fine.append(value if before is None else before[0][term] + value)
+    cols = pl.ds(coarse_at * LANES, near[0].shape[1])
+    coarse = dot_turned((k1_refs[0][:, cols], k1_refs[1][:, cols]), near)
+    return fine, coarse if before is None else before[1][...] + coarse
+
+
+def near_kernel(plan, terms, cells_ref, sent_ref, kf_ref, kf_low_ref, k1_ref, k1_low_ref, fine_ref, coarse_ref):
     rows, window = plan.fine_rows, plan.window_rows
-    total = jnp.zeros((plan.brick[2], 2 * LANES), F32)
-    left = (zl_ref[...], zl_low_ref[...])
+    blocks = [cells_ref[part, at : at + rows] for part in range(2) for at in (0, rows)]
+    near = side_by_side(sent_ref, 2 * rows, window, 3)
+    fine, coarse = gather_part(plan, terms, jnp.concatenate(blocks, axis=1), near, (kf_ref, kf_low_ref),
+                               (k1_ref, k1_low_ref), 0, 0, None)
+    for term in range(terms):
+        fine_ref[term] = fine[term]
+    coarse_ref[...] = coarse
+
+
+def middle_kernel(plan, terms, fine_in_ref, coarse_in_ref, got_ref, kf_ref, kf_low_ref, k1_ref, k1_low_ref,
+                  fine_ref, coarse_ref):
+    rows, window = plan.fine_rows, plan.window_rows
+    blocks, near = side_by_side(got_ref, 0, rows, 2), side_by_side(got_ref, 2 * rows, window, 3)
+    fine, coarse = gather_part(plan, terms, blocks, near, (kf_ref, kf_low_ref), (k1_ref, k1_low_ref), 4, 3,
+                               (fine_in_ref, coarse_in_ref))
+    for term in range(terms):
+        fine_ref[term] = fine[term]
+    coarse_ref[...] = coarse
+
+
+def far_kernel(plan, terms, fine_in_ref, coarse_in_ref, sent_ref, got_ref, kf_ref, kf_low_ref, k1_ref, k1_low_ref,
+               zf_ref, zf_low_ref, z1_ref, z1_low_ref, zc_ref, kc_ref, table_ref, out_ref):
+    rows, window, half = plan.fine_rows, plan.window_rows, plan.half
+    blocks, near = side_by_side(got_ref, 0, rows, 2), side_by_side(got_ref, 2 * rows, window, 6)
+    fine, coarse = gather_part(plan, terms, blocks, near, (kf_ref, kf_low_ref), (k1_ref, k1_low_ref), 6, 6,
+                               (fine_in_ref, coarse_in_ref))
+    at = 2 * rows + 6 * window
+    top = jnp.concatenate([sent_ref[at : at + plan.top_rows], got_ref[at : at + plan.top_rows]], axis=1)
+    top = dot_split(split(zc_ref[...]), split(top))
+    level_one = dot_turned(split(kc_ref[...]), split(top))
+    total = None
+    for term in range(terms):
+        piece = split(coarse[term * plan.out_cells : (term + 1) * plan.out_cells])
+        level_one = level_one + dot_split(piece, (z1_ref[term], z1_low_ref[term]))
+        value = dot_split(split(fine[term]), (zf_ref[term], zf_low_ref[term]))
+        total = value if total is None else total + value
+    table = exact_tables(plan, table_ref)
+    back = dot_right(level_one, table("back", LANES))
+    total = total + dot_left(table("back_right", 2 * LANES)[:, : plan.out_cells], back)
     for part in range(2):
-        blocks = (cells_ref[part, :rows], cells_ref[part, rows:])
-        total = add_fine(plan, total, blocks, left, (kl_ref, kl_low_ref), part, terms)
-    fine_ref[...] = total
-    coarse = jnp.zeros((plan.out_rows, LANES), F32)
-    left = (z1_ref[...], z1_low_ref[...])
-    for part in range(3):
-        at = 2 * rows + part * window
-        coarse = add_coarse(plan, coarse, sent_ref[at : at + window], left, (k1_ref, k1_low_ref), part, terms)
-    coarse_ref[...] = coarse
-
-
-def far_kernel(plan, terms, fine_ref, coarse_ref, first_ref, sent_ref, second_ref, zl_ref, zl_low_ref, kl_ref,
-               kl_low_ref, z1_ref, z1_low_ref, k1_ref, k1_low_ref, zc_ref, zc_low_ref, kc_ref, kc_low_ref, back_ref,
-               back_right_ref, out_ref):
-    rows, window, bz = plan.fine_rows, plan.window_rows, plan.brick[2]
-    total = fine_ref[...]
-    left = (zl_ref[...], zl_low_ref[...])
-    for part, source in ((2, first_ref), (3, second_ref)):
-        blocks = (source[:rows], source[rows : 2 * rows])
-        total = add_fine(plan, total, blocks, left, (kl_ref, kl_low_ref), part, terms)
-    coarse = coarse_ref[...]
-    left = (z1_ref[...], z1_low_ref[...])
-    for part in range(9):
-        source, place = (first_ref, part) if part < 3 else (second_ref, part - 3)
-        at = 2 * rows + place * window
-        coarse = add_coarse(plan, coarse, source[at : at + window], left, (k1_ref, k1_low_ref), part + 3, terms)
-    at = 2 * rows + 6 * window
-    for part, source in ((0, sent_ref), (1, second_ref)):
-        along_z = dot_split((zc_ref[...], zc_low_ref[...]), split(source[at : at + plan.top_rows]))
-        place = pl.ds(part * LANES, LANES)
-        coarse = coarse + dot_split(split(along_z), (kc_ref[place], kc_low_ref[place]))
-    total = total + dot_right(dot_left(back_ref[...], coarse), back_right_ref[...])
-    half = plan.half
-    for part in range(2):
-        cells = total[:, part * LANES : (part + 1) * LANES].T
-        out_ref[:, part * half : (part + 1) * half, :] = cells.reshape(plan.brick[0], half, bz)
-
-
-def norms(exponents):
-    offsets = jnp.arange(-REACH, REACH + 1).astype(F32)
-    return 1.0 / jnp.sum(jnp.exp(-exponents[..., None] * offsets * offsets), axis=-1)
-
-
-def gauss_of(exponents, scales, squared):
-    return scales[:, None, None] * jnp.exp(-exponents[:, None, None] * squared[None])
-
-
-def squares(difference):
-    return jnp.where(jnp.abs(difference) <= REACH, (difference * difference).astype(F32), FAR)
-
-
-def wrapped(difference, count):
-    return (difference + count // 2 + 2 * count) % count - count // 2
-
-
-def fine_weights(plan, exponents, amplitudes, even_x, even_y):
-    bx, by, bz = plan.brick
-    half = plan.half
-    scale = norms(exponents)
-    z_in = np.concatenate([np.arange(bz), np.arange(-REACH, 0), bz + np.arange(REACH)])
-    left = gauss_of(exponents, scale, squares(jnp.asarray(z_in[None, :] - np.arange(bz)[:, None])))
-    row = jnp.arange(8 * LANES)[:, None]
-    col = jnp.arange(2 * LANES)[None, :]
-    lane, block, group = row % LANES, (row // LANES) % 2, row // (2 * LANES)
-    strip = lane // (LANES // 2)
-    to_right = (strip == 0) == even_x
-    x_far = jnp.where(to_right, bx, -REACH) + (lane % (LANES // 2)) // half
-    x_in = jnp.where(block == 0, lane // half, x_far)
-    y_far = jnp.where((group == 3) == even_y, by, -half)
-    y_in = jnp.where(group < 2, group * half, y_far) + lane % half
-    x_out, y_out = (col % LANES) // half, (col // LANES) * half + col % half
-    right = gauss_of(exponents, amplitudes * scale * scale, squares(x_in - x_out) + squares(y_in - y_out))
-    return split_wide(left.reshape(-1, plan.fine_rows)), split_wide(right)
-
-
-def coarse_weights(plan, exponents, amplitudes, even_x, even_y):
-    bx, by, bz = (size // 2 for size in plan.brick)
-    scale = norms(exponents)
-    z_in = np.arange(plan.window_rows) - GAUSSIAN_RIM
-    z_out = np.arange(plan.out_rows) - 1
-    distance = np.where((np.arange(plan.window_rows) < plan.window)[None, :], z_in[None, :] - z_out[:, None], 2 * REACH)
-    distance = np.where((np.arange(plan.out_rows) < plan.out_z)[:, None], distance, 2 * REACH)
-    left = gauss_of(exponents, scale, squares(jnp.asarray(distance)))
-    row = jnp.arange(12 * LANES)[:, None]
-    col = jnp.arange(LANES)[None, :]
-    lane, slot, group = row % LANES, (row // LANES) % 3, row // (3 * LANES)
-    cell = lane // plan.cy
-    to_right = (slot == 1) == even_x
-    toward = jnp.where(to_right, bx, -bx)
-    x_in = jnp.where(slot == 0, 0, toward) + cell - 1
-    extra = jnp.where(to_right, 2 * bx + bx - 1, -2 * bx - 1) + cell - plan.cx
-    x_in = jnp.where(cell >= plan.cx, extra, x_in)
-    used = cell < jnp.where(slot == 2, plan.cx + 2, plan.cx)
-    toward = jnp.where((group == 2) == even_y, by, -by)
-    y_in = jnp.where(group == 0, 0, jnp.where(group == 3, 2 * by, toward)) + lane % plan.cy - 1
-    x_out, y_out = col // plan.cy - 1, col % plan.cy - 1
-    squared = squares(wrapped(x_in - x_out, bx * plan.counts[0])) + squares(wrapped(y_in - y_out, by * plan.counts[1]))
-    squared = jnp.where(used & (col < plan.cx * plan.cy), squared, FAR)
-    right = gauss_of(exponents, amplitudes * scale * scale, squared)
-    return split_wide(left.reshape(-1, plan.window_rows)), split_wide(right)
-
-
-def top_weights(plan, place, top_x, top_y, top_z):
-    bx, by, bz = plan.brick
-    nx, ny, nz = plan.counts
-    four = (bx // 16, by // 16, bz // 16)
-
-    def spread(kernel, axis, rows):
-        whole = prolong_three_whole(kernel.shape[0])
-        size = plan.brick[axis] // 2
-        wide = np.concatenate([whole[-1:], whole, whole[: size + 8]], axis=0)
-        mine = lax.dynamic_slice(jnp.asarray(wide), (place[axis] * size, 0), (rows, kernel.shape[0]))
-        return jnp.dot(mine, kernel, precision=HIGHEST)
-
-    def pick(index, used, count):
-        return jnp.where((index[:, None] % count == jnp.arange(count)[None, :]) & used[:, None], 1.0, 0.0)
-
-    row = jnp.arange(plan.top_rows)
-    side, cell = row // (plan.top_rows // 2), row % (plan.top_rows // 2)
-    z_in = jnp.where(side == 0, place[2], nz - 1 - place[2]) * four[2] + cell - 1 + nz * four[2]
-    left = jnp.dot(
-        spread(top_z, 2, plan.out_rows), pick(z_in, cell < plan.top_z, nz * four[2]).T, precision=HIGHEST
-    )
-    row = jnp.arange(2 * LANES)
-    lane, partner = row % LANES, row // LANES
-    group, cell = lane // plan.group, lane % plan.group
-    used = cell < plan.top_x * plan.top_y
-    x_dev = place[0] ^ (group % 2) ^ (3 * ((group // 2) % 2))
-    y_dev = place[1] ^ partner ^ (3 * (group // 4))
-    x_in = x_dev * four[0] + cell // plan.top_y - 1 + nx * four[0]
-    y_in = y_dev * four[1] + cell % plan.top_y - 1 + ny * four[1]
-    along_x = jnp.dot(pick(x_in, used, nx * four[0]), spread(top_x, 0, plan.cx).T, precision=HIGHEST)
-    along_y = jnp.dot(pick(y_in, used, ny * four[1]), spread(top_y, 1, plan.cy).T, precision=HIGHEST)
-    col = np.arange(LANES)
-    cols_x = (np.arange(plan.cx)[:, None] == col[None, :] // plan.cy).astype(np.float32)
-    cols_y = (np.arange(plan.cy)[:, None] == col[None, :] % plan.cy).astype(np.float32)
-    right = jnp.dot(along_x, cols_x, precision=HIGHEST) * jnp.dot(along_y, cols_y, precision=HIGHEST)
-    return split_wide(left), split_wide(right)
-
-
-def call(body, shapes, *operands, scalars=0):
+        cells = total[part * LANES : (part + 1) * LANES]
+        out_ref[:, part * half : (part + 1) * half, :] = cells.reshape(plan.brick[0], half, plan.brick[2])
+
+
+def call(body, shapes, *operands, scalars=0, after=(), last=False, plain=False, scratch=()):
     specs = [pl.BlockSpec(memory_space=pltpu.SMEM)] * scalars
     specs += [pl.BlockSpec(memory_space=pltpu.VMEM)] * (len(operands) - scalars)
-    out = pl.pallas_call(
-        body,
-        out_shape=[jax.ShapeDtypeStruct(shape, F32) for shape in shapes],
+    if scratch:
+        specs[-1] = pl.BlockSpec(memory_space=pl.ANY)
+    specs += [pl.BlockSpec(memory_space=pl.ANY)] * len(after)
+
+    def keep(operand, space=pltpu.VMEM):
+        return pltpu.with_memory_space_constraint(operand, space)
+
+    if plain:
+        operands = tuple(keep(operand, pltpu.HBM) for operand in operands)
+    kept = list(operands) if plain else [keep(operand) for operand in operands[scalars:]]
+    kept = kept[scalars:] if plain else kept
+    kept += [keep(operand) for operand in after]
+    kinds = [shape if isinstance(shape[-1], int) else shape[0] for shape in shapes]
+    types = [F32 if isinstance(shape[-1], int) else shape[1] for shape in shapes]
+    first = len(operands)
+
+    def run(*refs):
+        body(*refs[:first], *refs[first + len(after) :])
+
+    return pl.pallas_call(
+        run,
+        out_shape=[
+            jax.ShapeDtypeStruct(kind, kept_as) if last else pltpu.VMEM(kind, kept_as)
+            for kind, kept_as in zip(kinds, types)
+        ],
         in_specs=specs,
         out_specs=[pl.BlockSpec(memory_space=pltpu.VMEM)] * len(shapes),
-    )(*operands)
-    return out
+        scratch_shapes=scratch,
+        compiler_params=pltpu.CompilerParams(vmem_limit_bytes=8 << 20),
+    )(*operands[:scalars], *kept)
 
 
 def pair(value, axis, bits):
@@ -559,11 +714,10 @@
 
 
 def local_short(plan, charges, exponents, amplitudes, top_x, top_y, top_z):
-    place = [lax.axis_index(axis) for axis in ("gx", "gy", "gz")]
-    where = jnp.stack(place).astype(jnp.int32)
-    even_x, even_y = place[0] % 2 == 0, place[1] % 2 == 0
+    where = jnp.stack([lax.axis_index(axis) for axis in ("gx", "gy", "gz")]).astype(jnp.int32)
     terms = exponents.shape[1]
     bx, by, bz = plan.brick
+    rows, window = plan.fine_rows, plan.window_rows
     bind = functools.partial
 
     own, sent_z = call(
@@ -572,30 +726,70 @@
         charges,
         *np_split(plan.top_left),
         *np_split(np.stack(plan.top_right)),
+        plain=True,
     )
     got_z = pair(sent_z, "gz", 1)
-    fine_left, fine_right = fine_weights(plan, exponents[0], amplitudes[0], even_x, even_y)
-    coarse_left, coarse_right = coarse_weights(plan, exponents[1], amplitudes[1], even_x, even_y)
-    top_left, top_right = top_weights(plan, place, top_x, top_y, top_z)
-
+    table = plan.constants((top_x, top_y, top_z))
+    table, params = call(
+        bind(setup_kernel, plan, terms),
+        [table.shape, (6 * terms + 3 * 16, LANES)],
+        exponents,
+        amplitudes,
+        top_x,
+        top_y,
+        top_z,
+        jnp.asarray(table),
+        scalars=2,
+        after=(sent_z,),
+        plain=True,
+        scratch=[pltpu.SemaphoreType.DMA],
+    )
     fine, sent_a = call(
         bind(spread_kernel, plan),
-        [(2, plan.fine_rows, LANES), (plan.message, LANES)],
+        [(2, rows, LANES), (plan.message, LANES)],
         where,
         own,
         sent_z,
         got_z,
-        jnp.asarray(plan.rest_left, BF16),
-        jnp.asarray(np.stack(plan.rest_right), BF16),
+        table,
         scalars=1,
     )
     got_a = pair(sent_a, "gx", 1)
-    (sent_b,) = call(bind(pass_kernel, plan), [(plan.message, LANES)], where, fine, sent_a, got_a, scalars=1)
+    kf = ((terms, 2 * LANES, 8 * LANES), BF16)
+    *kf, zf, zf_low = call(
+        bind(fine_weights_kernel, plan, terms),
+        [kf, kf, ((terms, rows, LANES), BF16), ((terms, rows, LANES), BF16)],
+        where,
+        params,
+        table,
+        scalars=1,
+        after=(sent_a,),
+    )
+    (sent_b,) = call(
+        bind(pass_kernel, plan), [(plan.message, LANES)], where, fine, sent_a, got_a, scalars=1, after=(zf,)
+    )
     got_b = pair(sent_b, "gx", 3)
-    size = 2 * plan.fine_rows + 3 * plan.window_rows + plan.top_rows
+    k1 = ((terms * plan.out_cells, 12 * LANES), BF16)
+    *k1, z1, z1_low, zc, kc = call(
+        bind(coarse_weights_kernel, plan, terms),
+        [
+            k1,
+            k1,
+            ((terms, window, LANES), BF16),
+            ((terms, window, LANES), BF16),
+            (LANES, plan.top_rows),
+            (plan.out_cells, 2 * LANES),
+        ],
+        where,
+        params,
+        table,
+        scalars=1,
+        after=(sent_b,),
+    )
+    size = 2 * rows + 3 * window + plan.top_rows
     cells, sent_c = call(
         bind(stack_kernel, plan),
-        [(2, 2 * plan.fine_rows, LANES), (size, LANES)],
+        [(2, 2 * rows, LANES), (size, LANES)],
         where,
         fine,
         sent_a,
@@ -603,29 +797,39 @@
         got_a,
         got_b,
         scalars=1,
+        after=(z1,),
     )
     got_c = pair(sent_c, "gy", 3)
-    weights = (*fine_left, *fine_right, *coarse_left, *coarse_right)
-    near_fine, near_coarse = call(
-        bind(near_kernel, plan, terms), [(bz, 2 * LANES), (plan.out_rows, LANES)], cells, sent_c, *weights
-    )
+    sums = [(terms, 2 * LANES, rows), (terms * plan.out_cells, window)]
+    near = call(bind(near_kernel, plan, terms), sums, cells, sent_c, *kf, *k1)
     (sent_d,) = call(
-        bind(share_kernel, plan), [(size + 3 * plan.window_rows, LANES)], where, cells, sent_c, got_c, scalars=1
+        bind(share_kernel, plan),
+        [(size + 3 * window, LANES)],
+        where,
+        cells,
+        sent_c,
+        got_c,
+        scalars=1,
+        after=(near[1],),
     )
     got_d = pair(sent_d, "gy", 1)
+    middle = call(bind(middle_kernel, plan, terms), sums, *near, got_c, *kf, *k1, after=(sent_d,))
     (out,) = call(
         bind(far_kernel, plan, terms),
         [(bx, by, bz)],
-        near_fine,
-        near_coarse,
-        got_c,
+        *middle,
         sent_d,
         got_d,
-        *weights,
-        *top_left,
-        *top_right,
-        jnp.asarray(plan.back_left, BF16),
-        jnp.asarray(plan.back_right, BF16),
+        *kf,
+        *k1,
+        zf,
+        zf_low,
+        z1,
+        z1_low,
+        zc,
+        kc,
+        table,
+        last=True,
     )
     return out
 
@@ -638,7 +842,7 @@
 def local(*arguments):
     counts = tuple(lax.axis_size(axis) for axis in ("gx", "gy", "gz"))
     brick = arguments[0].shape
-    if fits(brick, counts):
+    if fits(brick, counts, arguments[3:]):
         return local_short(Plan(brick, counts), *arguments)
     return local_any(*arguments)
 

time: 71.1 us -> 36.4 us (0.51)
  other arithmetic: 12.5 us -> 0.08 us
  Pallas kernels: 27.2 us -> 15.1 us
  local copies, waits for them, and re-layouts: 4.6 us -> 0.59 us
  matrix products: 3.7 us -> 0 us
  waiting for transfers between devices: 14.4 us -> 11 us
  starting transfers between devices: 8.26 us -> 9.41 us
    pallas_call x7 -> x11, Pallas kernels: 27.2 us -> 15.1 us  [call(): pl.pallas_call(run, out_shape=[jax.ShapeDtypeStruct(kind, kept_as) if las...]
    convert_element_type x6 -> x0, other arithmetic: 8.13 us -> none  [the longest x5 8.13 us: split_wide(): return (high.astype(BF16), (value - high).astype(BF16))]
    dot_general x8 -> x0, matrix products: 3.7 us -> none  [the longest x3 1.36 us: spread(): return jnp.dot(mine, kernel, precision=HIGHEST)]
    unnamed x26 -> x0, local copies, waits for them, and re-layouts: 3.47 us -> none
    ppermute x5, waiting for transfers between devices: 14.4 us -> 11 us  [pair(): return lax.ppermute(value, axis, [(i, i ^ bits) for i in range(count)])]
    select_n x5 -> x0, other arithmetic: 1.31 us -> none  [the longest x1 1.24 us: coarse_weights(): squared = jnp.where(used & (col < plan.cx * plan.cy), squared, FAR)]
    ppermute x5, starting transfers between devices: 8.26 us -> 9.41 us  [pair(): return lax.ppermute(value, axis, [(i, i ^ bits) for i in range(count)])]
    mul x1 -> x0, other arithmetic: 0.77 us -> none  [coarse_weights(): right = gauss_of(exponents, amplitudes * scale * scale, squared)]
  transfers between devices with their start and end apart: 5 -> 5, of which waited for: 3 -> 4; matrix products, arithmetic and copies ran while one was open for 24% -> 0% of each run, Pallas kernels for 11% -> 22%
where the time goes in v2:
time: 36.4 us; the launch traced here: 36.2 us
  Pallas kernels  15.1 us (41%)
  waiting for transfers between devices  11 us (30%)
  starting transfers between devices  9.41 us (26%)
  local copies, waits for them, and re-layouts  0.59 us (2%)
    pallas_call x11, Pallas kernels, call(): pl.pallas_call(run, out_shape=[jax.ShapeDtypeStruct(kind, kept_as) if las...  15.1 us
    ppermute x5, waiting for transfers between devices, pair(): return lax.ppermute(value, axis, [(i, i ^ bits) for i in range(count)])  11 us
    ppermute x5, starting transfers between devices, pair(): return lax.ppermute(value, axis, [(i, i ^ bits) for i in range(count)])  9.41 us
  transfers between devices with their start and end apart: 5, of which 4 were waited for; matrix products, arithmetic and copies ran while one was open for 0% of the time, Pallas kernels for 22%

profile of v2, /device:TPU:0, one launch (start us, length us, event | category | flops | bytes accessed | tf_op | source)
XLA Modules:
  0.0 36.2 jit_solution(5781723251622476784)
XLA Ops:
  0.0 0.6 %jit_solution_.3.refs_2_ = bf16[16,128]{1,0:T(8,128)(2,1)} broadcast(bf16[]{:T(256)} %constant.22.clone), dimensions={} | broadcast | bytes 4098 | tf_op jit(solution)
  0.6 1.4 %shard_map.109 = (f32[2,128,128]{2,1,0:T(8,128)S(1)}, f32[112,128]{1,0:T(8,128)S(1)}) custom-call(f32[16,16,128]{2,1,0:T(8,128)} %refs_0_.2, bf16[16,128]{1,0:T(8,128)(2,1)} %constant.21.clone.refs_1_, bf16[16,128]{1,0:T(8,128)(2,1)} %jit_solution_.3.refs_2_, bf16[2,128,128]{2,1,0:T(8,128)(2,1)} %constant.23.clone.refs_3_, ...), custom_call_target="tpu_custom_call" | custom-call | tf_op jit(solution)/shard_map/pallas_call | solution.py:698
  2.0 3.0 %collective-permute-start = (f32[112,128]{1,0:T(8,128)S(1)}, f32[112,128]{1,0:T(8,128)S(1)}, u32[]{:S(2)}, u32[]{:S(2)}) collective-permute-start(f32[112,128]{1,0:T(8,128)S(1)} %get-tuple-element.28.refs_6_.refs_2_), channel_id=1, source_target_pairs={{0,1},{1,0},{2,3},{3,2},{4,5},{5,4},{6,7},{7,6},{8,9},{9,8},{10,11... | collective-permute-start | bytes 172040 | tf_op jit(solution)/shard_map/ppermute | solution.py:713
  5.0 2.1 %shard_map.110 = (f32[2336,128]{1,0:T(8,128)S(1)}, f32[72,128]{1,0:T(8,128)S(1)}) custom-call(f32[2,4]{1,0:T(2,128)} %refs_0_.3, f32[2,4]{1,0:T(2,128)} %refs_1_.2, f32[4,4]{1,0:T(4,128)} %refs_2_.2, f32[4,4]{1,0:T(4,128)} %refs_3_.2, f32[16,16]{1,0:T(8,128)} %refs_4_.2, f32[2336,128]{1,0:T(8,128)} %constant.25.clone.refs_5_, ...), custom_call_target="tpu_custom_call" | custom-call | tf_op jit(solution)/shard_map/pallas_call | solution.py:698
  7.1 0.1 pad_add_fusion.refs_0_
  7.2 0.0 collective-permute-done.refs_3_
  7.2 0.9 %shard_map.111 = (f32[2,144,128]{2,1,0:T(8,128)S(1)}, f32[264,128]{1,0:T(8,128)S(1)}) custom-call(s32[3]{0:T(128)S(1)} %pad_add_fusion.refs_0_, f32[2,128,128]{2,1,0:T(8,128)S(1)} %get-tuple-element.27.refs_1_, f32[112,128]{1,0:T(8,128)S(1)} %get-tuple-element.28.refs_6_.refs_2_, f32[112,128]{1,0:T(8,128)S(1)} %collective-permute-done.refs_3_, ...), custom_call_target="tpu_custom_call" | custom-call | tf_op jit(solution)/shard_map/pallas_call | solution.py:698
  8.1 2.1 %collective-permute-start.1 = (f32[264,128]{1,0:T(8,128)S(1)}, f32[264,128]{1,0:T(8,128)S(1)}, u32[]{:S(2)}, u32[]{:S(2)}) collective-permute-start(f32[264,128]{1,0:T(8,128)S(1)} %get-tuple-element.31.refs_3_.refs_2_), channel_id=1, source_target_pairs={{0,8},{8,0},{16,24},{24,16},{1,9},{9,1},{17,25},{25,17},{2,10},{10... | collective-permute-start | bytes 405512 | tf_op jit(solution)/shard_map/ppermute | solution.py:713
  10.2 1.8 %shard_map.112 = (bf16[4,256,1024]{2,1,0:T(8,128)(2,1)S(1)}, bf16[4,256,1024]{2,1,0:T(8,128)(2,1)S(1)}, bf16[4,144,128]{2,1,0:T(8,128)(2,1)S(1)}, bf16[4,144,128]{2,1,0:T(8,128)(2,1)S(1)}) custom-call(s32[3]{0:T(128)S(1)} %pad_add_fusion.refs_0_, f32[72,128]{1,0:T(8,128)S(1)} %get-tuple-element.32.refs_1_, ...), custom_call_target="tpu_custom_call" | custom-call | tf_op jit(solution)/shard_map/pallas_call | solution.py:698
  12.0 1.2 %collective-permute-done.1.refs_3_.refs_4_ = f32[264,128]{1,0:T(8,128)S(1)} collective-permute-done((f32[264,128]{1,0:T(8,128)S(1)}, f32[264,128]{1,0:T(8,128)S(1)}, u32[]{:S(2)}, u32[]{:S(2)}) %collective-permute-start.1) | collective-permute-done | bytes 135200 | tf_op jit(solution)/shard_map/ppermute | solution.py:713
  13.2 0.7 %shard_map.113.refs_3_ = f32[264,128]{1,0:T(8,128)S(1)} custom-call(s32[3]{0:T(128)S(1)} %pad_add_fusion.refs_0_, f32[2,144,128]{2,1,0:T(8,128)S(1)} %get-tuple-element.30.refs_1_, f32[264,128]{1,0:T(8,128)S(1)} %get-tuple-element.31.refs_3_.refs_2_, f32[264,128]{1,0:T(8,128)S(1)} %collective-permute-done.1.refs_3_.refs_4_, ...), custom_call_target="tpu_custom_call" | custom-call | tf_op jit(solution)/shard_map/pallas_call | solution.py:698
  13.9 4.1 %collective-permute-start.2 = (f32[264,128]{1,0:T(8,128)S(1)}, f32[264,128]{1,0:T(8,128)S(1)}, u32[]{:S(2)}, u32[]{:S(2)}) collective-permute-start(f32[264,128]{1,0:T(8,128)S(1)} %shard_map.113.refs_3_), channel_id=1, source_target_pairs={{0,24},{8,16},{16,8},{24,0},{1,25},{9,17},{17,9},{25,1},{2,26},{10... | collective-permute-start | bytes 405512 | tf_op jit(solution)/shard_map/ppermute | solution.py:713
  18.0 2.0 %shard_map.114 = (bf16[448,1536]{1,0:T(8,128)(2,1)S(1)}, bf16[448,1536]{1,0:T(8,128)(2,1)S(1)}, bf16[4,88,128]{2,1,0:T(8,128)(2,1)S(1)}, bf16[4,88,128]{2,1,0:T(...) custom-call(s32[3]{0:T(128)S(1)} %pad_add_fusion.refs_0_, f32[72,128]{1,0:T(8,128)S(1)} %get-tuple-element.32.refs_1_, ...), custom_call_target="tpu_custom_call" | custom-call | tf_op jit(solution)/shard_map/pallas_call | solution.py:698
  20.0 1.1 %collective-permute-done.2.refs_5_ = f32[264,128]{1,0:T(8,128)S(1)} collective-permute-done((f32[264,128]{1,0:T(8,128)S(1)}, f32[264,128]{1,0:T(8,128)S(1)}, u32[]{:S(2)}, u32[]{:S(2)}) %collective-permute-start.2) | collective-permute-done | bytes 135200 | tf_op jit(solution)/shard_map/ppermute | solution.py:713
  21.1 0.6 %shard_map.115 = (f32[2,288,128]{2,1,0:T(8,128)S(1)}, f32[584,128]{1,0:T(8,128)S(1)}) custom-call(s32[3]{0:T(128)S(1)} %pad_add_fusion.refs_0_, f32[2,144,128]{2,1,0:T(8,128)S(1)} %get-tuple-element.30.refs_1_, f32[264,128]{1,0:T(8,128)S(1)} %get-tuple-element.31.refs_3_.refs_2_, f32[264,128]{1,0:T(8,128)S(1)} %shard_map.113.refs_3_, ...), custom_call_target="tpu_custom_call" | custom-call | tf_op jit(solution)/shard_map/pallas_call | solution.py:698
  21.8 0.1 collective-permute-start.3
  21.8 1.3 %shard_map.116 = (f32[4,256,144]{2,1,0:T(8,128)S(1)}, f32[448,88]{1,0:T(8,128)S(1)}) custom-call(f32[2,288,128]{2,1,0:T(8,128)S(1)} %get-tuple-element.35.refs_0_.refs_1_, f32[584,128]{1,0:T(8,128)S(1)} %get-tuple-element.36.refs_1_.refs_2_, bf16[4,256,1024]{2,1,0:T(8,128)(2,1)S(1)} %get-tuple-element.37.refs_2_.refs_3_.refs_4_, ...), custom_call_target="tpu_custom_call" | custom-call | tf_op jit(solution)/shard_map/pallas_call | solution.py:698
  23.1 7.8 %collective-permute-done.3.refs_3_.refs_2_ = f32[584,128]{1,0:T(8,128)S(1)} collective-permute-done((f32[584,128]{1,0:T(8,128)S(1)}, f32[584,128]{1,0:T(8,128)S(1)}, u32[]{:S(2)}, u32[]{:S(2)}) %collective-permute-start.3) | collective-permute-done | bytes 299040 | tf_op jit(solution)/shard_map/ppermute | solution.py:713
  30.9 0.6 %shard_map.117.refs_7_.refs_2_ = f32[848,128]{1,0:T(8,128)S(1)} custom-call(s32[3]{0:T(128)S(1)} %pad_add_fusion.refs_0_, f32[2,288,128]{2,1,0:T(8,128)S(1)} %get-tuple-element.35.refs_0_.refs_1_, f32[584,128]{1,0:T(8,128)S(1)} %get-tuple-element.36.refs_1_.refs_2_, f32[584,128]{1,0:T(8,128)S(1)} %collective-permute-done.3.refs_3_.refs_2_, ...), custom_call_target="tpu_custom_call" | custom-call | tf_op jit(solution)/shard_map/pallas_call | solution.py:698
  31.5 0.2 collective-permute-start.4
  31.7 0.9 %shard_map.118 = (f32[4,256,144]{2,1,0:T(8,128)S(1)}, f32[448,88]{1,0:T(8,128)S(1)}) custom-call(f32[4,256,144]{2,1,0:T(8,128)S(1)} %get-tuple-element.41.refs_0_, f32[448,88]{1,0:T(8,128)S(1)} %get-tuple-element.42.refs_4_.refs_1_, f32[584,128]{1,0:T(8,128)S(1)} %collective-permute-done.3.refs_3_.refs_2_, ...), custom_call_target="tpu_custom_call" | custom-call | tf_op jit(solution)/shard_map/pallas_call | solution.py:698
  32.6 0.8 %collective-permute-done.4.refs_3_ = f32[848,128]{1,0:T(8,128)S(1)} collective-permute-done((f32[848,128]{1,0:T(8,128)S(1)}, f32[848,128]{1,0:T(8,128)S(1)}, u32[]{:S(2)}, u32[]{:S(2)}) %collective-permute-start.4) | collective-permute-done | bytes 434208 | tf_op jit(solution)/shard_map/ppermute | solution.py:713
  33.4 2.9 %shard_map.119 = f32[16,16,128]{2,1,0:T(8,128)} custom-call(f32[4,256,144]{2,1,0:T(8,128)S(1)} %get-tuple-element.43.refs_0_, f32[448,88]{1,0:T(8,128)S(1)} %get-tuple-element.44.refs_1_, f32[848,128]{1,0:T(8,128)S(1)} %shard_map.117.refs_7_.refs_2_, f32[848,128]{1,0:T(8,128)S(1)} %collective-permute-done.4.refs_3_, ...), custom_call_target="tpu_custom_call" | custom-call | tf_op jit(solution)/shard_map/pallas_call | solution.py:698
Async XLA Ops:
  2.0 5.2 %collective-permute-start = (f32[112,128]{1,0:T(8,128)S(1)}, f32[112,128]{1,0:T(8,128)S(1)}, u32[]{:S(2)}, u32[]{:S(2)}) collective-permute-start(f32[112,128]{1,0:T(8,128)S(1)} %get-tuple-element.28.refs_6_.refs_2_), channel_id=1, source_target_pairs={{0,1},{1,0},{2,3},{3,2},{4,5},{5,4},{6,7},{7,6},{8,9},{9,8},{10,11... | collective-permute-start | bytes 172040 | tf_op jit(solution)/shard_map/ppermute | solution.py:713
  8.1 5.1 %collective-permute-start.1 = (f32[264,128]{1,0:T(8,128)S(1)}, f32[264,128]{1,0:T(8,128)S(1)}, u32[]{:S(2)}, u32[]{:S(2)}) collective-permute-start(f32[264,128]{1,0:T(8,128)S(1)} %get-tuple-element.31.refs_3_.refs_2_), channel_id=1, source_target_pairs={{0,8},{8,0},{16,24},{24,16},{1,9},{9,1},{17,25},{25,17},{2,10},{10... | collective-permute-start | bytes 405512 | tf_op jit(solution)/shard_map/ppermute | solution.py:713
  13.9 7.2 %collective-permute-start.2 = (f32[264,128]{1,0:T(8,128)S(1)}, f32[264,128]{1,0:T(8,128)S(1)}, u32[]{:S(2)}, u32[]{:S(2)}) collective-permute-start(f32[264,128]{1,0:T(8,128)S(1)} %shard_map.113.refs_3_), channel_id=1, source_target_pairs={{0,24},{8,16},{16,8},{24,0},{1,25},{9,17},{17,9},{25,1},{2,26},{10... | collective-permute-start | bytes 405512 | tf_op jit(solution)/shard_map/ppermute | solution.py:713
  21.8 9.2 %collective-permute-start.3 = (f32[584,128]{1,0:T(8,128)S(1)}, f32[584,128]{1,0:T(8,128)S(1)}, u32[]{:S(2)}, u32[]{:S(2)}) collective-permute-start(f32[584,128]{1,0:T(8,128)S(1)} %get-tuple-element.36.refs_1_.refs_2_), channel_id=1, source_target_pairs={{0,6},{2,4},{4,2},{6,0},{1,7},{3,5},{5,3},{7,1},{8,14},{10,12},{12... | collective-permute-start | bytes 897032 | tf_op jit(solution)/shard_map/ppermute | solution.py:713
  31.5 1.8 %collective-permute-start.4 = (f32[848,128]{1,0:T(8,128)S(1)}, f32[848,128]{1,0:T(8,128)S(1)}, u32[]{:S(2)}, u32[]{:S(2)}) collective-permute-start(f32[848,128]{1,0:T(8,128)S(1)} %shard_map.117.refs_7_.refs_2_), channel_id=1, source_target_pairs={{0,2},{2,0},{4,6},{6,4},{1,3},{3,1},{5,7},{7,5},{8,10},{10,8},{12,... | collective-permute-start | bytes 1302536 | tf_op jit(solution)/shard_map/ppermute | solution.py:713

commit v3 on v2

--- a/solution.py
+++ b/solution.py
@@ -398,17 +398,18 @@
     )
 
 
-def start_kernel(plan, charges_ref, left_ref, left_low_ref, right_ref, right_low_ref, own_ref, out_ref):
+def start_kernel(plan, charges_ref, table_ref, own_ref, out_ref):
     bx, by, bz = plan.brick
     rim, half = plan.rim, plan.half
-    top = None
+    top, size = None, plan.top_rows // 2
+    left = split(table_ref[:size])
     for part in range(2):
         cells = charges_ref[:, part * half : (part + 1) * half, :].reshape(LANES, bz).T
         own_ref[part] = cells
         out_ref[2 * rim * part : 2 * rim * part + rim] = cells[:rim]
         out_ref[2 * rim * part + rim : 2 * rim * (part + 1)] = cells[bz - rim :]
-        rows = dot_split((left_ref[...], left_low_ref[...]), split(cells))
-        rows = dot_split(split(rows), (right_ref[part], right_low_ref[part]))
+        right = split(table_ref[size + LANES * part : size + LANES * (part + 1)])
+        rows = dot_split(split(dot_split(left, split(cells))), right)
         top = rows if top is None else top + rows
     out_ref[4 * rim :] = top
 
@@ -437,7 +438,8 @@
     copy.wait()
 
 
-def spread_kernel(plan, place_ref, own_ref, sent_ref, got_ref, table_ref, fine_ref, out_ref):
+def spread_kernel(plan, place_ref, own_ref, sent_ref, got_ref, table_ref, fine_ref, out_ref, side_x_ref,
+                  side_y_ref):
     bx, by, bz = plan.brick
     rim, rows = plan.rim, plan.fine_rows
     table = exact_tables(plan, table_ref)
@@ -455,17 +457,18 @@
     low, high = halves(fine_ref[0], fine_ref[1])
     even = place_ref[0] % 2 == 0
     out_ref[:rows] = jnp.where(even, high, low)
+    side_x_ref[...] = jnp.where(even, low, high)
+    side_y_ref[:rows] = jnp.where(place_ref[1] % 2 == 0, fine_ref[0], fine_ref[1])
+    side_y_ref[rows:] = coarse
     out_ref[rows : rows + plan.window_rows] = coarse
     top = rows + plan.window_rows
     out_ref[top : top + plan.top_rows // 2] = sent_ref[4 * rim :]
     out_ref[top + plan.top_rows // 2 :] = got_ref[4 * rim :]
 
 
-def pass_kernel(plan, place_ref, fine_ref, sent_ref, got_ref, out_ref):
+def pass_kernel(plan, place_ref, sent_ref, got_ref, out_ref):
     rows = plan.fine_rows
     even = place_ref[0] % 2 == 0
-    low, high = halves(fine_ref[0], fine_ref[1])
-    out_ref[:rows] = jnp.where(even, low, high)
     own = sent_ref[rows : rows + plan.window_rows]
     far = got_ref[rows : rows + plan.window_rows]
     lane = lanes_of(plan.window_rows)
@@ -475,34 +478,33 @@
     right = right + jnp.where((lane >= all_lanes) & (lane < all_lanes + edge), pltpu.roll(far, edge, 1), 0.0)
     left = own + jnp.where(lane < edge, pltpu.roll(far, LANES - last, 1), 0.0)
     left = left + jnp.where((lane >= all_lanes) & (lane < all_lanes + edge), pltpu.roll(far, all_lanes, 1), 0.0)
-    out_ref[rows : rows + plan.window_rows] = jnp.where(even, right, left)
+    out_ref[: plan.window_rows] = jnp.where(even, right, left)
     top = rows + plan.window_rows
-    out_ref[top:] = sent_ref[top:] + pltpu.roll(got_ref[top:], plan.group, 1)
-
-
-def stack_kernel(plan, place_ref, fine_ref, first_sent_ref, sent_ref, first_ref, second_ref, cells_ref, out_ref):
+    out_ref[plan.window_rows :] = sent_ref[top:] + pltpu.roll(got_ref[top:], plan.group, 1)
+
+
+def stack_kernel(plan, place_ref, fine_ref, sent_ref, first_ref, side_ref, second_ref, cells_ref, out_ref):
     rows, window = plan.fine_rows, plan.window_rows
-    low, high = halves(first_ref[:rows], second_ref[:rows])
+    low, high = halves(first_ref[:rows], side_ref[...])
     for part, other in ((0, low), (1, high)):
         cells_ref[part, :rows] = fine_ref[part]
         cells_ref[part, rows:] = other
-    even = place_ref[1] % 2 == 0
-    out_ref[: 2 * rows] = jnp.where(even, cells_ref[0], cells_ref[1])
-    at = 2 * rows
-    for source in (first_sent_ref, first_ref, second_ref):
-        out_ref[at : at + window] = source[rows : rows + window]
-        at = at + window
-    out_ref[at:] = sent_ref[rows + window :] + pltpu.roll(second_ref[rows + window :], 2 * plan.group, 1)
-
-
-def share_kernel(plan, place_ref, cells_ref, sent_ref, got_ref, out_ref):
+    out_ref[:rows] = jnp.where(place_ref[1] % 2 == 0, low, high)
+    out_ref[rows : rows + window] = first_ref[rows : rows + window]
+    out_ref[rows + window : rows + 2 * window] = second_ref[:window]
+    out_ref[rows + 2 * window :] = sent_ref[window:] + pltpu.roll(second_ref[window:], 2 * plan.group, 1)
+
+
+def share_kernel(plan, place_ref, cells_ref, own_ref, sent_ref, side_ref, got_ref, out_ref):
     rows, window = plan.fine_rows, plan.window_rows
     even = place_ref[1] % 2 == 0
     out_ref[: 2 * rows] = jnp.where(even, cells_ref[1], cells_ref[0])
-    at, size = 2 * rows, 3 * window
-    out_ref[at : at + size] = sent_ref[at : at + size]
-    out_ref[at + size : at + 2 * size] = got_ref[at : at + size]
-    out_ref[at + 2 * size :] = sent_ref[at + size :] + pltpu.roll(got_ref[at + size :], 4 * plan.group, 1)
+    at = 2 * rows
+    for source, start, count in ((own_ref, rows, 1), (sent_ref, rows, 2), (side_ref, rows, 1), (got_ref, rows, 2)):
+        out_ref[at : at + count * window] = source[start : start + count * window]
+        at = at + count * window
+    start = rows + 2 * window
+    out_ref[at:] = sent_ref[start:] + pltpu.roll(got_ref[start:], 4 * plan.group, 1)
 
 
 def dot_turned(left, right):
@@ -627,10 +629,11 @@
     return fine, coarse if before is None else before[1][...] + coarse
 
 
-def near_kernel(plan, terms, cells_ref, sent_ref, kf_ref, kf_low_ref, k1_ref, k1_low_ref, fine_ref, coarse_ref):
+def near_kernel(plan, terms, cells_ref, own_ref, first_ref, second_ref, kf_ref, kf_low_ref, k1_ref, k1_low_ref, fine_ref, coarse_ref):
     rows, window = plan.fine_rows, plan.window_rows
     blocks = [cells_ref[part, at : at + rows] for part in range(2) for at in (0, rows)]
-    near = side_by_side(sent_ref, 2 * rows, window, 3)
+    near = [own_ref[rows : rows + window], first_ref[rows : rows + window], second_ref[:window]]
+    near = jnp.concatenate(near, axis=1)
     fine, coarse = gather_part(plan, terms, jnp.concatenate(blocks, axis=1), near, (kf_ref, kf_low_ref),
                                (k1_ref, k1_low_ref), 0, 0, None)
     for term in range(terms):
@@ -638,10 +641,11 @@
     coarse_ref[...] = coarse
 
 
-def middle_kernel(plan, terms, fine_in_ref, coarse_in_ref, got_ref, kf_ref, kf_low_ref, k1_ref, k1_low_ref,
+def middle_kernel(plan, terms, fine_in_ref, coarse_in_ref, side_ref, got_ref, kf_ref, kf_low_ref, k1_ref, k1_low_ref,
                   fine_ref, coarse_ref):
     rows, window = plan.fine_rows, plan.window_rows
-    blocks, near = side_by_side(got_ref, 0, rows, 2), side_by_side(got_ref, 2 * rows, window, 3)
+    blocks = jnp.concatenate([side_ref[:rows], got_ref[:rows]], axis=1)
+    near = jnp.concatenate([side_ref[rows:], side_by_side(got_ref, rows, window, 2)], axis=1)
     fine, coarse = gather_part(plan, terms, blocks, near, (kf_ref, kf_low_ref), (k1_ref, k1_low_ref), 4, 3,
                                (fine_in_ref, coarse_in_ref))
     for term in range(terms):
@@ -724,8 +728,7 @@
         bind(start_kernel, plan),
         [(2, bz, LANES), (4 * plan.rim + plan.top_rows // 2, LANES)],
         charges,
-        *np_split(plan.top_left),
-        *np_split(np.stack(plan.top_right)),
+        jnp.asarray(np.concatenate([plan.top_left, *plan.top_right])),
         plain=True,
     )
     got_z = pair(sent_z, "gz", 1)
@@ -744,9 +747,9 @@
         plain=True,
         scratch=[pltpu.SemaphoreType.DMA],
     )
-    fine, sent_a = call(
+    fine, sent_a, side_x, side_y = call(
         bind(spread_kernel, plan),
-        [(2, rows, LANES), (plan.message, LANES)],
+        [(2, rows, LANES), (plan.message, LANES), (rows, LANES), (rows + window, LANES)],
         where,
         own,
         sent_z,
@@ -755,18 +758,10 @@
         scalars=1,
     )
     got_a = pair(sent_a, "gx", 1)
-    kf = ((terms, 2 * LANES, 8 * LANES), BF16)
-    *kf, zf, zf_low = call(
-        bind(fine_weights_kernel, plan, terms),
-        [kf, kf, ((terms, rows, LANES), BF16), ((terms, rows, LANES), BF16)],
-        where,
-        params,
-        table,
-        scalars=1,
-        after=(sent_a,),
-    )
+    got_x = pair(side_x, "gx", 3)
+    got_y = pair(side_y, "gy", 3)
     (sent_b,) = call(
-        bind(pass_kernel, plan), [(plan.message, LANES)], where, fine, sent_a, got_a, scalars=1, after=(zf,)
+        bind(pass_kernel, plan), [(plan.message - rows, LANES)], where, sent_a, got_a, scalars=1
     )
     got_b = pair(sent_b, "gx", 3)
     k1 = ((terms * plan.out_cells, 12 * LANES), BF16)
@@ -786,34 +781,46 @@
         scalars=1,
         after=(sent_b,),
     )
-    size = 2 * rows + 3 * window + plan.top_rows
+    size = rows + 2 * window + plan.top_rows
     cells, sent_c = call(
         bind(stack_kernel, plan),
         [(2, 2 * rows, LANES), (size, LANES)],
         where,
         fine,
-        sent_a,
         sent_b,
         got_a,
+        got_x,
         got_b,
         scalars=1,
-        after=(z1,),
+        after=(z1, got_y),
     )
     got_c = pair(sent_c, "gy", 3)
+    kf = ((terms, 2 * LANES, 8 * LANES), BF16)
+    *kf, zf, zf_low = call(
+        bind(fine_weights_kernel, plan, terms),
+        [kf, kf, ((terms, rows, LANES), BF16), ((terms, rows, LANES), BF16)],
+        where,
+        params,
+        table,
+        scalars=1,
+        after=(sent_c,),
+    )
     sums = [(terms, 2 * LANES, rows), (terms * plan.out_cells, window)]
-    near = call(bind(near_kernel, plan, terms), sums, cells, sent_c, *kf, *k1)
+    near = call(bind(near_kernel, plan, terms), sums, cells, sent_a, got_a, got_b, *kf, *k1, after=(sent_c,))
     (sent_d,) = call(
         bind(share_kernel, plan),
-        [(size + 3 * window, LANES)],
+        [(2 * rows + 6 * window + plan.top_rows, LANES)],
         where,
         cells,
+        sent_a,
         sent_c,
+        got_y,
         got_c,
         scalars=1,
         after=(near[1],),
     )
     got_d = pair(sent_d, "gy", 1)
-    middle = call(bind(middle_kernel, plan, terms), sums, *near, got_c, *kf, *k1, after=(sent_d,))
+    middle = call(bind(middle_kernel, plan, terms), sums, *near, got_y, got_c, *kf, *k1, after=(sent_d,))
     (out,) = call(
         bind(far_kernel, plan, terms),
         [(bx, by, bz)],
@@ -834,11 +841,6 @@
     return out
 
 
-def np_split(table):
-    high = table.astype(BF16)
-    return jnp.asarray(high), jnp.asarray((table - high.astype(np.float32)).astype(BF16))
-
-
 def local(*arguments):
     counts = tuple(lax.axis_size(axis) for axis in ("gx", "gy", "gz"))
     brick = arguments[0].shape

time: 36.4 us -> 33 us (0.907)
  waiting for transfers between devices: 11 us -> 5.74 us
  starting transfers between devices: 9.41 us -> 11.8 us
  local copies, waits for them, and re-layouts: 0.59 us -> 0 us
    ppermute x5 -> x7, waiting for transfers between devices: 11 us -> 5.74 us  [pair(): return lax.ppermute(value, axis, [(i, i ^ bits) for i in range(count)])]
    ppermute x5 -> x7, starting transfers between devices: 9.41 us -> 11.8 us  [pair(): return lax.ppermute(value, axis, [(i, i ^ bits) for i in range(count)])]
    another operation x1 -> x0, local copies, waits for them, and re-layouts: 0.59 us -> none
  transfers between devices with their start and end apart: 5 -> 7, of which waited for: 4 -> 4; matrix products, arithmetic and copies ran while one was open for 0% -> 0% of each run, Pallas kernels for 22% -> 26%
where the time goes in v3:
time: 33 us; the launch traced here: 32.8 us
  Pallas kernels  15.1 us (46%)
  starting transfers between devices  11.8 us (36%)
  waiting for transfers between devices  5.74 us (17%)
    pallas_call x11, Pallas kernels, call(): pl.pallas_call(run, out_shape=[jax.ShapeDtypeStruct(kind, kept_as) if las...  15.1 us
    ppermute x7, starting transfers between devices, pair(): return lax.ppermute(value, axis, [(i, i ^ bits) for i in range(count)])  11.8 us
    ppermute x7, waiting for transfers between devices, pair(): return lax.ppermute(value, axis, [(i, i ^ bits) for i in range(count)])  5.74 us
  transfers between devices with their start and end apart: 7, of which 4 were waited for; matrix products, arithmetic and copies ran while one was open for 0% of the time, Pallas kernels for 26%

profile of v3, /device:TPU:0, one launch (start us, length us, event | category | flops | bytes accessed | tf_op | source)
XLA Modules:
  0.0 32.8 jit_solution(12592780901634515867)
XLA Ops:
  0.0 1.4 %shard_map.82 = (f32[2,128,128]{2,1,0:T(8,128)S(1)}, f32[112,128]{1,0:T(8,128)S(1)}) custom-call(f32[16,16,128]{2,1,0:T(8,128)} %refs_0_.2, f32[272,128]{1,0:T(8,128)} %constant.15.clone.refs_1_), custom_call_target="tpu_custom_call" | custom-call | tf_op jit(solution)/shard_map/pallas_call | solution.py:702
  1.4 3.0 %collective-permute-start = (f32[112,128]{1,0:T(8,128)S(1)}, f32[112,128]{1,0:T(8,128)S(1)}, u32[]{:S(2)}, u32[]{:S(2)}) collective-permute-start(f32[112,128]{1,0:T(8,128)S(1)} %get-tuple-element.30.refs_6_.refs_2_), channel_id=1, source_target_pairs={{0,1},{1,0},{2,3},{3,2},{4,5},{5,4},{6,7},{7,6},{8,9},{9,8},{10,11... | collective-permute-start | bytes 172040 | tf_op jit(solution)/shard_map/ppermute | solution.py:717
  4.4 2.1 %shard_map.83 = (f32[2336,128]{1,0:T(8,128)S(1)}, f32[72,128]{1,0:T(8,128)S(1)}) custom-call(f32[2,4]{1,0:T(2,128)} %refs_0_.3, f32[2,4]{1,0:T(2,128)} %refs_1_.2, f32[4,4]{1,0:T(4,128)} %refs_2_.1, f32[4,4]{1,0:T(4,128)} %refs_3_.1, f32[16,16]{1,0:T(8,128)} %refs_4_.1, f32[2336,128]{1,0:T(8,128)} %constant.16.clone.refs_5_, ...), custom_call_target="tpu_custom_call" | custom-call | tf_op jit(solution)/shard_map/pallas_call | solution.py:702
  6.5 0.1 pad_add_fusion.refs_0_
  6.6 0.0 collective-permute-done.refs_3_
  6.6 0.9 %shard_map.84 = (f32[2,144,128]{2,1,0:T(8,128)S(1)}, f32[264,128]{1,0:T(8,128)S(1)}, f32[144,128]{1,0:T(8,128)S(1)}, f32[232,128]{1,0:T(8,128)S(1)}) custom-call(s32[3]{0:T(128)S(1)} %pad_add_fusion.refs_0_, f32[2,128,128]{2,1,0:T(8,128)S(1)} %get-tuple-element.29.refs_1_, f32[112,128]{1,0:T(8,128)S(1)} %get-tuple-element.30.refs_6_.refs_2_, ...), custom_call_target="tpu_custom_call" | custom-call | tf_op jit(solution)/shard_map/pallas_call | solution.py:702
  7.5 2.1 %collective-permute-start.1 = (f32[264,128]{1,0:T(8,128)S(1)}, f32[264,128]{1,0:T(8,128)S(1)}, u32[]{:S(2)}, u32[]{:S(2)}) collective-permute-start(f32[264,128]{1,0:T(8,128)S(1)} %get-tuple-element.33.refs_1_.refs_2_), channel_id=1, source_target_pairs={{0,8},{8,0},{16,24},{24,16},{1,9},{9,1},{17,25},{25,17},{2,10},{10... | collective-permute-start | bytes 405512 | tf_op jit(solution)/shard_map/ppermute | solution.py:717
  9.6 0.0 collective-permute-start.4
  9.6 2.5 %collective-permute-start.2 = (f32[144,128]{1,0:T(8,128)S(1)}, f32[144,128]{1,0:T(8,128)S(1)}, u32[]{:S(2)}, u32[]{:S(2)}) collective-permute-start(f32[144,128]{1,0:T(8,128)S(1)} %get-tuple-element.34), channel_id=1, source_target_pairs={{0,24},{8,16},{16,8},{24,0},{1,25},{9,17},{17,9},{25,1},{2,26},{10... | collective-permute-start | bytes 221192 | tf_op jit(solution)/shard_map/ppermute | solution.py:717
  12.1 0.5 %collective-permute-done.1.refs_2_.refs_3_ = f32[264,128]{1,0:T(8,128)S(1)} collective-permute-done((f32[264,128]{1,0:T(8,128)S(1)}, f32[264,128]{1,0:T(8,128)S(1)}, u32[]{:S(2)}, u32[]{:S(2)}) %collective-permute-start.1) | collective-permute-done | bytes 135200 | tf_op jit(solution)/shard_map/ppermute | solution.py:717
  12.6 0.7 %shard_map.85.refs_3_.refs_2_ = f32[120,128]{1,0:T(8,128)S(1)} custom-call(s32[3]{0:T(128)S(1)} %pad_add_fusion.refs_0_, f32[264,128]{1,0:T(8,128)S(1)} %get-tuple-element.33.refs_1_.refs_2_, f32[264,128]{1,0:T(8,128)S(1)} %collective-permute-done.1.refs_2_.refs_3_), custom_call_target="tpu_custom_call" | custom-call | tf_op jit(solution)/shard_map/pallas_call | solution.py:702
  13.3 4.1 %collective-permute-start.3 = (f32[120,128]{1,0:T(8,128)S(1)}, f32[120,128]{1,0:T(8,128)S(1)}, u32[]{:S(2)}, u32[]{:S(2)}) collective-permute-start(f32[120,128]{1,0:T(8,128)S(1)} %shard_map.85.refs_3_.refs_2_), channel_id=1, source_target_pairs={{0,24},{8,16},{16,8},{24,0},{1,25},{9,17},{17,9},{25,1},{2,26},{10... | collective-permute-start | bytes 184328 | tf_op jit(solution)/shard_map/ppermute | solution.py:717
  17.4 2.0 %shard_map.86 = (bf16[448,1536]{1,0:T(8,128)(2,1)S(1)}, bf16[448,1536]{1,0:T(8,128)(2,1)S(1)}, bf16[4,88,128]{2,1,0:T(8,128)(2,1)S(1)}, bf16[4,88,128]{2,1,0:T(8...) custom-call(s32[3]{0:T(128)S(1)} %pad_add_fusion.refs_0_, f32[72,128]{1,0:T(8,128)S(1)} %get-tuple-element.35.refs_1_, ...), custom_call_target="tpu_custom_call" | custom-call | tf_op jit(solution)/shard_map/pallas_call | solution.py:702
  19.4 0.0 collective-permute-done.2.refs_4_
  19.4 0.0 collective-permute-done.4.refs_7_.refs_4_.refs_2_
  19.4 0.6 %collective-permute-done.3.refs_5_.refs_3_ = f32[120,128]{1,0:T(8,128)S(1)} collective-permute-done((f32[120,128]{1,0:T(8,128)S(1)}, f32[120,128]{1,0:T(8,128)S(1)}, u32[]{:S(2)}, u32[]{:S(2)}) %collective-permute-start.3) | collective-permute-done | bytes 61472 | tf_op jit(solution)/shard_map/ppermute | solution.py:717
  20.0 0.6 %shard_map.87 = (f32[2,288,128]{2,1,0:T(8,128)S(1)}, f32[352,128]{1,0:T(8,128)S(1)}) custom-call(s32[3]{0:T(128)S(1)} %pad_add_fusion.refs_0_, f32[2,144,128]{2,1,0:T(8,128)S(1)} %get-tuple-element.32.refs_1_, f32[120,128]{1,0:T(8,128)S(1)} %shard_map.85.refs_3_.refs_2_, f32[264,128]{1,0:T(8,128)S(1)} %collective-permute-done.1.refs_2_.refs_3_, ...), custom_call_target="tpu_custom_call" | custom-call | tf_op jit(solution)/shard_map/pallas_call | solution.py:702
  20.6 0.1 collective-permute-start.5
  20.7 1.8 %shard_map.88 = (bf16[4,256,1024]{2,1,0:T(8,128)(2,1)S(1)}, bf16[4,256,1024]{2,1,0:T(8,128)(2,1)S(1)}, bf16[4,144,128]{2,1,0:T(8,128)(2,1)S(1)}, bf16[4,144,128]{2,1,0:T(8,128)(2,1)S(1)}) custom-call(s32[3]{0:T(128)S(1)} %pad_add_fusion.refs_0_, f32[72,128]{1,0:T(8,128)S(1)} %get-tuple-element.35.refs_1_, ...), custom_call_target="tpu_custom_call" | custom-call | tf_op jit(solution)/shard_map/pallas_call | solution.py:702
  22.5 1.3 %shard_map.89 = (f32[4,256,144]{2,1,0:T(8,128)S(1)}, f32[448,88]{1,0:T(8,128)S(1)}) custom-call(f32[2,288,128]{2,1,0:T(8,128)S(1)} %get-tuple-element.38.refs_0_.refs_1_, f32[264,128]{1,0:T(8,128)S(1)} %get-tuple-element.33.refs_1_.refs_2_, f32[264,128]{1,0:T(8,128)S(1)} %collective-permute-done.1.refs_2_.refs_3_, ...), custom_call_target="tpu_custom_call" | custom-call | tf_op jit(solution)/shard_map/pallas_call | solution.py:702
  23.8 3.7 %collective-permute-done.5.refs_5_.refs_3_ = f32[352,128]{1,0:T(8,128)S(1)} collective-permute-done((f32[352,128]{1,0:T(8,128)S(1)}, f32[352,128]{1,0:T(8,128)S(1)}, u32[]{:S(2)}, u32[]{:S(2)}) %collective-permute-start.5) | collective-permute-done | bytes 180256 | tf_op jit(solution)/shard_map/ppermute | solution.py:717
  27.4 0.6 %shard_map.90.refs_8_.refs_2_ = f32[848,128]{1,0:T(8,128)S(1)} custom-call(s32[3]{0:T(128)S(1)} %pad_add_fusion.refs_0_, f32[2,288,128]{2,1,0:T(8,128)S(1)} %get-tuple-element.38.refs_0_.refs_1_, f32[264,128]{1,0:T(8,128)S(1)} %get-tuple-element.33.refs_1_.refs_2_, f32[352,128]{1,0:T(8,128)S(1)} %get-tuple-element.39.refs_3_.refs_8_, ...), custom_call_target="tpu_custom_call" | custom-call | tf_op jit(solution)/shard_map/pallas_call | solution.py:702
  28.1 0.0 collective-permute-start.6
  28.1 0.9 %shard_map.91 = (f32[4,256,144]{2,1,0:T(8,128)S(1)}, f32[448,88]{1,0:T(8,128)S(1)}) custom-call(f32[4,256,144]{2,1,0:T(8,128)S(1)} %get-tuple-element.44.refs_0_, f32[448,88]{1,0:T(8,128)S(1)} %get-tuple-element.45.refs_6_.refs_1_, f32[232,128]{1,0:T(8,128)S(1)} %collective-permute-done.4.refs_7_.refs_4_.refs_2_, ...), custom_call_target="tpu_custom_call" | custom-call | tf_op jit(solution)/shard_map/pallas_call | solution.py:702
  29.0 0.9 %collective-permute-done.6.refs_3_ = f32[848,128]{1,0:T(8,128)S(1)} collective-permute-done((f32[848,128]{1,0:T(8,128)S(1)}, f32[848,128]{1,0:T(8,128)S(1)}, u32[]{:S(2)}, u32[]{:S(2)}) %collective-permute-start.6) | collective-permute-done | bytes 434208 | tf_op jit(solution)/shard_map/ppermute | solution.py:717
  29.9 2.9 %shard_map.92 = f32[16,16,128]{2,1,0:T(8,128)} custom-call(f32[4,256,144]{2,1,0:T(8,128)S(1)} %get-tuple-element.46.refs_0_, f32[448,88]{1,0:T(8,128)S(1)} %get-tuple-element.47.refs_1_, f32[848,128]{1,0:T(8,128)S(1)} %shard_map.90.refs_8_.refs_2_, f32[848,128]{1,0:T(8,128)S(1)} %collective-permute-done.6.refs_3_, ...), custom_call_target="tpu_custom_call" | custom-call | tf_op jit(solution)/shard_map/pallas_call | solution.py:702
Async XLA Ops:
  1.4 5.2 %collective-permute-start = (f32[112,128]{1,0:T(8,128)S(1)}, f32[112,128]{1,0:T(8,128)S(1)}, u32[]{:S(2)}, u32[]{:S(2)}) collective-permute-start(f32[112,128]{1,0:T(8,128)S(1)} %get-tuple-element.30.refs_6_.refs_2_), channel_id=1, source_target_pairs={{0,1},{1,0},{2,3},{3,2},{4,5},{5,4},{6,7},{7,6},{8,9},{9,8},{10,11... | collective-permute-start | bytes 172040 | tf_op jit(solution)/shard_map/ppermute | solution.py:717
  7.5 5.1 %collective-permute-start.1 = (f32[264,128]{1,0:T(8,128)S(1)}, f32[264,128]{1,0:T(8,128)S(1)}, u32[]{:S(2)}, u32[]{:S(2)}) collective-permute-start(f32[264,128]{1,0:T(8,128)S(1)} %get-tuple-element.33.refs_1_.refs_2_), channel_id=1, source_target_pairs={{0,8},{8,0},{16,24},{24,16},{1,9},{9,1},{17,25},{25,17},{2,10},{10... | collective-permute-start | bytes 405512 | tf_op jit(solution)/shard_map/ppermute | solution.py:717
  9.6 9.7 %collective-permute-start.4 = (f32[232,128]{1,0:T(8,128)S(1)}, f32[232,128]{1,0:T(8,128)S(1)}, u32[]{:S(2)}, u32[]{:S(2)}) collective-permute-start(f32[232,128]{1,0:T(8,128)S(1)} %get-tuple-element.37), channel_id=1, source_target_pairs={{0,6},{2,4},{4,2},{6,0},{1,7},{3,5},{5,3},{7,1},{8,14},{10,12},{12... | collective-permute-start | bytes 356360 | tf_op jit(solution)/shard_map/ppermute | solution.py:717
  9.6 9.7 %collective-permute-start.2 = (f32[144,128]{1,0:T(8,128)S(1)}, f32[144,128]{1,0:T(8,128)S(1)}, u32[]{:S(2)}, u32[]{:S(2)}) collective-permute-start(f32[144,128]{1,0:T(8,128)S(1)} %get-tuple-element.34), channel_id=1, source_target_pairs={{0,24},{8,16},{16,8},{24,0},{1,25},{9,17},{17,9},{25,1},{2,26},{10... | collective-permute-start | bytes 221192 | tf_op jit(solution)/shard_map/ppermute | solution.py:717
  13.3 6.7 %collective-permute-start.3 = (f32[120,128]{1,0:T(8,128)S(1)}, f32[120,128]{1,0:T(8,128)S(1)}, u32[]{:S(2)}, u32[]{:S(2)}) collective-permute-start(f32[120,128]{1,0:T(8,128)S(1)} %shard_map.85.refs_3_.refs_2_), channel_id=1, source_target_pairs={{0,24},{8,16},{16,8},{24,0},{1,25},{9,17},{17,9},{25,1},{2,26},{10... | collective-permute-start | bytes 184328 | tf_op jit(solution)/shard_map/ppermute | solution.py:717
  20.6 6.8 %collective-permute-start.5 = (f32[352,128]{1,0:T(8,128)S(1)}, f32[352,128]{1,0:T(8,128)S(1)}, u32[]{:S(2)}, u32[]{:S(2)}) collective-permute-start(f32[352,128]{1,0:T(8,128)S(1)} %get-tuple-element.39.refs_3_.refs_8_), channel_id=1, source_target_pairs={{0,6},{2,4},{4,2},{6,0},{1,7},{3,5},{5,3},{7,1},{8,14},{10,12},{12... | collective-permute-start | bytes 540680 | tf_op jit(solution)/shard_map/ppermute | solution.py:717
  28.1 1.8 %collective-permute-start.6 = (f32[848,128]{1,0:T(8,128)S(1)}, f32[848,128]{1,0:T(8,128)S(1)}, u32[]{:S(2)}, u32[]{:S(2)}) collective-permute-start(f32[848,128]{1,0:T(8,128)S(1)} %shard_map.90.refs_8_.refs_2_), channel_id=1, source_target_pairs={{0,2},{2,0},{4,6},{6,4},{1,3},{3,1},{5,7},{7,5},{8,10},{10,8},{12,... | collective-permute-start | bytes 1302536 | tf_op jit(solution)/shard_map/ppermute | solution.py:717

commit v4 on v3

--- a/solution.py
+++ b/solution.py
@@ -7,6 +7,7 @@
 from jax.experimental import pallas as pl
 from jax.experimental.pallas import tpu as pltpu
 from jax.sharding import PartitionSpec as P
+
 
 REACH = 8
 
@@ -204,7 +205,6 @@
         self.window = bz // 2 + 2 * GAUSSIAN_RIM
         self.window_rows = up8(self.window)
         self.out_z = bz // 2 + 2
-        self.out_rows = up8(self.out_z)
         self.top_rows = 2 * up8(bz // 16 + 2)
         self.top_z = bz // 16 + 2
         self.top_x, self.top_y = bx // 16 + 2, by // 16 + 2
@@ -253,9 +253,10 @@
             "back": self.back_left,
             "back_right": self.back_right,
             "spread_x": spread_x.reshape(-1, 16),
-            "pick_x": pick_x.transpose(0, 2, 1, 3).reshape(-1, LANES),
+            "pick_x": pick_x[:, :, 0].reshape(-1, LANES),
             "spread_y": spread_y.reshape(-1, 16),
-            "pick_y": pick_y.transpose(0, 2, 1, 3).reshape(-1, LANES),
+            "pick_y": pick_y[:, :, 0].reshape(-1, LANES),
+            "pick_pair": pick_y[:, :, 1].reshape(-1, LANES),
             "spread_z": spread_z.reshape(-1, 16),
             "pick_z": pick_z.reshape(-1, self.top_rows),
             "lift_x": lift_x,
@@ -271,7 +272,7 @@
         return np.concatenate(pieces)
 
     def fine_tables(self):
-        bx, by, bz = self.brick
+        bx, _, bz = self.brick
         x_of, y_of = self.own_cells()
         strip, x_far = np.arange(LANES) // (LANES // 2), x_of % (LANES // 2 // self.half)
         right, left = bx + x_far, x_far - REACH
@@ -282,7 +283,7 @@
         return padded(cells, 8, LANES), squared.astype(np.float32)
 
     def coarse_tables(self):
-        bx, by, bz = (size // 2 for size in self.brick)
+        bx, _, _ = (size // 2 for size in self.brick)
         lane = np.arange(LANES)
         cell, count = lane // self.cy, self.cx * self.cy
         own = cell - 1
@@ -315,7 +316,7 @@
                 index = (place * size - 1 + np.arange(outs)) % (8 * count)
                 spread.append(padded(whole[index], 16 if axis < 2 else LANES, 16))
                 if axis == 0:
-                    cells = (place ^ (group % 2) ^ (3 * ((group // 2) % 2))) * four[0] + cell // self.top_y - 1
+                    cells = (place ^ (group % 4)) * four[0] + cell // self.top_y - 1
                     valid = used
                 elif axis == 1:
                     cells = (place ^ partner ^ (3 * (group // 4))) * four[1] + cell % self.top_y - 1
@@ -378,6 +379,10 @@
     return dot(left[0], right[0]) + dot(left[1], right[0]) + dot(left[0], right[1])
 
 
+def pick(flags_ref, axis, even, odd):
+    return jnp.where(jnp.broadcast_to(flags_ref[axis : axis + 1], even.shape) < 0.5, even, odd)
+
+
 def exact_tables(plan, ref):
     def read(name, rows, at=0):
         start = plan.starts[name] + at * rows
@@ -399,7 +404,7 @@
 
 
 def start_kernel(plan, charges_ref, table_ref, own_ref, out_ref):
-    bx, by, bz = plan.brick
+    _, _, bz = plan.brick
     rim, half = plan.rim, plan.half
     top, size = None, plan.top_rows // 2
     left = split(table_ref[:size])
@@ -414,33 +419,17 @@
     out_ref[4 * rim :] = top
 
 
-def setup_kernel(plan, terms, exponents_ref, amplitudes_ref, tops_x_ref, tops_y_ref, tops_z_ref, table_ref, kept_ref,
-                 params_ref, semaphore):
-    copy = pltpu.make_async_copy(table_ref, kept_ref, semaphore)
-    copy.start()
-    offsets = lax.broadcasted_iota(jnp.int32, (1, LANES), 1).astype(F32) - REACH
-    squared = jnp.where(offsets <= REACH, offsets * offsets, FAR)
-    for level in range(2):
-        for term in range(terms):
-            exponent = exponents_ref[level, term]
-            scale = 1.0 / jnp.sum(jnp.exp(squared * -exponent), axis=1, keepdims=True)
-            scale = jnp.broadcast_to(scale, (1, LANES))
-            row = 3 * terms * level + term
-            params_ref[row : row + 1] = jnp.zeros((1, LANES), F32) + exponent
-            row = row + terms
-            params_ref[row : row + 1] = scale * scale * amplitudes_ref[level, term]
-            row = row + terms
-            params_ref[row : row + 1] = scale
-    params_ref[6 * terms :] = jnp.zeros((3 * 16, LANES), F32)
-    for axis, source in enumerate((tops_x_ref, tops_y_ref, tops_z_ref)):
-        at, count = 6 * terms + 16 * axis, source.shape[0]
-        params_ref[at : at + count, :count] = source[...]
-    copy.wait()
-
-
-def spread_kernel(plan, place_ref, own_ref, sent_ref, got_ref, table_ref, fine_ref, out_ref, side_x_ref,
+def setup_kernel(count, *refs):
+    copies = [pltpu.make_async_copy(refs[at], refs[count + at], refs[2 * count].at[at]) for at in range(count)]
+    for copy in copies:
+        copy.start()
+    for copy in copies:
+        copy.wait()
+
+
+def spread_kernel(plan, flags_ref, own_ref, sent_ref, got_ref, table_ref, fine_ref, out_ref, side_x_ref,
                   side_y_ref):
-    bx, by, bz = plan.brick
+    _, _, bz = plan.brick
     rim, rows = plan.rim, plan.fine_rows
     table = exact_tables(plan, table_ref)
     coarse = None
@@ -455,10 +444,9 @@
         summed = dot_right(summed, table("rest_right", LANES, part))
         coarse = summed if coarse is None else coarse + summed
     low, high = halves(fine_ref[0], fine_ref[1])
-    even = place_ref[0] % 2 == 0
-    out_ref[:rows] = jnp.where(even, high, low)
-    side_x_ref[...] = jnp.where(even, low, high)
-    side_y_ref[:rows] = jnp.where(place_ref[1] % 2 == 0, fine_ref[0], fine_ref[1])
+    out_ref[:rows] = pick(flags_ref, 0, high, low)
+    side_x_ref[...] = pick(flags_ref, 0, low, high)
+    side_y_ref[:rows] = pick(flags_ref, 1, fine_ref[0], fine_ref[1])
     side_y_ref[rows:] = coarse
     out_ref[rows : rows + plan.window_rows] = coarse
     top = rows + plan.window_rows
@@ -466,45 +454,40 @@
     out_ref[top + plan.top_rows // 2 :] = got_ref[4 * rim :]
 
 
-def pass_kernel(plan, place_ref, sent_ref, got_ref, out_ref):
+def half_of(plan, flags_ref, strip_ref):
     rows = plan.fine_rows
-    even = place_ref[0] % 2 == 0
+    low, high = halves(strip_ref[: rows // 2], strip_ref[rows // 2 : rows])
+    return pick(flags_ref, 1, low, high)
+
+
+def pass_kernel(plan, flags_ref, sent_ref, got_ref, out_ref, side_ref):
+    rows = plan.fine_rows
     own = sent_ref[rows : rows + plan.window_rows]
     far = got_ref[rows : rows + plan.window_rows]
     lane = lanes_of(plan.window_rows)
-    edge, all_lanes = 2 * plan.cy, plan.cx * plan.cy
-    last = all_lanes - edge
-    right = own + jnp.where((lane >= last) & (lane < all_lanes), pltpu.roll(far, last, 1), 0.0)
-    right = right + jnp.where((lane >= all_lanes) & (lane < all_lanes + edge), pltpu.roll(far, edge, 1), 0.0)
-    left = own + jnp.where(lane < edge, pltpu.roll(far, LANES - last, 1), 0.0)
-    left = left + jnp.where((lane >= all_lanes) & (lane < all_lanes + edge), pltpu.roll(far, all_lanes, 1), 0.0)
-    out_ref[: plan.window_rows] = jnp.where(even, right, left)
+    edge, count = 2 * plan.cy, plan.cx * plan.cy
+    last = count - edge
+    beyond = (lane >= count) & (lane < count + edge)
+    left = far + jnp.where(lane < edge, pltpu.roll(own, LANES - last, 1), 0.0)
+    left = left + jnp.where(beyond, pltpu.roll(own, count, 1), 0.0)
+    right = far + jnp.where((lane >= last) & (lane < count), pltpu.roll(own, last, 1), 0.0)
+    right = right + jnp.where(beyond, pltpu.roll(own, edge, 1), 0.0)
+    out_ref[: plan.window_rows] = pick(flags_ref, 0, left, right)
     top = rows + plan.window_rows
     out_ref[plan.window_rows :] = sent_ref[top:] + pltpu.roll(got_ref[top:], plan.group, 1)
-
-
-def stack_kernel(plan, place_ref, fine_ref, sent_ref, first_ref, side_ref, second_ref, cells_ref, out_ref):
+    side_ref[: rows // 2] = half_of(plan, flags_ref, got_ref)
+    side_ref[rows // 2 :] = far
+
+
+def stack_kernel(plan, flags_ref, fine_ref, sent_ref, first_ref, side_ref, second_ref, cells_ref, out_ref):
     rows, window = plan.fine_rows, plan.window_rows
     low, high = halves(first_ref[:rows], side_ref[...])
     for part, other in ((0, low), (1, high)):
         cells_ref[part, :rows] = fine_ref[part]
         cells_ref[part, rows:] = other
-    out_ref[:rows] = jnp.where(place_ref[1] % 2 == 0, low, high)
-    out_ref[rows : rows + window] = first_ref[rows : rows + window]
-    out_ref[rows + window : rows + 2 * window] = second_ref[:window]
-    out_ref[rows + 2 * window :] = sent_ref[window:] + pltpu.roll(second_ref[window:], 2 * plan.group, 1)
-
-
-def share_kernel(plan, place_ref, cells_ref, own_ref, sent_ref, side_ref, got_ref, out_ref):
-    rows, window = plan.fine_rows, plan.window_rows
-    even = place_ref[1] % 2 == 0
-    out_ref[: 2 * rows] = jnp.where(even, cells_ref[1], cells_ref[0])
-    at = 2 * rows
-    for source, start, count in ((own_ref, rows, 1), (sent_ref, rows, 2), (side_ref, rows, 1), (got_ref, rows, 2)):
-        out_ref[at : at + count * window] = source[start : start + count * window]
-        at = at + count * window
-    start = rows + 2 * window
-    out_ref[at:] = sent_ref[start:] + pltpu.roll(got_ref[start:], 4 * plan.group, 1)
+    out_ref[: rows // 2] = half_of(plan, flags_ref, side_ref)
+    out_ref[rows // 2 : rows // 2 + window] = second_ref[:window]
+    out_ref[rows // 2 + window :] = sent_ref[window:] + pltpu.roll(second_ref[window:], 2 * plan.group, 1)
 
 
 def dot_turned(left, right):
@@ -514,18 +497,17 @@
     return product(left[0], right[0]) + product(left[1], right[0]) + product(left[0], right[1])
 
 
-def fine_weights_kernel(plan, terms, place_ref, params_ref, table_ref, kf_ref, kf_low_ref, zf_ref, zf_low_ref):
-    bx, by, bz = plan.brick
+def fine_weights_kernel(plan, terms, flags_ref, params_ref, table_ref, kf_ref, kf_low_ref, zf_ref, zf_low_ref):
+    bx, by, _ = plan.brick
     cells_ref = table_ref.at[pl.ds(plan.starts["fine_cells"], 8)]
     dz_ref = table_ref.at[pl.ds(plan.starts["fine_dz"], plan.fine_rows)]
     half = plan.half
-    even_x, even_y = place_ref[0] % 2 == 0, place_ref[1] % 2 == 0
     own_x, own_y = cells_ref[0:1], cells_ref[1:2]
-    far_x = jnp.where(even_x, cells_ref[2:3], cells_ref[3:4])
+    far_x = pick(flags_ref, 0, cells_ref[2:3], cells_ref[3:4])
     x_out = lax.broadcasted_iota(jnp.int32, (bx, LANES), 0).astype(F32)
     y_out = lax.broadcasted_iota(jnp.int32, (half, LANES), 0).astype(F32)
-    y_low, y_high = F32(-half), F32(by)
-    y_far = jnp.where(even_y, y_low, y_high), jnp.where(even_y, y_high, y_low)
+    y_far = jnp.full((1, LANES), -half, F32)
+    y_far = pick(flags_ref, 1, y_far, y_far + half + by)
 
     def decay(exponent, distance):
         return jnp.where(jnp.abs(distance) <= REACH, jnp.exp(-exponent * distance * distance), 0.0)
@@ -535,7 +517,7 @@
         scale = params_ref[terms + term : terms + term + 1]
         along_x = [decay(exponent, x_in - x_out)[:, None, :] for x_in in (own_x, far_x)]
         for group in range(4):
-            y_in = own_y + (F32(group * half) if group < 2 else y_far[group - 2])
+            y_in = own_y + (F32(group * half) if group < 2 else y_far)
             for part in range(2):
                 along_y = decay(exponent, y_in - (y_out + part * half)) * scale
                 for block in range(2):
@@ -548,8 +530,27 @@
         )
 
 
-def coarse_weights_kernel(plan, terms, place_ref, params_ref, table_ref, k1_ref, k1_low_ref, z1_ref, z1_low_ref,
-                          zc_ref, kc_ref):
+def set_params(terms, exponents_ref, amplitudes_ref, tops, params_ref):
+    offsets = lax.broadcasted_iota(jnp.int32, (1, LANES), 1).astype(F32) - REACH
+    squared = jnp.where(offsets <= REACH, offsets * offsets, FAR)
+    for level in range(2):
+        for term in range(terms):
+            at = slice(level, level + 1), slice(term, term + 1)
+            exponent = exponents_ref[at]
+            scale = 1.0 / jnp.sum(jnp.exp(-exponent * squared), axis=1, keepdims=True)
+            row = 3 * terms * level + term
+            for value in (exponent, scale * scale * amplitudes_ref[at], scale):
+                params_ref[row : row + 1] = jnp.broadcast_to(value, (1, LANES))
+                row = row + terms
+    params_ref[6 * terms :] = jnp.zeros((3 * 16, LANES), F32)
+    for axis, source in enumerate(tops):
+        at, count = 6 * terms + 16 * axis, source.shape[0]
+        params_ref[at : at + count, :count] = source[...]
+
+
+def coarse_weights_kernel(plan, terms, place_ref, table_ref, exponents_ref, amplitudes_ref, top_x_ref, top_y_ref,
+                          top_z_ref, params_ref, k1_ref, k1_low_ref, z1_ref, z1_low_ref, zc_ref, kc_ref):
+    set_params(terms, exponents_ref, amplitudes_ref, (top_x_ref, top_y_ref, top_z_ref), params_ref)
     cells_ref = table_ref.at[pl.ds(plan.starts["coarse_cells"], 16)]
     at, count = plan.starts["out_cells"], plan.out_cells
     out_cells_ref = [table_ref[at + count * part : at + count * (part + 1)] for part in range(3)]
@@ -570,7 +571,7 @@
         used = cells_ref[7:8] if slot < 2 else cells_ref[8:9]
         squares_x.append(squared(x_in - x_out, bx * plan.counts[0]) + used)
     toward = jnp.where(even_y, F32(by), F32(-by))
-    for group, offset in enumerate((F32(0), -toward, toward, F32(2 * by))):
+    for group, offset in enumerate((F32(0), -toward, -toward, F32(2 * by))):
         square_y = squared(cells_ref[6:7] + offset - y_out, by * plan.counts[1]) + out_cells_ref[2]
         for slot in range(3):
             total = squares_x[slot] + square_y
@@ -599,89 +600,118 @@
         return table_ref[pl.ds(pl.multiple_of(plan.starts[name] + at * rows, 8), rows)]
 
     size = 16
-    along = []
-    for axis, (spread, pick) in enumerate((("spread_x", "pick_x"), ("spread_y", "pick_y"))):
+
+    def along(axis, spread, pick, place):
         top = params_ref[6 * terms + size * axis : 6 * terms + size * (axis + 1)]
-        picked = read(pick, 2 * size, place_ref[axis])
-        picked = jnp.concatenate([picked[:size], picked[size:]], axis=1)
-        value = chain(read(spread, size, place_ref[axis])[:, :size], top)[:, :size]
-        along.append(chain(value, picked))
+        value = chain(read(spread, size, place)[:, :size], top)[:, :size]
+        return chain(value, read(pick, size, place))
+
+    along_x = along(0, "spread_x", "pick_x", place_ref[0])
+    lift_x, lift_y = (read(name, plan.out_cells)[:, :size] for name in ("lift_x", "lift_y"))
+    along_x = chain(lift_x, along_x)
+    right = []
+    for partner in range(2):
+        place = place_ref[1] + partner * (1 - 2 * (place_ref[1] % 2))
+        along_y = along(1, "spread_y", ("pick_y", "pick_pair")[partner], place)
+        right.append(along_x * chain(lift_y, along_y))
     top = params_ref[6 * terms + 2 * size : 6 * terms + 3 * size]
     value = chain(read("spread_z", LANES, place_ref[2])[:, :size], top)[:, :size]
     left = chain(value, read("pick_z", size, place_ref[2])[:, : plan.top_rows])
-    lift_x, lift_y = (read(name, plan.out_cells)[:, :size] for name in ("lift_x", "lift_y"))
-    return left, chain(lift_x, along[0]) * chain(lift_y, along[1])
-
-
-def side_by_side(source, start, rows, count):
-    return jnp.concatenate([source[start + rows * at : start + rows * (at + 1)] for at in range(count)], axis=1)
-
-
-def gather_part(plan, terms, blocks, near, kf_refs, k1_refs, fine_at, coarse_at, before):
-    cells, near = split(blocks), split(near)
-    fine_cols = pl.ds(fine_at * LANES, blocks.shape[1])
-    fine = []
+    return left, jnp.concatenate(right, axis=1)
+
+
+def sum_fine(terms, blocks, refs, at):
+    cells, cols = split(blocks), pl.ds(at * LANES, blocks.shape[1])
+    return [dot_turned((refs[0][term, :, cols], refs[1][term, :, cols]), cells) for term in range(terms)]
+
+
+def sum_coarse(blocks, refs, at):
+    cols = pl.ds(at * LANES, blocks.shape[1])
+    return dot_turned((refs[0][:, cols], refs[1][:, cols]), split(blocks))
+
+
+def fine_potential(fine, refs):
+    total = None
+    for term, value in enumerate(fine):
+        value = dot_split(split(value), (refs[0][term], refs[1][term]))
+        total = value if total is None else total + value
+    return total
+
+
+def coarse_potential(plan, terms, coarse, refs, top, kernel, table_ref):
+    level_one = dot_turned(split(kernel), split(top))
     for term in range(terms):
-        value = dot_turned((kf_refs[0][term, :, fine_cols], kf_refs[1][term, :, fine_cols]), cells)
-        fine.append(value if before is None else before[0][term] + value)
-    cols = pl.ds(coarse_at * LANES, near[0].shape[1])
-    coarse = dot_turned((k1_refs[0][:, cols], k1_refs[1][:, cols]), near)
-    return fine, coarse if before is None else before[1][...] + coarse
-
-
-def near_kernel(plan, terms, cells_ref, own_ref, first_ref, second_ref, kf_ref, kf_low_ref, k1_ref, k1_low_ref, fine_ref, coarse_ref):
+        piece = split(coarse[term * plan.out_cells : (term + 1) * plan.out_cells])
+        level_one = level_one + dot_split(piece, (refs[0][term], refs[1][term]))
+    table = exact_tables(plan, table_ref)
+    back = dot_right(level_one, table("back", LANES))
+    return dot_left(table("back_right", 2 * LANES)[:, : plan.out_cells], back)
+
+
+def near_kernel(plan, terms, flags_ref, cells_ref, own_ref, first_ref, second_ref, kf_ref, kf_low_ref, k1_ref,
+                k1_low_ref, zf_ref, zf_low_ref, fine_ref, coarse_ref, give_fine_ref, give_coarse_ref):
     rows, window = plan.fine_rows, plan.window_rows
-    blocks = [cells_ref[part, at : at + rows] for part in range(2) for at in (0, rows)]
+    kf, k1 = (kf_ref, kf_low_ref), (k1_ref, k1_low_ref)
+    groups = [jnp.concatenate([cells_ref[part, :rows], cells_ref[part, rows:]], axis=1) for part in range(2)]
     near = [own_ref[rows : rows + window], first_ref[rows : rows + window], second_ref[:window]]
     near = jnp.concatenate(near, axis=1)
-    fine, coarse = gather_part(plan, terms, jnp.concatenate(blocks, axis=1), near, (kf_ref, kf_low_ref),
-                               (k1_ref, k1_low_ref), 0, 0, None)
-    for term in range(terms):
-        fine_ref[term] = fine[term]
-    coarse_ref[...] = coarse
-
-
-def middle_kernel(plan, terms, fine_in_ref, coarse_in_ref, side_ref, got_ref, kf_ref, kf_low_ref, k1_ref, k1_low_ref,
-                  fine_ref, coarse_ref):
-    rows, window = plan.fine_rows, plan.window_rows
-    blocks = jnp.concatenate([side_ref[:rows], got_ref[:rows]], axis=1)
-    near = jnp.concatenate([side_ref[rows:], side_by_side(got_ref, rows, window, 2)], axis=1)
-    fine, coarse = gather_part(plan, terms, blocks, near, (kf_ref, kf_low_ref), (k1_ref, k1_low_ref), 4, 3,
-                               (fine_in_ref, coarse_in_ref))
-    for term in range(terms):
-        fine_ref[term] = fine[term]
-    coarse_ref[...] = coarse
-
-
-def far_kernel(plan, terms, fine_in_ref, coarse_in_ref, sent_ref, got_ref, kf_ref, kf_low_ref, k1_ref, k1_low_ref,
-               zf_ref, zf_low_ref, z1_ref, z1_low_ref, zc_ref, kc_ref, table_ref, out_ref):
-    rows, window, half = plan.fine_rows, plan.window_rows, plan.half
-    blocks, near = side_by_side(got_ref, 0, rows, 2), side_by_side(got_ref, 2 * rows, window, 6)
-    fine, coarse = gather_part(plan, terms, blocks, near, (kf_ref, kf_low_ref), (k1_ref, k1_low_ref), 6, 6,
-                               (fine_in_ref, coarse_in_ref))
-    at = 2 * rows + 6 * window
-    top = jnp.concatenate([sent_ref[at : at + plan.top_rows], got_ref[at : at + plan.top_rows]], axis=1)
-    top = dot_split(split(zc_ref[...]), split(top))
-    level_one = dot_turned(split(kc_ref[...]), split(top))
-    total = None
-    for term in range(terms):
-        piece = split(coarse[term * plan.out_cells : (term + 1) * plan.out_cells])
-        level_one = level_one + dot_split(piece, (z1_ref[term], z1_low_ref[term]))
-        value = dot_split(split(fine[term]), (zf_ref[term], zf_low_ref[term]))
-        total = value if total is None else total + value
-    table = exact_tables(plan, table_ref)
-    back = dot_right(level_one, table("back", LANES))
-    total = total + dot_left(table("back_right", 2 * LANES)[:, : plan.out_cells], back)
+    other = [pick(flags_ref, 1, cells_ref[1, at : at + rows], cells_ref[0, at : at + rows]) for at in (0, rows)]
+    other = jnp.concatenate(other, axis=1)
+    give_fine_ref[...] = fine_potential(sum_fine(terms, other, kf, 6), (zf_ref, zf_low_ref))
+    give_coarse_ref[...] = sum_coarse(near, k1, 6)
+    for term, value in enumerate(sum_fine(terms, jnp.concatenate(groups, axis=1), kf, 0)):
+        fine_ref[term] = value
+    coarse_ref[...] = sum_coarse(near, k1, 0)
+
+
+def top_charges(plan, sent_ref, got_ref, zc_ref):
+    start = plan.fine_rows // 2 + plan.window_rows
+    top = sent_ref[start:] + pltpu.roll(got_ref[start:], 4 * plan.group, 1)
+    return dot_split(split(zc_ref[...]), split(top))
+
+
+def arrived(plan, side_ref, strip_ref, got_ref):
+    rows = plan.fine_rows
+    pieces = [side_ref[rows:], strip_ref[rows // 2 :], got_ref[rows // 2 : rows // 2 + plan.window_rows]]
+    return jnp.concatenate(pieces, axis=1)
+
+
+def give_kernel(plan, terms, fine_ref, coarse_ref, side_ref, strip_ref, sent_ref, got_ref, k1_ref, k1_low_ref,
+                z1_ref, z1_low_ref, zc_ref, kc_ref, table_ref, out_ref):
+    coarse = coarse_ref[...] + sum_coarse(arrived(plan, side_ref, strip_ref, got_ref), (k1_ref, k1_low_ref), 9)
+    top = top_charges(plan, sent_ref, got_ref, zc_ref)
+    out_ref[...] = fine_ref[...] + coarse_potential(
+        plan, terms, coarse, (z1_ref, z1_low_ref), top, kc_ref[:, LANES:], table_ref
+    )
+
+
+def keep_kernel(plan, terms, fine_ref, coarse_ref, side_ref, strip_ref, sent_ref, got_ref, kf_ref, kf_low_ref,
+                k1_ref, k1_low_ref, zf_ref, zf_low_ref, z1_ref, z1_low_ref, zc_ref, kc_ref, table_ref, out_ref):
+    rows = plan.fine_rows
+    strips = jnp.concatenate(halves(strip_ref[: rows // 2], got_ref[: rows // 2]), axis=0)
+    blocks = jnp.concatenate([side_ref[:rows], strips], axis=1)
+    fine = sum_fine(terms, blocks, (kf_ref, kf_low_ref), 4)
+    fine = [fine_ref[term] + value for term, value in enumerate(fine)]
+    coarse = coarse_ref[...] + sum_coarse(arrived(plan, side_ref, strip_ref, got_ref), (k1_ref, k1_low_ref), 3)
+    top = top_charges(plan, sent_ref, got_ref, zc_ref)
+    out_ref[...] = fine_potential(fine, (zf_ref, zf_low_ref)) + coarse_potential(
+        plan, terms, coarse, (z1_ref, z1_low_ref), top, kc_ref[:, :LANES], table_ref
+    )
+
+
+def add_kernel(plan, own_ref, got_ref, out_ref):
+    half = plan.half
     for part in range(2):
-        cells = total[part * LANES : (part + 1) * LANES]
+        rows = pl.ds(part * LANES, LANES)
+        cells = own_ref[rows] + got_ref[rows]
         out_ref[:, part * half : (part + 1) * half, :] = cells.reshape(plan.brick[0], half, plan.brick[2])
 
 
-def call(body, shapes, *operands, scalars=0, after=(), last=False, plain=False, scratch=()):
+def call(body, shapes, *operands, scalars=0, after=(), last=False, plain=False, copies=0):
     specs = [pl.BlockSpec(memory_space=pltpu.SMEM)] * scalars
     specs += [pl.BlockSpec(memory_space=pltpu.VMEM)] * (len(operands) - scalars)
-    if scratch:
-        specs[-1] = pl.BlockSpec(memory_space=pl.ANY)
+    if copies:
+        specs = [pl.BlockSpec(memory_space=pl.ANY)] * len(operands)
     specs += [pl.BlockSpec(memory_space=pl.ANY)] * len(after)
 
     def keep(operand, space=pltpu.VMEM):
@@ -707,9 +737,9 @@
         ],
         in_specs=specs,
         out_specs=[pl.BlockSpec(memory_space=pltpu.VMEM)] * len(shapes),
-        scratch_shapes=scratch,
+        scratch_shapes=[pltpu.SemaphoreType.DMA((copies,))] if copies else (),
         compiler_params=pltpu.CompilerParams(vmem_limit_bytes=8 << 20),
-    )(*operands[:scalars], *kept)
+    )(*(operands[:scalars] if plain else [keep(operand, pltpu.SMEM) for operand in operands[:scalars]]), *kept)
 
 
 def pair(value, axis, bits):
@@ -719,6 +749,7 @@
 
 def local_short(plan, charges, exponents, amplitudes, top_x, top_y, top_z):
     where = jnp.stack([lax.axis_index(axis) for axis in ("gx", "gy", "gz")]).astype(jnp.int32)
+    flags = jnp.broadcast_to((where % 2).astype(F32)[:, None], (3, LANES))
     terms = exponents.shape[1]
     bx, by, bz = plan.brick
     rows, window = plan.fine_rows, plan.window_rows
@@ -732,42 +763,41 @@
         plain=True,
     )
     got_z = pair(sent_z, "gz", 1)
-    table = plan.constants((top_x, top_y, top_z))
-    table, params = call(
-        bind(setup_kernel, plan, terms),
-        [table.shape, (6 * terms + 3 * 16, LANES)],
-        exponents,
-        amplitudes,
-        top_x,
-        top_y,
-        top_z,
-        jnp.asarray(table),
-        scalars=2,
+    held = (jnp.asarray(plan.constants((top_x, top_y, top_z))), exponents, amplitudes, top_x, top_y, top_z)
+    table, *small = call(
+        bind(setup_kernel, len(held)),
+        [array.shape for array in held],
+        *held,
         after=(sent_z,),
         plain=True,
-        scratch=[pltpu.SemaphoreType.DMA],
+        copies=len(held),
     )
     fine, sent_a, side_x, side_y = call(
         bind(spread_kernel, plan),
         [(2, rows, LANES), (plan.message, LANES), (rows, LANES), (rows + window, LANES)],
-        where,
+        flags,
         own,
         sent_z,
         got_z,
         table,
-        scalars=1,
     )
     got_a = pair(sent_a, "gx", 1)
     got_x = pair(side_x, "gx", 3)
     got_y = pair(side_y, "gy", 3)
-    (sent_b,) = call(
-        bind(pass_kernel, plan), [(plan.message - rows, LANES)], where, sent_a, got_a, scalars=1
-    )
-    got_b = pair(sent_b, "gx", 3)
+    sent_b, side_b = call(
+        bind(pass_kernel, plan),
+        [(plan.message - rows, LANES), (rows // 2 + window, LANES)],
+        flags,
+        sent_a,
+        got_a,
+    )
+    got_b = pair(sent_b, "gx", 2)
+    got_s = pair(side_b, "gy", 3)
     k1 = ((terms * plan.out_cells, 12 * LANES), BF16)
-    *k1, z1, z1_low, zc, kc = call(
+    params, *k1, z1, z1_low, zc, kc = call(
         bind(coarse_weights_kernel, plan, terms),
         [
+            (6 * terms + 3 * 16, LANES),
             k1,
             k1,
             ((terms, window, LANES), BF16),
@@ -776,68 +806,70 @@
             (plan.out_cells, 2 * LANES),
         ],
         where,
-        params,
         table,
+        *small,
         scalars=1,
         after=(sent_b,),
     )
-    size = rows + 2 * window + plan.top_rows
+    size = rows // 2 + window + plan.top_rows
     cells, sent_c = call(
         bind(stack_kernel, plan),
         [(2, 2 * rows, LANES), (size, LANES)],
-        where,
+        flags,
         fine,
         sent_b,
         got_a,
         got_x,
         got_b,
-        scalars=1,
-        after=(z1, got_y),
+        after=(z1, got_y, got_s),
     )
     got_c = pair(sent_c, "gy", 3)
     kf = ((terms, 2 * LANES, 8 * LANES), BF16)
     *kf, zf, zf_low = call(
         bind(fine_weights_kernel, plan, terms),
         [kf, kf, ((terms, rows, LANES), BF16), ((terms, rows, LANES), BF16)],
-        where,
+        flags,
         params,
         table,
-        scalars=1,
         after=(sent_c,),
     )
-    sums = [(terms, 2 * LANES, rows), (terms * plan.out_cells, window)]
-    near = call(bind(near_kernel, plan, terms), sums, cells, sent_a, got_a, got_b, *kf, *k1, after=(sent_c,))
-    (sent_d,) = call(
-        bind(share_kernel, plan),
-        [(2 * rows + 6 * window + plan.top_rows, LANES)],
-        where,
+    give = (2 * LANES, bz)
+    fine_sum, coarse_sum, give_fine, give_coarse = call(
+        bind(near_kernel, plan, terms),
+        [(terms, 2 * LANES, rows), (terms * plan.out_cells, window), give, (terms * plan.out_cells, window)],
+        flags,
         cells,
         sent_a,
-        sent_c,
-        got_y,
-        got_c,
-        scalars=1,
-        after=(near[1],),
-    )
-    got_d = pair(sent_d, "gy", 1)
-    middle = call(bind(middle_kernel, plan, terms), sums, *near, got_y, got_c, *kf, *k1, after=(sent_d,))
-    (out,) = call(
-        bind(far_kernel, plan, terms),
-        [(bx, by, bz)],
-        *middle,
-        sent_d,
-        got_d,
+        got_a,
+        got_b,
         *kf,
         *k1,
         zf,
         zf_low,
-        z1,
-        z1_low,
-        zc,
-        kc,
-        table,
-        last=True,
-    )
+        after=(sent_c,),
+    )
+    ends = (z1, z1_low, zc, kc, table)
+    (sent_d,) = call(
+        bind(give_kernel, plan, terms), [give], give_fine, give_coarse, got_y, got_s, sent_c, got_c, *k1, *ends
+    )
+    got_d = pair(sent_d, "gy", 1)
+    (kept,) = call(
+        bind(keep_kernel, plan, terms),
+        [give],
+        fine_sum,
+        coarse_sum,
+        got_y,
+        got_s,
+        sent_c,
+        got_c,
+        *kf,
+        *k1,
+        zf,
+        zf_low,
+        *ends,
+        after=(sent_d,),
+    )
+    (out,) = call(bind(add_kernel, plan), [(bx, by, bz)], kept, got_d, last=True)
     return out
 
 

time: 33 us -> 32.5 us (0.985)
  waiting for transfers between devices: 5.74 us -> 7.92 us
  Pallas kernels: 15.1 us -> 13.1 us
  starting transfers between devices: 11.8 us -> 11.1 us
    ppermute x7 -> x8, waiting for transfers between devices: 5.74 us -> 7.92 us  [pair(): return lax.ppermute(value, axis, [(i, i ^ bits) for i in range(count)])]
    pallas_call x11, Pallas kernels: 15.1 us -> 13.1 us  [call(): pl.pallas_call(run, out_shape=[jax.ShapeDtypeStruct(kind, kept_as) if las...]
    ppermute x7 -> x8, starting transfers between devices: 11.8 us -> 11.1 us  [pair(): return lax.ppermute(value, axis, [(i, i ^ bits) for i in range(count)])]
  transfers between devices with their start and end apart: 7 -> 8, of which waited for: 4 -> 5; matrix products, arithmetic and copies ran while one was open for 0% -> 0% of each run, Pallas kernels for 26% -> 28%
where the time goes in v4:
time: 32.5 us; the launch traced here: 32.3 us
  Pallas kernels  13.1 us (40%)
  starting transfers between devices  11.1 us (34%)
  waiting for transfers between devices  7.92 us (24%)
    pallas_call x11, Pallas kernels, call(): pl.pallas_call(run, out_shape=[jax.ShapeDtypeStruct(kind, kept_as) if las...  13.1 us
    ppermute x8, starting transfers between devices, pair(): return lax.ppermute(value, axis, [(i, i ^ bits) for i in range(count)])  11.1 us
    ppermute x8, waiting for transfers between devices, pair(): return lax.ppermute(value, axis, [(i, i ^ bits) for i in range(count)])  7.92 us
  transfers between devices with their start and end apart: 8, of which 5 were waited for; matrix products, arithmetic and copies ran while one was open for 0% of the time, Pallas kernels for 28%

profile of v4, /device:TPU:0, one launch (start us, length us, event | category | flops | bytes accessed | tf_op | source)
XLA Modules:
  0.0 32.3 jit_solution(17066258496272090738)
XLA Ops:
  0.0 1.4 %shard_map.82 = (f32[2,128,128]{2,1,0:T(8,128)S(1)}, f32[112,128]{1,0:T(8,128)S(1)}) custom-call(f32[16,16,128]{2,1,0:T(8,128)} %refs_0_.2, f32[272,128]{1,0:T(8,128)} %constant.30.clone.refs_1_), custom_call_target="tpu_custom_call" | custom-call | tf_op jit(solution)/shard_map/pallas_call | solution.py:732
  1.4 3.0 %collective-permute-start = (f32[112,128]{1,0:T(8,128)S(1)}, f32[112,128]{1,0:T(8,128)S(1)}, u32[]{:S(2)}, u32[]{:S(2)}) collective-permute-start(f32[112,128]{1,0:T(8,128)S(1)} %get-tuple-element.37.refs_6_.refs_2_), channel_id=1, source_target_pairs={{0,1},{1,0},{2,3},{3,2},{4,5},{5,4},{6,7},{7,6},{8,9},{9,8},{10,11... | collective-permute-start | bytes 172040 | tf_op jit(solution)/shard_map/ppermute | solution.py:747
  4.4 1.3 %shard_map.83 = (f32[2272,128]{1,0:T(8,128)S(1)}, f32[2,4]{1,0:T(2,128)S(1)}, f32[2,4]{1,0:T(2,128)S(1)}, f32[4,4]{1,0:T(4,128)S(1)}, f32[4,4]{1,0:T(4,128)S(1)}, /*index=5*/f32[16,16]{1,0:T(8,128)S(1)}) custom-call(f32[2272,128]{1,0:T(8,128)} %constant.31.clone.refs_0_, f32[2,4]{1,0:T(2,128)} %refs_1_.2, f32[2,4]{1,0:T(2,128)} %refs_2_.1, f32[4,4]{1,0:T(4,128)} %refs_3_.1, ...), custom_call_target="tpu_custom_call" | custom-call | tf_op jit(solution)/shard_map/pallas_call | solution.py:732
  5.7 0.1 fusion
  5.8 0.7 %collective-permute-done.refs_3_ = f32[112,128]{1,0:T(8,128)S(1)} collective-permute-done((f32[112,128]{1,0:T(8,128)S(1)}, f32[112,128]{1,0:T(8,128)S(1)}, u32[]{:S(2)}, u32[]{:S(2)}) %collective-permute-start) | collective-permute-done | bytes 57376 | tf_op jit(solution)/shard_map/ppermute | solution.py:747
  6.5 0.1 broadcast_in_dim.2.refs_0_
  6.6 0.4 %shard_map.84 = (f32[2,144,128]{2,1,0:T(8,128)S(1)}, f32[264,128]{1,0:T(8,128)S(1)}, f32[144,128]{1,0:T(8,128)S(1)}, f32[232,128]{1,0:T(8,128)S(1)}) custom-call(f32[3,128]{1,0:T(4,128)S(1)} %broadcast_in_dim.2.refs_0_, f32[2,128,128]{2,1,0:T(8,128)S(1)} %get-tuple-element.36.refs_1_, f32[112,128]{1,0:T(8,128)S(1)} %get-tuple-element.37.refs_6_.refs_2_, ...), custom_call_target="tpu_custom_call" | custom-call | tf_op jit(solution)/shard_map/pallas_call | solution.py:732
  7.0 2.2 %collective-permute-start.1 = (f32[264,128]{1,0:T(8,128)S(1)}, f32[264,128]{1,0:T(8,128)S(1)}, u32[]{:S(2)}, u32[]{:S(2)}) collective-permute-start(f32[264,128]{1,0:T(8,128)S(1)} %get-tuple-element.40.refs_1_.refs_2_), channel_id=1, source_target_pairs={{0,8},{8,0},{16,24},{24,16},{1,9},{9,1},{17,25},{25,17},{2,10},{10... | collective-permute-start | bytes 405512 | tf_op jit(solution)/shard_map/ppermute | solution.py:747
  9.2 0.0 collective-permute-start.4
  9.2 3.0 %collective-permute-done.1.refs_2_.refs_3_ = f32[264,128]{1,0:T(8,128)S(1)} collective-permute-done((f32[264,128]{1,0:T(8,128)S(1)}, f32[264,128]{1,0:T(8,128)S(1)}, u32[]{:S(2)}, u32[]{:S(2)}) %collective-permute-start.1) | collective-permute-done | bytes 135200 | tf_op jit(solution)/shard_map/ppermute | solution.py:747
  12.2 0.1 shard_map.85
  12.3 0.1 collective-permute-start.5
  12.4 4.1 %collective-permute-start.2 = (f32[144,128]{1,0:T(8,128)S(1)}, f32[144,128]{1,0:T(8,128)S(1)}, u32[]{:S(2)}, u32[]{:S(2)}) collective-permute-start(f32[144,128]{1,0:T(8,128)S(1)} %get-tuple-element.42), channel_id=1, source_target_pairs={{0,24},{8,16},{16,8},{24,0},{1,25},{9,17},{17,9},{25,1},{2,26},{10... | collective-permute-start | bytes 221192 | tf_op jit(solution)/shard_map/ppermute | solution.py:747
  16.5 0.0 collective-permute-start.3
  16.5 2.2 %shard_map.86 = (f32[72,128]{1,0:T(8,128)S(1)}, bf16[448,1536]{1,0:T(8,128)(2,1)S(1)}, bf16[448,1536]{1,0:T(8,128)(2,1)S(1)}, bf16[4,88,128]{2,1,0:T(8,128)(2,1)...) custom-call(s32[3]{0:T(128)S(1)} %get-tuple-element.68.refs_0_, ...), custom_call_target="tpu_custom_call" | custom-call | tf_op jit(solution)/shard_map/pallas_call | solution.py:732
  18.7 0.2 collective-permute-done.2.refs_4_
  18.9 0.0 collective-permute-done.4.refs_7_.refs_2_
  18.9 3.8 %collective-permute-done.3.refs_5_.refs_4_ = f32[120,128]{1,0:T(8,128)S(1)} collective-permute-done((f32[120,128]{1,0:T(8,128)S(1)}, f32[120,128]{1,0:T(8,128)S(1)}, u32[]{:S(2)}, u32[]{:S(2)}) %collective-permute-start.3) | collective-permute-done | bytes 61472 | tf_op jit(solution)/shard_map/ppermute | solution.py:747
  22.7 0.0 collective-permute-done.5.refs_8_.refs_3_
  22.7 0.1 shard_map.87
  22.8 1.0 %collective-permute-start.6 = (f32[192,128]{1,0:T(8,128)S(1)}, f32[192,128]{1,0:T(8,128)S(1)}, u32[]{:S(2)}, u32[]{:S(2)}) collective-permute-start(f32[192,128]{1,0:T(8,128)S(1)} %get-tuple-element.53.refs_3_.refs_11_.refs_4_), channel_id=1, source_target_pairs={{0,6},{2,4},{4,2},{6,0},{1,7},{3,5},{5,3},{7,1},{8,14},{10,12},{12... | collective-permute-start | bytes 294920 | tf_op jit(solution)/shard_map/ppermute | solution.py:747
  23.8 0.9 %shard_map.88 = (bf16[4,256,1024]{2,1,0:T(8,128)(2,1)S(1)}, bf16[4,256,1024]{2,1,0:T(8,128)(2,1)S(1)}, bf16[4,144,128]{2,1,0:T(8,128)(2,1)S(1)}, bf16[4,144,128]{2,1,0:T(8,128)(2,1)S(1)}) custom-call(f32[3,128]{1,0:T(4,128)S(1)} %broadcast_in_dim.2.refs_0_, f32[72,128]{1,0:T(8,128)S(1)} %get-tuple-element.52.refs_1_, ...), custom_call_target="tpu_custom_call" | custom-call | tf_op jit(solution)/shard_map/pallas_call | solution.py:732
  24.8 2.4 %shard_map.89 = (f32[4,256,144]{2,1,0:T(8,128)S(1)}, f32[448,88]{1,0:T(8,128)S(1)}, f32[256,128]{1,0:T(8,128)S(1)}, f32[448,88]{1,0:T(8,128)S(1)}) custom-call(f32[3,128]{1,0:T(4,128)S(1)} %broadcast_in_dim.2.refs_0_, f32[2,288,128]{2,1,0:T(8,128)S(1)} %get-tuple-element.51.refs_1_, f32[264,128]{1,0:T(8,128)S(1)} %get-tuple-element.40.refs_1_.refs_2_, ...), custom_call_target="tpu_custom_call" | custom-call | tf_op jit(solution)/shard_map/pallas_call | solution.py:732
  27.2 0.2 collective-permute-done.6.refs_5_
  27.4 1.5 %shard_map.90.refs_17_ = f32[256,128]{1,0:T(8,128)S(1)} custom-call(f32[256,128]{1,0:T(8,128)S(1)} %get-tuple-element.65.refs_0_, f32[448,88]{1,0:T(8,128)S(1)} %get-tuple-element.66.refs_1_, f32[232,128]{1,0:T(8,128)S(1)} %collective-permute-done.4.refs_7_.refs_2_, f32[160,128]{1,0:T(8,128)S(1)} %collective-permute-done.5.refs_8_.refs_3_, ...), custom_call_target="tpu_custom_call" | custom-call | tf_op jit(solution)/shard_map/pallas_call | solution.py:732
  28.9 0.7 %collective-permute-start.7 = (f32[256,128]{1,0:T(8,128)S(1)}, f32[256,128]{1,0:T(8,128)S(1)}, u32[]{:S(2)}, u32[]{:S(2)}) collective-permute-start(f32[256,128]{1,0:T(8,128)S(1)} %shard_map.90.refs_17_), channel_id=1, source_target_pairs={{0,2},{2,0},{4,6},{6,4},{1,3},{3,1},{5,7},{7,5},{8,10},{10,8},{12,... | collective-permute-start | bytes 393224 | tf_op jit(solution)/shard_map/ppermute | solution.py:747
  29.6 2.0 %shard_map.91.refs_0_ = f32[256,128]{1,0:T(8,128)S(1)} custom-call(f32[4,256,144]{2,1,0:T(8,128)S(1)} %get-tuple-element.60.refs_0_, f32[448,88]{1,0:T(8,128)S(1)} %get-tuple-element.61.refs_1_, f32[232,128]{1,0:T(8,128)S(1)} %collective-permute-done.4.refs_7_.refs_2_, f32[160,128]{1,0:T(8,128)S(1)} %collective-permute-done.5.refs_8_.refs_3_, ...), custom_call_target="tpu_custom_call" | custom-call | tf_op jit(solution)/shard_map/pallas_call | solution.py:732
  31.6 0.0 collective-permute-done.7.refs_1_
  31.7 0.7 %shard_map.92 = f32[16,16,128]{2,1,0:T(8,128)} custom-call(f32[256,128]{1,0:T(8,128)S(1)} %shard_map.91.refs_0_, f32[256,128]{1,0:T(8,128)S(1)} %collective-permute-done.7.refs_1_), custom_call_target="tpu_custom_call" | custom-call | tf_op jit(solution)/shard_map/pallas_call | solution.py:732
Async XLA Ops:
  1.4 5.1 %collective-permute-start = (f32[112,128]{1,0:T(8,128)S(1)}, f32[112,128]{1,0:T(8,128)S(1)}, u32[]{:S(2)}, u32[]{:S(2)}) collective-permute-start(f32[112,128]{1,0:T(8,128)S(1)} %get-tuple-element.37.refs_6_.refs_2_), channel_id=1, source_target_pairs={{0,1},{1,0},{2,3},{3,2},{4,5},{5,4},{6,7},{7,6},{8,9},{9,8},{10,11... | collective-permute-start | bytes 172040 | tf_op jit(solution)/shard_map/ppermute | solution.py:747
  7.0 5.2 %collective-permute-start.1 = (f32[264,128]{1,0:T(8,128)S(1)}, f32[264,128]{1,0:T(8,128)S(1)}, u32[]{:S(2)}, u32[]{:S(2)}) collective-permute-start(f32[264,128]{1,0:T(8,128)S(1)} %get-tuple-element.40.refs_1_.refs_2_), channel_id=1, source_target_pairs={{0,8},{8,0},{16,24},{24,16},{1,9},{9,1},{17,25},{25,17},{2,10},{10... | collective-permute-start | bytes 405512 | tf_op jit(solution)/shard_map/ppermute | solution.py:747
  9.2 9.8 %collective-permute-start.4 = (f32[232,128]{1,0:T(8,128)S(1)}, f32[232,128]{1,0:T(8,128)S(1)}, u32[]{:S(2)}, u32[]{:S(2)}) collective-permute-start(f32[232,128]{1,0:T(8,128)S(1)} %get-tuple-element.49), channel_id=1, source_target_pairs={{0,6},{2,4},{4,2},{6,0},{1,7},{3,5},{5,3},{7,1},{8,14},{10,12},{12... | collective-permute-start | bytes 356360 | tf_op jit(solution)/shard_map/ppermute | solution.py:747
  12.3 10.4 %collective-permute-start.5 = (f32[160,128]{1,0:T(8,128)S(1)}, f32[160,128]{1,0:T(8,128)S(1)}, u32[]{:S(2)}, u32[]{:S(2)}) collective-permute-start(f32[160,128]{1,0:T(8,128)S(1)} %get-tuple-element.50), channel_id=1, source_target_pairs={{0,6},{2,4},{4,2},{6,0},{1,7},{3,5},{5,3},{7,1},{8,14},{10,12},{12... | collective-permute-start | bytes 245768 | tf_op jit(solution)/shard_map/ppermute | solution.py:747
  12.4 6.5 %collective-permute-start.2 = (f32[144,128]{1,0:T(8,128)S(1)}, f32[144,128]{1,0:T(8,128)S(1)}, u32[]{:S(2)}, u32[]{:S(2)}) collective-permute-start(f32[144,128]{1,0:T(8,128)S(1)} %get-tuple-element.42), channel_id=1, source_target_pairs={{0,24},{8,16},{16,8},{24,0},{1,25},{9,17},{17,9},{25,1},{2,26},{10... | collective-permute-start | bytes 221192 | tf_op jit(solution)/shard_map/ppermute | solution.py:747
  16.5 6.2 %collective-permute-start.3 = (f32[120,128]{1,0:T(8,128)S(1)}, f32[120,128]{1,0:T(8,128)S(1)}, u32[]{:S(2)}, u32[]{:S(2)}) collective-permute-start(f32[120,128]{1,0:T(8,128)S(1)} %get-tuple-element.41.refs_7_.refs_2_), channel_id=1, source_target_pairs={{0,16},{8,24},{16,0},{24,8},{1,17},{9,25},{17,1},{25,9},{2,18},{10... | collective-permute-start | bytes 184328 | tf_op jit(solution)/shard_map/ppermute | solution.py:747
  22.8 4.6 %collective-permute-start.6 = (f32[192,128]{1,0:T(8,128)S(1)}, f32[192,128]{1,0:T(8,128)S(1)}, u32[]{:S(2)}, u32[]{:S(2)}) collective-permute-start(f32[192,128]{1,0:T(8,128)S(1)} %get-tuple-element.53.refs_3_.refs_11_.refs_4_), channel_id=1, source_target_pairs={{0,6},{2,4},{4,2},{6,0},{1,7},{3,5},{5,3},{7,1},{8,14},{10,12},{12... | collective-permute-start | bytes 294920 | tf_op jit(solution)/shard_map/ppermute | solution.py:747
  28.9 2.7 %collective-permute-start.7 = (f32[256,128]{1,0:T(8,128)S(1)}, f32[256,128]{1,0:T(8,128)S(1)}, u32[]{:S(2)}, u32[]{:S(2)}) collective-permute-start(f32[256,128]{1,0:T(8,128)S(1)} %shard_map.90.refs_17_), channel_id=1, source_target_pairs={{0,2},{2,0},{4,6},{6,4},{1,3},{3,1},{5,7},{7,5},{8,10},{10,8},{12,... | collective-permute-start | bytes 393224 | tf_op jit(solution)/shard_map/ppermute | solution.py:747

commit v5 on v4

--- a/solution.py
+++ b/solution.py
@@ -490,11 +490,12 @@
     out_ref[rows // 2 + window :] = sent_ref[window:] + pltpu.roll(second_ref[window:], 2 * plan.group, 1)
 
 
+def turned(left, right):
+    return lax.dot_general(left, right, (((1,), (1,)), ((), ())), preferred_element_type=F32)
+
+
 def dot_turned(left, right):
-    def product(first, second):
-        return lax.dot_general(first, second, (((1,), (1,)), ((), ())), preferred_element_type=F32)
-
-    return product(left[0], right[0]) + product(left[1], right[0]) + product(left[0], right[1])
+    return turned(left[0], right[0]) + turned(left[1], right[0]) + turned(left[0], right[1])
 
 
 def fine_weights_kernel(plan, terms, flags_ref, params_ref, table_ref, kf_ref, kf_low_ref, zf_ref, zf_low_ref):
@@ -516,7 +517,7 @@
         exponent = params_ref[term : term + 1]
         scale = params_ref[terms + term : terms + term + 1]
         along_x = [decay(exponent, x_in - x_out)[:, None, :] for x_in in (own_x, far_x)]
-        for group in range(4):
+        for group in range(3):
             y_in = own_y + (F32(group * half) if group < 2 else y_far)
             for part in range(2):
                 along_y = decay(exponent, y_in - (y_out + part * half)) * scale
@@ -571,7 +572,7 @@
         used = cells_ref[7:8] if slot < 2 else cells_ref[8:9]
         squares_x.append(squared(x_in - x_out, bx * plan.counts[0]) + used)
     toward = jnp.where(even_y, F32(by), F32(-by))
-    for group, offset in enumerate((F32(0), -toward, -toward, F32(2 * by))):
+    for group, offset in enumerate((F32(0), -toward, F32(2 * by))):
         square_y = squared(cells_ref[6:7] + offset - y_out, by * plan.counts[1]) + out_cells_ref[2]
         for slot in range(3):
             total = squares_x[slot] + square_y
@@ -626,8 +627,13 @@
 
 
 def sum_coarse(blocks, refs, at):
-    cols = pl.ds(at * LANES, blocks.shape[1])
-    return dot_turned((refs[0][:, cols], refs[1][:, cols]), split(blocks))
+    cols, count = pl.ds(at * LANES, blocks.shape[1]), blocks.shape[0]
+    high = blocks.astype(BF16)
+    exact = high.astype(F32)
+    gap = jnp.zeros((LANES - count, blocks.shape[1]), F32)
+    both = jnp.concatenate([exact, gap, blocks - exact], axis=0).astype(BF16)
+    sums = turned(refs[0][:, cols], both)
+    return sums[:, :count] + sums[:, LANES : LANES + count] + turned(refs[1][:, cols], high)
 
 
 def fine_potential(fine, refs):
@@ -657,8 +663,8 @@
     near = jnp.concatenate(near, axis=1)
     other = [pick(flags_ref, 1, cells_ref[1, at : at + rows], cells_ref[0, at : at + rows]) for at in (0, rows)]
     other = jnp.concatenate(other, axis=1)
-    give_fine_ref[...] = fine_potential(sum_fine(terms, other, kf, 6), (zf_ref, zf_low_ref))
-    give_coarse_ref[...] = sum_coarse(near, k1, 6)
+    give_fine_ref[...] = fine_potential(sum_fine(terms, other, kf, 4), (zf_ref, zf_low_ref))
+    give_coarse_ref[...] = sum_coarse(near, k1, 3)
     for term, value in enumerate(sum_fine(terms, jnp.concatenate(groups, axis=1), kf, 0)):
         fine_ref[term] = value
     coarse_ref[...] = sum_coarse(near, k1, 0)
@@ -678,7 +684,7 @@
 
 def give_kernel(plan, terms, fine_ref, coarse_ref, side_ref, strip_ref, sent_ref, got_ref, k1_ref, k1_low_ref,
                 z1_ref, z1_low_ref, zc_ref, kc_ref, table_ref, out_ref):
-    coarse = coarse_ref[...] + sum_coarse(arrived(plan, side_ref, strip_ref, got_ref), (k1_ref, k1_low_ref), 9)
+    coarse = coarse_ref[...] + sum_coarse(arrived(plan, side_ref, strip_ref, got_ref), (k1_ref, k1_low_ref), 6)
     top = top_charges(plan, sent_ref, got_ref, zc_ref)
     out_ref[...] = fine_ref[...] + coarse_potential(
         plan, terms, coarse, (z1_ref, z1_low_ref), top, kc_ref[:, LANES:], table_ref
@@ -793,7 +799,7 @@
     )
     got_b = pair(sent_b, "gx", 2)
     got_s = pair(side_b, "gy", 3)
-    k1 = ((terms * plan.out_cells, 12 * LANES), BF16)
+    k1 = ((terms * plan.out_cells, 9 * LANES), BF16)
     params, *k1, z1, z1_low, zc, kc = call(
         bind(coarse_weights_kernel, plan, terms),
         [
@@ -824,7 +830,7 @@
         after=(z1, got_y, got_s),
     )
     got_c = pair(sent_c, "gy", 3)
-    kf = ((terms, 2 * LANES, 8 * LANES), BF16)
+    kf = ((terms, 2 * LANES, 6 * LANES), BF16)
     *kf, zf, zf_low = call(
         bind(fine_weights_kernel, plan, terms),
         [kf, kf, ((terms, rows, LANES), BF16), ((terms, rows, LANES), BF16)],

time: 32.5 us -> 31.9 us (0.982)
  Pallas kernels: 13.1 us -> 12.3 us
  waiting for transfers between devices: 7.92 us -> 8.34 us
    pallas_call x11, Pallas kernels: 13.1 us -> 12.3 us  [call(): pl.pallas_call(run, out_shape=[jax.ShapeDtypeStruct(kind, kept_as) if las...]
    ppermute x8, waiting for transfers between devices: 7.92 us -> 8.34 us  [pair(): return lax.ppermute(value, axis, [(i, i ^ bits) for i in range(count)])]
  transfers between devices with their start and end apart: 8 -> 8, of which waited for: 5 -> 5; matrix products, arithmetic and copies ran while one was open for 0% -> 0% of each run, Pallas kernels for 28% -> 27%
where the time goes in v5:
time: 31.9 us; the launch traced here: 31.7 us
  Pallas kernels  12.3 us (39%)
  starting transfers between devices  10.8 us (34%)
  waiting for transfers between devices  8.34 us (26%)
    pallas_call x11, Pallas kernels, call(): pl.pallas_call(run, out_shape=[jax.ShapeDtypeStruct(kind, kept_as) if las...  12.3 us
    ppermute x8, starting transfers between devices, pair(): return lax.ppermute(value, axis, [(i, i ^ bits) for i in range(count)])  10.8 us
    ppermute x8, waiting for transfers between devices, pair(): return lax.ppermute(value, axis, [(i, i ^ bits) for i in range(count)])  8.34 us
  transfers between devices with their start and end apart: 8, of which 5 were waited for; matrix products, arithmetic and copies ran while one was open for 0% of the time, Pallas kernels for 27%

profile of v5, /device:TPU:0, one launch (start us, length us, event | category | flops | bytes accessed | tf_op | source)
XLA Modules:
  0.0 31.7 jit_solution(5619685171760733256)
XLA Ops:
  0.0 1.4 %shard_map.82 = (f32[2,128,128]{2,1,0:T(8,128)S(1)}, f32[112,128]{1,0:T(8,128)S(1)}) custom-call(f32[16,16,128]{2,1,0:T(8,128)} %refs_0_.2, f32[272,128]{1,0:T(8,128)} %constant.30.clone.refs_1_), custom_call_target="tpu_custom_call" | custom-call | tf_op jit(solution)/shard_map/pallas_call | solution.py:738
  1.4 3.0 %collective-permute-start = (f32[112,128]{1,0:T(8,128)S(1)}, f32[112,128]{1,0:T(8,128)S(1)}, u32[]{:S(2)}, u32[]{:S(2)}) collective-permute-start(f32[112,128]{1,0:T(8,128)S(1)} %get-tuple-element.37.refs_6_.refs_2_), channel_id=1, source_target_pairs={{0,1},{1,0},{2,3},{3,2},{4,5},{5,4},{6,7},{7,6},{8,9},{9,8},{10,11... | collective-permute-start | bytes 172040 | tf_op jit(solution)/shard_map/ppermute | solution.py:753
  4.4 1.3 %shard_map.83 = (f32[2272,128]{1,0:T(8,128)S(1)}, f32[2,4]{1,0:T(2,128)S(1)}, f32[2,4]{1,0:T(2,128)S(1)}, f32[4,4]{1,0:T(4,128)S(1)}, f32[4,4]{1,0:T(4,128)S(1)}, /*index=5*/f32[16,16]{1,0:T(8,128)S(1)}) custom-call(f32[2272,128]{1,0:T(8,128)} %constant.31.clone.refs_0_, f32[2,4]{1,0:T(2,128)} %refs_1_.2, f32[2,4]{1,0:T(2,128)} %refs_2_.1, f32[4,4]{1,0:T(4,128)} %refs_3_.1, ...), custom_call_target="tpu_custom_call" | custom-call | tf_op jit(solution)/shard_map/pallas_call | solution.py:738
  5.7 0.1 fusion
  5.8 0.7 %collective-permute-done.refs_3_ = f32[112,128]{1,0:T(8,128)S(1)} collective-permute-done((f32[112,128]{1,0:T(8,128)S(1)}, f32[112,128]{1,0:T(8,128)S(1)}, u32[]{:S(2)}, u32[]{:S(2)}) %collective-permute-start) | collective-permute-done | bytes 57376 | tf_op jit(solution)/shard_map/ppermute | solution.py:753
  6.5 0.1 broadcast_in_dim.2.refs_0_
  6.6 0.4 %shard_map.84 = (f32[2,144,128]{2,1,0:T(8,128)S(1)}, f32[264,128]{1,0:T(8,128)S(1)}, f32[144,128]{1,0:T(8,128)S(1)}, f32[232,128]{1,0:T(8,128)S(1)}) custom-call(f32[3,128]{1,0:T(4,128)S(1)} %broadcast_in_dim.2.refs_0_, f32[2,128,128]{2,1,0:T(8,128)S(1)} %get-tuple-element.36.refs_1_, f32[112,128]{1,0:T(8,128)S(1)} %get-tuple-element.37.refs_6_.refs_2_, ...), custom_call_target="tpu_custom_call" | custom-call | tf_op jit(solution)/shard_map/pallas_call | solution.py:738
  7.0 2.2 %collective-permute-start.1 = (f32[264,128]{1,0:T(8,128)S(1)}, f32[264,128]{1,0:T(8,128)S(1)}, u32[]{:S(2)}, u32[]{:S(2)}) collective-permute-start(f32[264,128]{1,0:T(8,128)S(1)} %get-tuple-element.40.refs_1_.refs_2_), channel_id=1, source_target_pairs={{0,8},{8,0},{16,24},{24,16},{1,9},{9,1},{17,25},{25,17},{2,10},{10... | collective-permute-start | bytes 405512 | tf_op jit(solution)/shard_map/ppermute | solution.py:753
  9.2 0.0 collective-permute-start.4
  9.2 3.0 %collective-permute-done.1.refs_2_.refs_3_ = f32[264,128]{1,0:T(8,128)S(1)} collective-permute-done((f32[264,128]{1,0:T(8,128)S(1)}, f32[264,128]{1,0:T(8,128)S(1)}, u32[]{:S(2)}, u32[]{:S(2)}) %collective-permute-start.1) | collective-permute-done | bytes 135200 | tf_op jit(solution)/shard_map/ppermute | solution.py:753
  12.2 0.1 shard_map.85
  12.3 0.1 collective-permute-start.5
  12.4 4.1 %collective-permute-start.2 = (f32[144,128]{1,0:T(8,128)S(1)}, f32[144,128]{1,0:T(8,128)S(1)}, u32[]{:S(2)}, u32[]{:S(2)}) collective-permute-start(f32[144,128]{1,0:T(8,128)S(1)} %get-tuple-element.42), channel_id=1, source_target_pairs={{0,24},{8,16},{16,8},{24,0},{1,25},{9,17},{17,9},{25,1},{2,26},{10... | collective-permute-start | bytes 221192 | tf_op jit(solution)/shard_map/ppermute | solution.py:753
  16.5 0.0 collective-permute-start.3
  16.5 2.1 %shard_map.86 = (f32[72,128]{1,0:T(8,128)S(1)}, bf16[448,1152]{1,0:T(8,128)(2,1)S(1)}, bf16[448,1152]{1,0:T(8,128)(2,1)S(1)}, bf16[4,88,128]{2,1,0:T(8,128)(2,1)...) custom-call(s32[3]{0:T(128)S(1)} %get-tuple-element.68.refs_0_, ...), custom_call_target="tpu_custom_call" | custom-call | tf_op jit(solution)/shard_map/pallas_call | solution.py:738
  18.6 0.3 %collective-permute-done.2.refs_4_ = f32[144,128]{1,0:T(8,128)S(1)} collective-permute-done((f32[144,128]{1,0:T(8,128)S(1)}, f32[144,128]{1,0:T(8,128)S(1)}, u32[]{:S(2)}, u32[]{:S(2)}) %collective-permute-start.2) | collective-permute-done | bytes 73760 | tf_op jit(solution)/shard_map/ppermute | solution.py:753
  18.9 0.0 collective-permute-done.4.refs_7_.refs_2_
  18.9 3.8 %collective-permute-done.3.refs_5_.refs_4_ = f32[120,128]{1,0:T(8,128)S(1)} collective-permute-done((f32[120,128]{1,0:T(8,128)S(1)}, f32[120,128]{1,0:T(8,128)S(1)}, u32[]{:S(2)}, u32[]{:S(2)}) %collective-permute-start.3) | collective-permute-done | bytes 61472 | tf_op jit(solution)/shard_map/ppermute | solution.py:753
  22.7 0.0 collective-permute-done.5.refs_8_.refs_3_
  22.7 0.1 shard_map.87
  22.8 1.0 %collective-permute-start.6 = (f32[192,128]{1,0:T(8,128)S(1)}, f32[192,128]{1,0:T(8,128)S(1)}, u32[]{:S(2)}, u32[]{:S(2)}) collective-permute-start(f32[192,128]{1,0:T(8,128)S(1)} %get-tuple-element.53.refs_3_.refs_11_.refs_4_), channel_id=1, source_target_pairs={{0,6},{2,4},{4,2},{6,0},{1,7},{3,5},{5,3},{7,1},{8,14},{10,12},{12... | collective-permute-start | bytes 294920 | tf_op jit(solution)/shard_map/ppermute | solution.py:753
  23.8 0.8 %shard_map.88 = (bf16[4,256,768]{2,1,0:T(8,128)(2,1)S(1)}, bf16[4,256,768]{2,1,0:T(8,128)(2,1)S(1)}, bf16[4,144,128]{2,1,0:T(8,128)(2,1)S(1)}, bf16[4,144,128]{2,1,0:T(8,128)(2,1)S(1)}) custom-call(f32[3,128]{1,0:T(4,128)S(1)} %broadcast_in_dim.2.refs_0_, f32[72,128]{1,0:T(8,128)S(1)} %get-tuple-element.52.refs_1_, ...), custom_call_target="tpu_custom_call" | custom-call | tf_op jit(solution)/shard_map/pallas_call | solution.py:738
  24.6 2.2 %shard_map.89 = (f32[4,256,144]{2,1,0:T(8,128)S(1)}, f32[448,88]{1,0:T(8,128)S(1)}, f32[256,128]{1,0:T(8,128)S(1)}, f32[448,88]{1,0:T(8,128)S(1)}) custom-call(f32[3,128]{1,0:T(4,128)S(1)} %broadcast_in_dim.2.refs_0_, f32[2,288,128]{2,1,0:T(8,128)S(1)} %get-tuple-element.51.refs_1_, f32[264,128]{1,0:T(8,128)S(1)} %get-tuple-element.40.refs_1_.refs_2_, ...), custom_call_target="tpu_custom_call" | custom-call | tf_op jit(solution)/shard_map/pallas_call | solution.py:738
  26.9 0.5 %collective-permute-done.6.refs_5_ = f32[192,128]{1,0:T(8,128)S(1)} collective-permute-done((f32[192,128]{1,0:T(8,128)S(1)}, f32[192,128]{1,0:T(8,128)S(1)}, u32[]{:S(2)}, u32[]{:S(2)}) %collective-permute-start.6) | collective-permute-done | bytes 98336 | tf_op jit(solution)/shard_map/ppermute | solution.py:753
  27.4 1.2 %shard_map.90.refs_17_ = f32[256,128]{1,0:T(8,128)S(1)} custom-call(f32[256,128]{1,0:T(8,128)S(1)} %get-tuple-element.65.refs_0_, f32[448,88]{1,0:T(8,128)S(1)} %get-tuple-element.66.refs_1_, f32[232,128]{1,0:T(8,128)S(1)} %collective-permute-done.4.refs_7_.refs_2_, f32[160,128]{1,0:T(8,128)S(1)} %collective-permute-done.5.refs_8_.refs_3_, ...), custom_call_target="tpu_custom_call" | custom-call | tf_op jit(solution)/shard_map/pallas_call | solution.py:738
  28.6 0.5 %collective-permute-start.7 = (f32[256,128]{1,0:T(8,128)S(1)}, f32[256,128]{1,0:T(8,128)S(1)}, u32[]{:S(2)}, u32[]{:S(2)}) collective-permute-start(f32[256,128]{1,0:T(8,128)S(1)} %shard_map.90.refs_17_), channel_id=1, source_target_pairs={{0,2},{2,0},{4,6},{6,4},{1,3},{3,1},{5,7},{7,5},{8,10},{10,8},{12,... | collective-permute-start | bytes 393224 | tf_op jit(solution)/shard_map/ppermute | solution.py:753
  29.1 1.9 %shard_map.91.refs_0_ = f32[256,128]{1,0:T(8,128)S(1)} custom-call(f32[4,256,144]{2,1,0:T(8,128)S(1)} %get-tuple-element.60.refs_0_, f32[448,88]{1,0:T(8,128)S(1)} %get-tuple-element.61.refs_1_, f32[232,128]{1,0:T(8,128)S(1)} %collective-permute-done.4.refs_7_.refs_2_, f32[160,128]{1,0:T(8,128)S(1)} %collective-permute-done.5.refs_8_.refs_3_, ...), custom_call_target="tpu_custom_call" | custom-call | tf_op jit(solution)/shard_map/pallas_call | solution.py:738
  31.0 0.0 collective-permute-done.7.refs_1_
  31.1 0.7 %shard_map.92 = f32[16,16,128]{2,1,0:T(8,128)} custom-call(f32[256,128]{1,0:T(8,128)S(1)} %shard_map.91.refs_0_, f32[256,128]{1,0:T(8,128)S(1)} %collective-permute-done.7.refs_1_), custom_call_target="tpu_custom_call" | custom-call | tf_op jit(solution)/shard_map/pallas_call | solution.py:738
Async XLA Ops:
  1.4 5.1 %collective-permute-start = (f32[112,128]{1,0:T(8,128)S(1)}, f32[112,128]{1,0:T(8,128)S(1)}, u32[]{:S(2)}, u32[]{:S(2)}) collective-permute-start(f32[112,128]{1,0:T(8,128)S(1)} %get-tuple-element.37.refs_6_.refs_2_), channel_id=1, source_target_pairs={{0,1},{1,0},{2,3},{3,2},{4,5},{5,4},{6,7},{7,6},{8,9},{9,8},{10,11... | collective-permute-start | bytes 172040 | tf_op jit(solution)/shard_map/ppermute | solution.py:753
  7.0 5.2 %collective-permute-start.1 = (f32[264,128]{1,0:T(8,128)S(1)}, f32[264,128]{1,0:T(8,128)S(1)}, u32[]{:S(2)}, u32[]{:S(2)}) collective-permute-start(f32[264,128]{1,0:T(8,128)S(1)} %get-tuple-element.40.refs_1_.refs_2_), channel_id=1, source_target_pairs={{0,8},{8,0},{16,24},{24,16},{1,9},{9,1},{17,25},{25,17},{2,10},{10... | collective-permute-start | bytes 405512 | tf_op jit(solution)/shard_map/ppermute | solution.py:753
  9.2 9.8 %collective-permute-start.4 = (f32[232,128]{1,0:T(8,128)S(1)}, f32[232,128]{1,0:T(8,128)S(1)}, u32[]{:S(2)}, u32[]{:S(2)}) collective-permute-start(f32[232,128]{1,0:T(8,128)S(1)} %get-tuple-element.49), channel_id=1, source_target_pairs={{0,6},{2,4},{4,2},{6,0},{1,7},{3,5},{5,3},{7,1},{8,14},{10,12},{12... | collective-permute-start | bytes 356360 | tf_op jit(solution)/shard_map/ppermute | solution.py:753
  12.3 10.4 %collective-permute-start.5 = (f32[160,128]{1,0:T(8,128)S(1)}, f32[160,128]{1,0:T(8,128)S(1)}, u32[]{:S(2)}, u32[]{:S(2)}) collective-permute-start(f32[160,128]{1,0:T(8,128)S(1)} %get-tuple-element.50), channel_id=1, source_target_pairs={{0,6},{2,4},{4,2},{6,0},{1,7},{3,5},{5,3},{7,1},{8,14},{10,12},{12... | collective-permute-start | bytes 245768 | tf_op jit(solution)/shard_map/ppermute | solution.py:753
  12.4 6.5 %collective-permute-start.2 = (f32[144,128]{1,0:T(8,128)S(1)}, f32[144,128]{1,0:T(8,128)S(1)}, u32[]{:S(2)}, u32[]{:S(2)}) collective-permute-start(f32[144,128]{1,0:T(8,128)S(1)} %get-tuple-element.42), channel_id=1, source_target_pairs={{0,24},{8,16},{16,8},{24,0},{1,25},{9,17},{17,9},{25,1},{2,26},{10... | collective-permute-start | bytes 221192 | tf_op jit(solution)/shard_map/ppermute | solution.py:753
  16.5 6.2 %collective-permute-start.3 = (f32[120,128]{1,0:T(8,128)S(1)}, f32[120,128]{1,0:T(8,128)S(1)}, u32[]{:S(2)}, u32[]{:S(2)}) collective-permute-start(f32[120,128]{1,0:T(8,128)S(1)} %get-tuple-element.41.refs_7_.refs_2_), channel_id=1, source_target_pairs={{0,16},{8,24},{16,0},{24,8},{1,17},{9,25},{17,1},{25,9},{2,18},{10... | collective-permute-start | bytes 184328 | tf_op jit(solution)/shard_map/ppermute | solution.py:753
  22.8 4.6 %collective-permute-start.6 = (f32[192,128]{1,0:T(8,128)S(1)}, f32[192,128]{1,0:T(8,128)S(1)}, u32[]{:S(2)}, u32[]{:S(2)}) collective-permute-start(f32[192,128]{1,0:T(8,128)S(1)} %get-tuple-element.53.refs_3_.refs_11_.refs_4_), channel_id=1, source_target_pairs={{0,6},{2,4},{4,2},{6,0},{1,7},{3,5},{5,3},{7,1},{8,14},{10,12},{12... | collective-permute-start | bytes 294920 | tf_op jit(solution)/shard_map/ppermute | solution.py:753
  28.6 2.4 %collective-permute-start.7 = (f32[256,128]{1,0:T(8,128)S(1)}, f32[256,128]{1,0:T(8,128)S(1)}, u32[]{:S(2)}, u32[]{:S(2)}) collective-permute-start(f32[256,128]{1,0:T(8,128)S(1)} %shard_map.90.refs_17_), channel_id=1, source_target_pairs={{0,2},{2,0},{4,6},{6,4},{1,3},{3,1},{5,7},{7,5},{8,10},{10,8},{12,... | collective-permute-start | bytes 393224 | tf_op jit(solution)/shard_map/ppermute | solution.py:753

commit v6 on v5

--- a/solution.py
+++ b/solution.py
@@ -205,13 +205,14 @@
         self.window = bz // 2 + 2 * GAUSSIAN_RIM
         self.window_rows = up8(self.window)
         self.out_z = bz // 2 + 2
-        self.top_rows = 2 * up8(bz // 16 + 2)
+        self.sent_top = up8(bz // 16 + 2)
+        self.top_rows = up8(2 * (bz // 16 + 2))
         self.top_z = bz // 16 + 2
         self.top_x, self.top_y = bx // 16 + 2, by // 16 + 2
         self.group = 16
         x_of, y_of = self.own_cells()
         rz = reach_four(bz)
-        self.top_left = padded(rz, self.top_rows // 2, bz)
+        self.top_left = padded(rz, self.sent_top, bz)
         rx, ry = reach_four(bx), reach_four(by)
         self.top_right, self.rest_right = [], []
         sx = restrict_weights(np.arange(bx), np.arange(-1, bx // 2 + 1))
@@ -251,6 +252,7 @@
             "out_cells": out_cells.reshape(-1, LANES),
             "coarse_dz": coarse_dz,
             "back": self.back_left,
+            "back_turned": self.back_left.T,
             "back_right": self.back_right,
             "spread_x": spread_x.reshape(-1, 16),
             "pick_x": pick_x[:, :, 0].reshape(-1, LANES),
@@ -323,9 +325,9 @@
                     valid = used
                 else:
                     row = np.arange(self.top_rows)
-                    side, at = row // (self.top_rows // 2), row % (self.top_rows // 2)
+                    side, at = row // self.top_z, row % self.top_z
                     cells = (place ^ side) * four[2] + at - 1
-                    valid = at < self.top_z
+                    valid = side < 2
                 hot = (np.arange(count)[:, None] == (cells % count)[None, :]) & valid[None, :]
                 hot = padded(hot, 16, cells.size)
                 pick.append(hot if axis == 2 else hot.reshape(16, 2, LANES))
@@ -406,7 +408,7 @@
 def start_kernel(plan, charges_ref, table_ref, own_ref, out_ref):
     _, _, bz = plan.brick
     rim, half = plan.rim, plan.half
-    top, size = None, plan.top_rows // 2
+    top, size = None, plan.sent_top
     left = split(table_ref[:size])
     for part in range(2):
         cells = charges_ref[:, part * half : (part + 1) * half, :].reshape(LANES, bz).T
@@ -450,8 +452,11 @@
     side_y_ref[rows:] = coarse
     out_ref[rows : rows + plan.window_rows] = coarse
     top = rows + plan.window_rows
-    out_ref[top : top + plan.top_rows // 2] = sent_ref[4 * rim :]
-    out_ref[top + plan.top_rows // 2 :] = got_ref[4 * rim :]
+    cells = plan.top_z
+    out_ref[top : top + cells] = sent_ref[4 * rim : 4 * rim + cells]
+    out_ref[top + cells : top + 2 * cells] = got_ref[4 * rim : 4 * rim + cells]
+    if plan.top_rows > 2 * cells:
+        out_ref[top + 2 * cells :] = jnp.zeros((plan.top_rows - 2 * cells, LANES), F32)
 
 
 def half_of(plan, flags_ref, strip_ref):
@@ -549,16 +554,15 @@
         params_ref[at : at + count, :count] = source[...]
 
 
-def coarse_weights_kernel(plan, terms, place_ref, table_ref, exponents_ref, amplitudes_ref, top_x_ref, top_y_ref,
+def coarse_weights_kernel(plan, terms, flags_ref, table_ref, exponents_ref, amplitudes_ref, top_x_ref, top_y_ref,
                           top_z_ref, params_ref, k1_ref, k1_low_ref, z1_ref, z1_low_ref, zc_ref, kc_ref):
     set_params(terms, exponents_ref, amplitudes_ref, (top_x_ref, top_y_ref, top_z_ref), params_ref)
     cells_ref = table_ref.at[pl.ds(plan.starts["coarse_cells"], 16)]
     at, count = plan.starts["out_cells"], plan.out_cells
     out_cells_ref = [table_ref[at + count * part : at + count * (part + 1)] for part in range(3)]
     dz_ref = table_ref.at[pl.ds(plan.starts["coarse_dz"], plan.window_rows)]
-    zc_ref[...], kc_ref[...] = top_weights(plan, terms, place_ref, params_ref, table_ref)
+    zc_ref[...], kc_ref[...] = top_weights(plan, terms, flags_ref, params_ref, table_ref)
     bx, by = plan.brick[0] // 2, plan.brick[1] // 2
-    even_x, even_y = place_ref[0] % 2 == 0, place_ref[1] % 2 == 0
     base = 3 * terms
 
     def squared(distance, count):
@@ -568,10 +572,11 @@
     x_out, y_out = out_cells_ref[0], out_cells_ref[1]
     squares_x = []
     for slot in range(3):
-        x_in = jnp.where(even_x, cells_ref[2 * slot : 2 * slot + 1], cells_ref[2 * slot + 1 : 2 * slot + 2])
+        x_in = pick(flags_ref, 0, cells_ref[2 * slot : 2 * slot + 1], cells_ref[2 * slot + 1 : 2 * slot + 2])
         used = cells_ref[7:8] if slot < 2 else cells_ref[8:9]
         squares_x.append(squared(x_in - x_out, bx * plan.counts[0]) + used)
-    toward = jnp.where(even_y, F32(by), F32(-by))
+    toward = jnp.full((1, LANES), by, F32)
+    toward = pick(flags_ref, 1, toward, -toward)
     for group, offset in enumerate((F32(0), -toward, F32(2 * by))):
         square_y = squared(cells_ref[6:7] + offset - y_out, by * plan.counts[1]) + out_cells_ref[2]
         for slot in range(3):
@@ -587,38 +592,44 @@
     for term in range(terms):
         exponent = params_ref[base + term : base + term + 1]
         scale = params_ref[base + 2 * terms + term : base + 2 * terms + term + 1]
-        z1_ref[term], z1_low_ref[term] = split(jnp.exp(-exponent * dz_ref[...]) * scale)
-
-
-def top_weights(plan, terms, place_ref, params_ref, table_ref):
+        value = dot_right(jnp.exp(-exponent * dz_ref[...]) * scale, exact_tables(plan, table_ref)("back", LANES))
+        z1_ref[term], z1_low_ref[term] = split(value)
+
+
+def top_weights(plan, terms, flags_ref, params_ref, table_ref):
     def chain(*factors):
         value = factors[0]
         for factor in factors[1:]:
             value = dot_split(split(value), split(factor))
         return value
 
-    def read(name, rows, at=0):
-        return table_ref[pl.ds(pl.multiple_of(plan.starts[name] + at * rows, 8), rows)]
+    def read(name, rows, axis=None, partner=0):
+        start = plan.starts[name]
+        if axis is None:
+            return table_ref[start : start + rows]
+        total, first = None, 3 + sum(plan.counts[:axis])
+        for place in range(plan.counts[axis]):
+            flag = flags_ref[first + (place ^ partner) : first + (place ^ partner) + 1]
+            value = table_ref[start + rows * place : start + rows * (place + 1)] * flag
+            total = value if total is None else total + value
+        return total
 
     size = 16
 
-    def along(axis, spread, pick, place):
+    def along(axis, spread, chosen, partner=0):
         top = params_ref[6 * terms + size * axis : 6 * terms + size * (axis + 1)]
-        value = chain(read(spread, size, place)[:, :size], top)[:, :size]
-        return chain(value, read(pick, size, place))
-
-    along_x = along(0, "spread_x", "pick_x", place_ref[0])
+        value = chain(read(spread, size, axis, partner)[:, :size], top)[:, :size]
+        return chain(value, read(chosen, size, axis, partner))
+
     lift_x, lift_y = (read(name, plan.out_cells)[:, :size] for name in ("lift_x", "lift_y"))
-    along_x = chain(lift_x, along_x)
+    along_x = chain(lift_x, along(0, "spread_x", "pick_x"))
     right = []
-    for partner in range(2):
-        place = place_ref[1] + partner * (1 - 2 * (place_ref[1] % 2))
-        along_y = along(1, "spread_y", ("pick_y", "pick_pair")[partner], place)
-        right.append(along_x * chain(lift_y, along_y))
+    for partner, chosen in enumerate(("pick_y", "pick_pair")):
+        right.append(along_x * chain(lift_y, along(1, "spread_y", chosen, partner)))
     top = params_ref[6 * terms + 2 * size : 6 * terms + 3 * size]
-    value = chain(read("spread_z", LANES, place_ref[2])[:, :size], top)[:, :size]
-    left = chain(value, read("pick_z", size, place_ref[2])[:, : plan.top_rows])
-    return left, jnp.concatenate(right, axis=1)
+    value = chain(read("spread_z", LANES, 2)[:, :size], top)[:, :size]
+    left = chain(value, read("pick_z", size, 2)[:, : plan.top_rows])
+    return dot_left(read("back_turned", LANES).astype(BF16), left), jnp.concatenate(right, axis=1)
 
 
 def sum_fine(terms, blocks, refs, at):
@@ -650,8 +661,7 @@
         piece = split(coarse[term * plan.out_cells : (term + 1) * plan.out_cells])
         level_one = level_one + dot_split(piece, (refs[0][term], refs[1][term]))
     table = exact_tables(plan, table_ref)
-    back = dot_right(level_one, table("back", LANES))
-    return dot_left(table("back_right", 2 * LANES)[:, : plan.out_cells], back)
+    return dot_left(table("back_right", 2 * LANES)[:, : plan.out_cells], level_one)
 
 
 def near_kernel(plan, terms, flags_ref, cells_ref, own_ref, first_ref, second_ref, kf_ref, kf_low_ref, k1_ref,
@@ -754,8 +764,13 @@
 
 
 def local_short(plan, charges, exponents, amplitudes, top_x, top_y, top_z):
-    where = jnp.stack([lax.axis_index(axis) for axis in ("gx", "gy", "gz")]).astype(jnp.int32)
-    flags = jnp.broadcast_to((where % 2).astype(F32)[:, None], (3, LANES))
+    row = lax.broadcasted_iota(jnp.int32, (3 + sum(plan.counts), LANES), 0)
+    flags, first = jnp.zeros(row.shape, F32), 3
+    for axis, name in enumerate(("gx", "gy", "gz")):
+        place = lax.axis_index(name).astype(jnp.int32)
+        flags = jnp.where(row == axis, (place % 2).astype(F32), flags)
+        flags = jnp.where(row == first + place, 1.0, flags)
+        first = first + plan.counts[axis]
     terms = exponents.shape[1]
     bx, by, bz = plan.brick
     rows, window = plan.fine_rows, plan.window_rows
@@ -763,7 +778,7 @@
 
     own, sent_z = call(
         bind(start_kernel, plan),
-        [(2, bz, LANES), (4 * plan.rim + plan.top_rows // 2, LANES)],
+        [(2, bz, LANES), (4 * plan.rim + plan.sent_top, LANES)],
         charges,
         jnp.asarray(np.concatenate([plan.top_left, *plan.top_right])),
         plain=True,
@@ -811,10 +826,9 @@
             (LANES, plan.top_rows),
             (plan.out_cells, 2 * LANES),
         ],
-        where,
+        flags,
         table,
         *small,
-        scalars=1,
         after=(sent_b,),
     )
     size = rows // 2 + window + plan.top_rows

time: 31.9 us -> 31.4 us (0.984)
  Pallas kernels: 12.3 us -> 11.9 us
    pallas_call x11, Pallas kernels: 12.3 us -> 11.9 us  [call(): pl.pallas_call(run, out_shape=[jax.ShapeDtypeStruct(kind, kept_as) if las...]
  transfers between devices with their start and end apart: 8 -> 8, of which waited for: 5 -> 5; matrix products, arithmetic and copies ran while one was open for 0% -> 0% of each run, Pallas kernels for 27% -> 26%
where the time goes in v6:
time: 31.4 us; the launch traced here: 31.2 us
  Pallas kernels  11.9 us (38%)
  starting transfers between devices  10.8 us (34%)
  waiting for transfers between devices  8.25 us (26%)
    pallas_call x11, Pallas kernels, call(): pl.pallas_call(run, out_shape=[jax.ShapeDtypeStruct(kind, kept_as) if las...  11.9 us
    ppermute x8, starting transfers between devices, pair(): return lax.ppermute(value, axis, [(i, i ^ bits) for i in range(count)])  10.8 us
    ppermute x8, waiting for transfers between devices, pair(): return lax.ppermute(value, axis, [(i, i ^ bits) for i in range(count)])  8.25 us
  transfers between devices with their start and end apart: 8, of which 5 were waited for; matrix products, arithmetic and copies ran while one was open for 0% of the time, Pallas kernels for 26%

profile of v6, /device:TPU:0, one launch (start us, length us, event | category | flops | bytes accessed | tf_op | source)
XLA Modules:
  0.0 31.2 jit_solution(15681756224050431496)
XLA Ops:
  0.0 1.4 %shard_map.82 = (f32[2,128,128]{2,1,0:T(8,128)S(1)}, f32[112,128]{1,0:T(8,128)S(1)}) custom-call(f32[16,16,128]{2,1,0:T(8,128)} %refs_0_.2, f32[272,128]{1,0:T(8,128)} %constant.49.clone.refs_1_), custom_call_target="tpu_custom_call" | custom-call | tf_op jit(solution)/shard_map/pallas_call | solution.py:748
  1.4 3.0 %collective-permute-start = (f32[112,128]{1,0:T(8,128)S(1)}, f32[112,128]{1,0:T(8,128)S(1)}, u32[]{:S(2)}, u32[]{:S(2)}) collective-permute-start(f32[112,128]{1,0:T(8,128)S(1)} %get-tuple-element.37.refs_6_.refs_2_), channel_id=1, source_target_pairs={{0,1},{1,0},{2,3},{3,2},{4,5},{5,4},{6,7},{7,6},{8,9},{9,8},{10,11... | collective-permute-start | bytes 172040 | tf_op jit(solution)/shard_map/ppermute | solution.py:763
  4.4 0.1 select_select_fusion.refs_0_
  4.5 1.4 %shard_map.83 = (f32[2400,128]{1,0:T(8,128)S(1)}, f32[2,4]{1,0:T(2,128)S(1)}, f32[2,4]{1,0:T(2,128)S(1)}, f32[4,4]{1,0:T(4,128)S(1)}, f32[4,4]{1,0:T(4,128)S(1)}, /*index=5*/f32[16,16]{1,0:T(8,128)S(1)}) custom-call(f32[2400,128]{1,0:T(8,128)} %constant.50.clone.refs_0_, f32[2,4]{1,0:T(2,128)} %refs_1_.2, f32[2,4]{1,0:T(2,128)} %refs_2_.1, f32[4,4]{1,0:T(4,128)} %refs_3_.1, ...), custom_call_target="tpu_custom_call" | custom-call | tf_op jit(solution)/shard_map/pallas_call | solution.py:748
  5.9 0.7 %collective-permute-done.refs_3_ = f32[112,128]{1,0:T(8,128)S(1)} collective-permute-done((f32[112,128]{1,0:T(8,128)S(1)}, f32[112,128]{1,0:T(8,128)S(1)}, u32[]{:S(2)}, u32[]{:S(2)}) %collective-permute-start) | collective-permute-done | bytes 57376 | tf_op jit(solution)/shard_map/ppermute | solution.py:763
  6.5 0.4 %shard_map.84 = (f32[2,144,128]{2,1,0:T(8,128)S(1)}, f32[256,128]{1,0:T(8,128)S(1)}, f32[144,128]{1,0:T(8,128)S(1)}, f32[232,128]{1,0:T(8,128)S(1)}) custom-call(f32[13,128]{1,0:T(8,128)S(1)} %select_select_fusion.refs_0_, f32[2,128,128]{2,1,0:T(8,128)S(1)} %get-tuple-element.36.refs_1_, f32[112,128]{1,0:T(8,128)S(1)} %get-tuple-element.37.refs_6_.refs_2_, ...), custom_call_target="tpu_custom_call" | custom-call | tf_op jit(solution)/shard_map/pallas_call | solution.py:748
  6.9 2.2 %collective-permute-start.1 = (f32[256,128]{1,0:T(8,128)S(1)}, f32[256,128]{1,0:T(8,128)S(1)}, u32[]{:S(2)}, u32[]{:S(2)}) collective-permute-start(f32[256,128]{1,0:T(8,128)S(1)} %get-tuple-element.40.refs_1_.refs_2_), channel_id=1, source_target_pairs={{0,8},{8,0},{16,24},{24,16},{1,9},{9,1},{17,25},{25,17},{2,10},{10... | collective-permute-start | bytes 393224 | tf_op jit(solution)/shard_map/ppermute | solution.py:763
  9.1 0.0 collective-permute-start.4
  9.1 2.9 %collective-permute-done.1.refs_2_.refs_3_ = f32[256,128]{1,0:T(8,128)S(1)} collective-permute-done((f32[256,128]{1,0:T(8,128)S(1)}, f32[256,128]{1,0:T(8,128)S(1)}, u32[]{:S(2)}, u32[]{:S(2)}) %collective-permute-start.1) | collective-permute-done | bytes 131104 | tf_op jit(solution)/shard_map/ppermute | solution.py:763
  12.0 0.1 shard_map.85
  12.2 0.1 collective-permute-start.5
  12.3 4.1 %collective-permute-start.2 = (f32[144,128]{1,0:T(8,128)S(1)}, f32[144,128]{1,0:T(8,128)S(1)}, u32[]{:S(2)}, u32[]{:S(2)}) collective-permute-start(f32[144,128]{1,0:T(8,128)S(1)} %get-tuple-element.42), channel_id=1, source_target_pairs={{0,24},{8,16},{16,8},{24,0},{1,25},{9,17},{17,9},{25,1},{2,26},{10... | collective-permute-start | bytes 221192 | tf_op jit(solution)/shard_map/ppermute | solution.py:763
  16.4 0.0 collective-permute-start.3
  16.4 1.8 %shard_map.86 = (f32[72,128]{1,0:T(8,128)S(1)}, bf16[448,1152]{1,0:T(8,128)(2,1)S(1)}, bf16[448,1152]{1,0:T(8,128)(2,1)S(1)}, bf16[4,88,128]{2,1,0:T(8,128)(2,1)...) custom-call(f32[13,128]{1,0:T(8,128)S(1)} %select_select_fusion.refs_0_, ...), custom_call_target="tpu_custom_call" | custom-call | tf_op jit(solution)/shard_map/pallas_call | solution.py:748
  18.2 0.6 %collective-permute-done.2.refs_4_ = f32[144,128]{1,0:T(8,128)S(1)} collective-permute-done((f32[144,128]{1,0:T(8,128)S(1)}, f32[144,128]{1,0:T(8,128)S(1)}, u32[]{:S(2)}, u32[]{:S(2)}) %collective-permute-start.2) | collective-permute-done | bytes 73760 | tf_op jit(solution)/shard_map/ppermute | solution.py:763
  18.8 0.0 collective-permute-done.4.refs_7_.refs_2_
  18.8 3.6 %collective-permute-done.3.refs_5_.refs_4_ = f32[112,128]{1,0:T(8,128)S(1)} collective-permute-done((f32[112,128]{1,0:T(8,128)S(1)}, f32[112,128]{1,0:T(8,128)S(1)}, u32[]{:S(2)}, u32[]{:S(2)}) %collective-permute-start.3) | collective-permute-done | bytes 57376 | tf_op jit(solution)/shard_map/ppermute | solution.py:763
  22.4 0.0 collective-permute-done.5.refs_8_.refs_3_
  22.4 0.1 shard_map.87
  22.5 1.0 %collective-permute-start.6 = (f32[184,128]{1,0:T(8,128)S(1)}, f32[184,128]{1,0:T(8,128)S(1)}, u32[]{:S(2)}, u32[]{:S(2)}) collective-permute-start(f32[184,128]{1,0:T(8,128)S(1)} %get-tuple-element.53.refs_3_.refs_11_.refs_4_), channel_id=1, source_target_pairs={{0,6},{2,4},{4,2},{6,0},{1,7},{3,5},{5,3},{7,1},{8,14},{10,12},{12... | collective-permute-start | bytes 282632 | tf_op jit(solution)/shard_map/ppermute | solution.py:763
  23.5 0.8 %shard_map.88 = (bf16[4,256,768]{2,1,0:T(8,128)(2,1)S(1)}, bf16[4,256,768]{2,1,0:T(8,128)(2,1)S(1)}, bf16[4,144,128]{2,1,0:T(8,128)(2,1)S(1)}, bf16[4,144,128]{2,1,0:T(8,128)(2,1)S(1)}) custom-call(f32[13,128]{1,0:T(8,128)S(1)} %select_select_fusion.refs_0_, f32[72,128]{1,0:T(8,128)S(1)} %get-tuple-element.52.refs_1_, ...), custom_call_target="tpu_custom_call" | custom-call | tf_op jit(solution)/shard_map/pallas_call | solution.py:748
  24.3 2.2 %shard_map.89 = (f32[4,256,144]{2,1,0:T(8,128)S(1)}, f32[448,88]{1,0:T(8,128)S(1)}, f32[256,128]{1,0:T(8,128)S(1)}, f32[448,88]{1,0:T(8,128)S(1)}) custom-call(f32[13,128]{1,0:T(8,128)S(1)} %select_select_fusion.refs_0_, f32[2,288,128]{2,1,0:T(8,128)S(1)} %get-tuple-element.51.refs_1_, f32[256,128]{1,0:T(8,128)S(1)} %get-tuple-element.40.refs_1_.refs_2_, ...), custom_call_target="tpu_custom_call" | custom-call | tf_op jit(solution)/shard_map/pallas_call | solution.py:748
  26.6 0.4 %collective-permute-done.6.refs_5_ = f32[184,128]{1,0:T(8,128)S(1)} collective-permute-done((f32[184,128]{1,0:T(8,128)S(1)}, f32[184,128]{1,0:T(8,128)S(1)}, u32[]{:S(2)}, u32[]{:S(2)}) %collective-permute-start.6) | collective-permute-done | bytes 94240 | tf_op jit(solution)/shard_map/ppermute | solution.py:763
  27.0 1.2 %shard_map.90.refs_17_ = f32[256,128]{1,0:T(8,128)S(1)} custom-call(f32[256,128]{1,0:T(8,128)S(1)} %get-tuple-element.65.refs_0_, f32[448,88]{1,0:T(8,128)S(1)} %get-tuple-element.66.refs_1_, f32[232,128]{1,0:T(8,128)S(1)} %collective-permute-done.4.refs_7_.refs_2_, f32[160,128]{1,0:T(8,128)S(1)} %collective-permute-done.5.refs_8_.refs_3_, ...), custom_call_target="tpu_custom_call" | custom-call | tf_op jit(solution)/shard_map/pallas_call | solution.py:748
  28.2 0.5 %collective-permute-start.7 = (f32[256,128]{1,0:T(8,128)S(1)}, f32[256,128]{1,0:T(8,128)S(1)}, u32[]{:S(2)}, u32[]{:S(2)}) collective-permute-start(f32[256,128]{1,0:T(8,128)S(1)} %shard_map.90.refs_17_), channel_id=1, source_target_pairs={{0,2},{2,0},{4,6},{6,4},{1,3},{3,1},{5,7},{7,5},{8,10},{10,8},{12,... | collective-permute-start | bytes 393224 | tf_op jit(solution)/shard_map/ppermute | solution.py:763
  28.7 1.8 %shard_map.91.refs_0_ = f32[256,128]{1,0:T(8,128)S(1)} custom-call(f32[4,256,144]{2,1,0:T(8,128)S(1)} %get-tuple-element.60.refs_0_, f32[448,88]{1,0:T(8,128)S(1)} %get-tuple-element.61.refs_1_, f32[232,128]{1,0:T(8,128)S(1)} %collective-permute-done.4.refs_7_.refs_2_, f32[160,128]{1,0:T(8,128)S(1)} %collective-permute-done.5.refs_8_.refs_3_, ...), custom_call_target="tpu_custom_call" | custom-call | tf_op jit(solution)/shard_map/pallas_call | solution.py:748
  30.5 0.0 collective-permute-done.7.refs_1_
  30.5 0.7 %shard_map.92 = f32[16,16,128]{2,1,0:T(8,128)} custom-call(f32[256,128]{1,0:T(8,128)S(1)} %shard_map.91.refs_0_, f32[256,128]{1,0:T(8,128)S(1)} %collective-permute-done.7.refs_1_), custom_call_target="tpu_custom_call" | custom-call | tf_op jit(solution)/shard_map/pallas_call | solution.py:748
  (4 shorter events, 0.0 us)
Async XLA Ops:
  1.4 5.1 %collective-permute-start = (f32[112,128]{1,0:T(8,128)S(1)}, f32[112,128]{1,0:T(8,128)S(1)}, u32[]{:S(2)}, u32[]{:S(2)}) collective-permute-start(f32[112,128]{1,0:T(8,128)S(1)} %get-tuple-element.37.refs_6_.refs_2_), channel_id=1, source_target_pairs={{0,1},{1,0},{2,3},{3,2},{4,5},{5,4},{6,7},{7,6},{8,9},{9,8},{10,11... | collective-permute-start | bytes 172040 | tf_op jit(solution)/shard_map/ppermute | solution.py:763
  6.9 5.1 %collective-permute-start.1 = (f32[256,128]{1,0:T(8,128)S(1)}, f32[256,128]{1,0:T(8,128)S(1)}, u32[]{:S(2)}, u32[]{:S(2)}) collective-permute-start(f32[256,128]{1,0:T(8,128)S(1)} %get-tuple-element.40.refs_1_.refs_2_), channel_id=1, source_target_pairs={{0,8},{8,0},{16,24},{24,16},{1,9},{9,1},{17,25},{25,17},{2,10},{10... | collective-permute-start | bytes 393224 | tf_op jit(solution)/shard_map/ppermute | solution.py:763
  9.1 9.7 %collective-permute-start.4 = (f32[232,128]{1,0:T(8,128)S(1)}, f32[232,128]{1,0:T(8,128)S(1)}, u32[]{:S(2)}, u32[]{:S(2)}) collective-permute-start(f32[232,128]{1,0:T(8,128)S(1)} %get-tuple-element.49), channel_id=1, source_target_pairs={{0,6},{2,4},{4,2},{6,0},{1,7},{3,5},{5,3},{7,1},{8,14},{10,12},{12... | collective-permute-start | bytes 356360 | tf_op jit(solution)/shard_map/ppermute | solution.py:763
  12.2 10.2 %collective-permute-start.5 = (f32[160,128]{1,0:T(8,128)S(1)}, f32[160,128]{1,0:T(8,128)S(1)}, u32[]{:S(2)}, u32[]{:S(2)}) collective-permute-start(f32[160,128]{1,0:T(8,128)S(1)} %get-tuple-element.50), channel_id=1, source_target_pairs={{0,6},{2,4},{4,2},{6,0},{1,7},{3,5},{5,3},{7,1},{8,14},{10,12},{12... | collective-permute-start | bytes 245768 | tf_op jit(solution)/shard_map/ppermute | solution.py:763
  12.3 6.5 %collective-permute-start.2 = (f32[144,128]{1,0:T(8,128)S(1)}, f32[144,128]{1,0:T(8,128)S(1)}, u32[]{:S(2)}, u32[]{:S(2)}) collective-permute-start(f32[144,128]{1,0:T(8,128)S(1)} %get-tuple-element.42), channel_id=1, source_target_pairs={{0,24},{8,16},{16,8},{24,0},{1,25},{9,17},{17,9},{25,1},{2,26},{10... | collective-permute-start | bytes 221192 | tf_op jit(solution)/shard_map/ppermute | solution.py:763
  16.4 6.0 %collective-permute-start.3 = (f32[112,128]{1,0:T(8,128)S(1)}, f32[112,128]{1,0:T(8,128)S(1)}, u32[]{:S(2)}, u32[]{:S(2)}) collective-permute-start(f32[112,128]{1,0:T(8,128)S(1)} %get-tuple-element.41.refs_7_.refs_2_), channel_id=1, source_target_pairs={{0,16},{8,24},{16,0},{24,8},{1,17},{9,25},{17,1},{25,9},{2,18},{10... | collective-permute-start | bytes 172040 | tf_op jit(solution)/shard_map/ppermute | solution.py:763
  22.5 4.5 %collective-permute-start.6 = (f32[184,128]{1,0:T(8,128)S(1)}, f32[184,128]{1,0:T(8,128)S(1)}, u32[]{:S(2)}, u32[]{:S(2)}) collective-permute-start(f32[184,128]{1,0:T(8,128)S(1)} %get-tuple-element.53.refs_3_.refs_11_.refs_4_), channel_id=1, source_target_pairs={{0,6},{2,4},{4,2},{6,0},{1,7},{3,5},{5,3},{7,1},{8,14},{10,12},{12... | collective-permute-start | bytes 282632 | tf_op jit(solution)/shard_map/ppermute | solution.py:763
  28.2 2.3 %collective-permute-start.7 = (f32[256,128]{1,0:T(8,128)S(1)}, f32[256,128]{1,0:T(8,128)S(1)}, u32[]{:S(2)}, u32[]{:S(2)}) collective-permute-start(f32[256,128]{1,0:T(8,128)S(1)} %shard_map.90.refs_17_), channel_id=1, source_target_pairs={{0,2},{2,0},{4,6},{6,4},{1,3},{3,1},{5,7},{7,5},{8,10},{10,8},{12,... | collective-permute-start | bytes 393224 | tf_op jit(solution)/shard_map/ppermute | solution.py:763

commit v7 on v6

--- a/solution.py
+++ b/solution.py
@@ -664,20 +664,22 @@
     return dot_left(table("back_right", 2 * LANES)[:, : plan.out_cells], level_one)
 
 
-def near_kernel(plan, terms, flags_ref, cells_ref, own_ref, first_ref, second_ref, kf_ref, kf_low_ref, k1_ref,
-                k1_low_ref, zf_ref, zf_low_ref, fine_ref, coarse_ref, give_fine_ref, give_coarse_ref):
+def near_kernel(plan, terms, flags_ref, cells_ref, own_ref, first_ref, second_ref, side_ref, strip_ref, kf_ref,
+                kf_low_ref, k1_ref, k1_low_ref, zf_ref, zf_low_ref, fine_ref, coarse_ref, give_fine_ref,
+                give_coarse_ref):
     rows, window = plan.fine_rows, plan.window_rows
     kf, k1 = (kf_ref, kf_low_ref), (k1_ref, k1_low_ref)
-    groups = [jnp.concatenate([cells_ref[part, :rows], cells_ref[part, rows:]], axis=1) for part in range(2)]
+    cells = [cells_ref[part, at : at + rows] for part in range(2) for at in (0, rows)]
     near = [own_ref[rows : rows + window], first_ref[rows : rows + window], second_ref[:window]]
-    near = jnp.concatenate(near, axis=1)
-    other = [pick(flags_ref, 1, cells_ref[1, at : at + rows], cells_ref[0, at : at + rows]) for at in (0, rows)]
-    other = jnp.concatenate(other, axis=1)
-    give_fine_ref[...] = fine_potential(sum_fine(terms, other, kf, 4), (zf_ref, zf_low_ref))
-    give_coarse_ref[...] = sum_coarse(near, k1, 3)
-    for term, value in enumerate(sum_fine(terms, jnp.concatenate(groups, axis=1), kf, 0)):
+    early = [side_ref[rows:], strip_ref[rows // 2 :]]
+    other = [pick(flags_ref, 1, cells[2 + block], cells[block]) for block in range(2)]
+    other = sum_fine(terms, jnp.concatenate(other, axis=1), kf, 4)
+    give_fine_ref[...] = fine_potential(other, (zf_ref, zf_low_ref))
+    give_coarse_ref[...] = sum_coarse(jnp.concatenate(near + early, axis=1), k1, 3)
+    cells = jnp.concatenate(cells + [side_ref[:rows]], axis=1)
+    for term, value in enumerate(sum_fine(terms, cells, kf, 0)):
         fine_ref[term] = value
-    coarse_ref[...] = sum_coarse(near, k1, 0)
+    coarse_ref[...] = sum_coarse(jnp.concatenate(near + early, axis=1), k1, 0)
 
 
 def top_charges(plan, sent_ref, got_ref, zc_ref):
@@ -686,29 +688,26 @@
     return dot_split(split(zc_ref[...]), split(top))
 
 
-def arrived(plan, side_ref, strip_ref, got_ref):
-    rows = plan.fine_rows
-    pieces = [side_ref[rows:], strip_ref[rows // 2 :], got_ref[rows // 2 : rows // 2 + plan.window_rows]]
-    return jnp.concatenate(pieces, axis=1)
-
-
-def give_kernel(plan, terms, fine_ref, coarse_ref, side_ref, strip_ref, sent_ref, got_ref, k1_ref, k1_low_ref,
-                z1_ref, z1_low_ref, zc_ref, kc_ref, table_ref, out_ref):
-    coarse = coarse_ref[...] + sum_coarse(arrived(plan, side_ref, strip_ref, got_ref), (k1_ref, k1_low_ref), 6)
+def last_cells(plan, got_ref):
+    return got_ref[plan.fine_rows // 2 : plan.fine_rows // 2 + plan.window_rows]
+
+
+def give_kernel(plan, terms, fine_ref, coarse_ref, sent_ref, got_ref, k1_ref, k1_low_ref, z1_ref, z1_low_ref,
+                zc_ref, kc_ref, table_ref, out_ref):
+    coarse = coarse_ref[...] + sum_coarse(last_cells(plan, got_ref), (k1_ref, k1_low_ref), 8)
     top = top_charges(plan, sent_ref, got_ref, zc_ref)
     out_ref[...] = fine_ref[...] + coarse_potential(
         plan, terms, coarse, (z1_ref, z1_low_ref), top, kc_ref[:, LANES:], table_ref
     )
 
 
-def keep_kernel(plan, terms, fine_ref, coarse_ref, side_ref, strip_ref, sent_ref, got_ref, kf_ref, kf_low_ref,
-                k1_ref, k1_low_ref, zf_ref, zf_low_ref, z1_ref, z1_low_ref, zc_ref, kc_ref, table_ref, out_ref):
-    rows = plan.fine_rows
-    strips = jnp.concatenate(halves(strip_ref[: rows // 2], got_ref[: rows // 2]), axis=0)
-    blocks = jnp.concatenate([side_ref[:rows], strips], axis=1)
-    fine = sum_fine(terms, blocks, (kf_ref, kf_low_ref), 4)
+def keep_kernel(plan, terms, fine_ref, coarse_ref, strip_ref, sent_ref, got_ref, kf_ref, kf_low_ref, k1_ref,
+                k1_low_ref, zf_ref, zf_low_ref, z1_ref, z1_low_ref, zc_ref, kc_ref, table_ref, out_ref):
+    half = plan.fine_rows // 2
+    strips = jnp.concatenate(halves(strip_ref[:half], got_ref[:half]), axis=0)
+    fine = sum_fine(terms, strips, (kf_ref, kf_low_ref), 5)
     fine = [fine_ref[term] + value for term, value in enumerate(fine)]
-    coarse = coarse_ref[...] + sum_coarse(arrived(plan, side_ref, strip_ref, got_ref), (k1_ref, k1_low_ref), 3)
+    coarse = coarse_ref[...] + sum_coarse(last_cells(plan, got_ref), (k1_ref, k1_low_ref), 5)
     top = top_charges(plan, sent_ref, got_ref, zc_ref)
     out_ref[...] = fine_potential(fine, (zf_ref, zf_low_ref)) + coarse_potential(
         plan, terms, coarse, (z1_ref, z1_low_ref), top, kc_ref[:, :LANES], table_ref
@@ -831,6 +830,15 @@
         *small,
         after=(sent_b,),
     )
+    kf = ((terms, 2 * LANES, 6 * LANES), BF16)
+    *kf, zf, zf_low = call(
+        bind(fine_weights_kernel, plan, terms),
+        [kf, kf, ((terms, rows, LANES), BF16), ((terms, rows, LANES), BF16)],
+        flags,
+        params,
+        table,
+        after=(sent_b,),
+    )
     size = rows // 2 + window + plan.top_rows
     cells, sent_c = call(
         bind(stack_kernel, plan),
@@ -841,18 +849,9 @@
         got_a,
         got_x,
         got_b,
-        after=(z1, got_y, got_s),
+        after=(z1, zf, got_y, got_s),
     )
     got_c = pair(sent_c, "gy", 3)
-    kf = ((terms, 2 * LANES, 6 * LANES), BF16)
-    *kf, zf, zf_low = call(
-        bind(fine_weights_kernel, plan, terms),
-        [kf, kf, ((terms, rows, LANES), BF16), ((terms, rows, LANES), BF16)],
-        flags,
-        params,
-        table,
-        after=(sent_c,),
-    )
     give = (2 * LANES, bz)
     fine_sum, coarse_sum, give_fine, give_coarse = call(
         bind(near_kernel, plan, terms),
@@ -862,6 +861,8 @@
         sent_a,
         got_a,
         got_b,
+        got_y,
+        got_s,
         *kf,
         *k1,
         zf,
@@ -870,7 +871,7 @@
     )
     ends = (z1, z1_low, zc, kc, table)
     (sent_d,) = call(
-        bind(give_kernel, plan, terms), [give], give_fine, give_coarse, got_y, got_s, sent_c, got_c, *k1, *ends
+        bind(give_kernel, plan, terms), [give], give_fine, give_coarse, sent_c, got_c, *k1, *ends
     )
     got_d = pair(sent_d, "gy", 1)
     (kept,) = call(
@@ -878,7 +879,6 @@
         [give],
         fine_sum,
         coarse_sum,
-        got_y,
         got_s,
         sent_c,
         got_c,

time: 31.4 us -> 30.9 us (0.984)
  waiting for transfers between devices: 8.25 us -> 7.59 us
    ppermute x8, waiting for transfers between devices: 8.25 us -> 7.59 us  [pair(): return lax.ppermute(value, axis, [(i, i ^ bits) for i in range(count)])]
  transfers between devices with their start and end apart: 8 -> 8, of which waited for: 5 -> 4; matrix products, arithmetic and copies ran while one was open for 0% -> 0% of each run, Pallas kernels for 26% -> 28%
where the time goes in v7:
time: 30.9 us; the launch traced here: 30.7 us
  Pallas kernels  12 us (39%)
  starting transfers between devices  10.8 us (35%)
  waiting for transfers between devices  7.59 us (25%)
    pallas_call x11, Pallas kernels, call(): pl.pallas_call(run, out_shape=[jax.ShapeDtypeStruct(kind, kept_as) if las...  12 us
    ppermute x8, starting transfers between devices, pair(): return lax.ppermute(value, axis, [(i, i ^ bits) for i in range(count)])  10.8 us
    ppermute x8, waiting for transfers between devices, pair(): return lax.ppermute(value, axis, [(i, i ^ bits) for i in range(count)])  7.59 us
  transfers between devices with their start and end apart: 8, of which 4 were waited for; matrix products, arithmetic and copies ran while one was open for 0% of the time, Pallas kernels for 28%

profile of v7, /device:TPU:0, one launch (start us, length us, event | category | flops | bytes accessed | tf_op | source)
XLA Modules:
  0.0 30.7 jit_solution(9039245173053654703)
XLA Ops:
  0.0 1.4 %shard_map.82 = (f32[2,128,128]{2,1,0:T(8,128)S(1)}, f32[112,128]{1,0:T(8,128)S(1)}) custom-call(f32[16,16,128]{2,1,0:T(8,128)} %refs_0_.2, f32[272,128]{1,0:T(8,128)} %constant.49.clone.refs_1_), custom_call_target="tpu_custom_call" | custom-call | tf_op jit(solution)/shard_map/pallas_call | solution.py:747
  1.4 3.0 %collective-permute-start = (f32[112,128]{1,0:T(8,128)S(1)}, f32[112,128]{1,0:T(8,128)S(1)}, u32[]{:S(2)}, u32[]{:S(2)}) collective-permute-start(f32[112,128]{1,0:T(8,128)S(1)} %get-tuple-element.37.refs_6_.refs_2_), channel_id=1, source_target_pairs={{0,1},{1,0},{2,3},{3,2},{4,5},{5,4},{6,7},{7,6},{8,9},{9,8},{10,11... | collective-permute-start | bytes 172040 | tf_op jit(solution)/shard_map/ppermute | solution.py:762
  4.4 0.1 select_select_fusion.refs_0_
  4.5 1.4 %shard_map.83 = (f32[2400,128]{1,0:T(8,128)S(1)}, f32[2,4]{1,0:T(2,128)S(1)}, f32[2,4]{1,0:T(2,128)S(1)}, f32[4,4]{1,0:T(4,128)S(1)}, f32[4,4]{1,0:T(4,128)S(1)}, /*index=5*/f32[16,16]{1,0:T(8,128)S(1)}) custom-call(f32[2400,128]{1,0:T(8,128)} %constant.50.clone.refs_0_, f32[2,4]{1,0:T(2,128)} %refs_1_.2, f32[2,4]{1,0:T(2,128)} %refs_2_.1, f32[4,4]{1,0:T(4,128)} %refs_3_.1, ...), custom_call_target="tpu_custom_call" | custom-call | tf_op jit(solution)/shard_map/pallas_call | solution.py:747
  5.9 0.7 %collective-permute-done.refs_3_ = f32[112,128]{1,0:T(8,128)S(1)} collective-permute-done((f32[112,128]{1,0:T(8,128)S(1)}, f32[112,128]{1,0:T(8,128)S(1)}, u32[]{:S(2)}, u32[]{:S(2)}) %collective-permute-start) | collective-permute-done | bytes 57376 | tf_op jit(solution)/shard_map/ppermute | solution.py:762
  6.5 0.4 %shard_map.84 = (f32[2,144,128]{2,1,0:T(8,128)S(1)}, f32[256,128]{1,0:T(8,128)S(1)}, f32[144,128]{1,0:T(8,128)S(1)}, f32[232,128]{1,0:T(8,128)S(1)}) custom-call(f32[13,128]{1,0:T(8,128)S(1)} %select_select_fusion.refs_0_, f32[2,128,128]{2,1,0:T(8,128)S(1)} %get-tuple-element.36.refs_1_, f32[112,128]{1,0:T(8,128)S(1)} %get-tuple-element.37.refs_6_.refs_2_, ...), custom_call_target="tpu_custom_call" | custom-call | tf_op jit(solution)/shard_map/pallas_call | solution.py:747
  6.9 2.2 %collective-permute-start.1 = (f32[256,128]{1,0:T(8,128)S(1)}, f32[256,128]{1,0:T(8,128)S(1)}, u32[]{:S(2)}, u32[]{:S(2)}) collective-permute-start(f32[256,128]{1,0:T(8,128)S(1)} %get-tuple-element.40.refs_1_.refs_2_), channel_id=1, source_target_pairs={{0,8},{8,0},{16,24},{24,16},{1,9},{9,1},{17,25},{25,17},{2,10},{10... | collective-permute-start | bytes 393224 | tf_op jit(solution)/shard_map/ppermute | solution.py:762
  9.1 0.0 collective-permute-start.4
  9.1 2.9 %collective-permute-done.1.refs_2_.refs_3_ = f32[256,128]{1,0:T(8,128)S(1)} collective-permute-done((f32[256,128]{1,0:T(8,128)S(1)}, f32[256,128]{1,0:T(8,128)S(1)}, u32[]{:S(2)}, u32[]{:S(2)}) %collective-permute-start.1) | collective-permute-done | bytes 131104 | tf_op jit(solution)/shard_map/ppermute | solution.py:762
  12.0 0.1 shard_map.85
  12.2 0.1 collective-permute-start.5
  12.3 4.1 %collective-permute-start.2 = (f32[144,128]{1,0:T(8,128)S(1)}, f32[144,128]{1,0:T(8,128)S(1)}, u32[]{:S(2)}, u32[]{:S(2)}) collective-permute-start(f32[144,128]{1,0:T(8,128)S(1)} %get-tuple-element.42), channel_id=1, source_target_pairs={{0,24},{8,16},{16,8},{24,0},{1,25},{9,17},{17,9},{25,1},{2,26},{10... | collective-permute-start | bytes 221192 | tf_op jit(solution)/shard_map/ppermute | solution.py:762
  16.4 0.0 collective-permute-start.3
  16.4 1.8 %shard_map.86 = (f32[72,128]{1,0:T(8,128)S(1)}, bf16[448,1152]{1,0:T(8,128)(2,1)S(1)}, bf16[448,1152]{1,0:T(8,128)(2,1)S(1)}, bf16[4,88,128]{2,1,0:T(8,128)(2,1)...) custom-call(f32[13,128]{1,0:T(8,128)S(1)} %select_select_fusion.refs_0_, ...), custom_call_target="tpu_custom_call" | custom-call | tf_op jit(solution)/shard_map/pallas_call | solution.py:747
  18.2 0.8 %shard_map.87 = (bf16[4,256,768]{2,1,0:T(8,128)(2,1)S(1)}, bf16[4,256,768]{2,1,0:T(8,128)(2,1)S(1)}, bf16[4,144,128]{2,1,0:T(8,128)(2,1)S(1)}, bf16[4,144,128]{2,1,0:T(8,128)(2,1)S(1)}) custom-call(f32[13,128]{1,0:T(8,128)S(1)} %select_select_fusion.refs_0_, f32[72,128]{1,0:T(8,128)S(1)} %get-tuple-element.49.refs_1_, ...), custom_call_target="tpu_custom_call" | custom-call | tf_op jit(solution)/shard_map/pallas_call | solution.py:747
  19.0 0.0 collective-permute-done.2.refs_4_
  19.0 0.0 collective-permute-done.4.refs_8_.refs_5_
  19.0 3.4 %collective-permute-done.3.refs_5_.refs_4_ = f32[112,128]{1,0:T(8,128)S(1)} collective-permute-done((f32[112,128]{1,0:T(8,128)S(1)}, f32[112,128]{1,0:T(8,128)S(1)}, u32[]{:S(2)}, u32[]{:S(2)}) %collective-permute-start.3) | collective-permute-done | bytes 57376 | tf_op jit(solution)/shard_map/ppermute | solution.py:762
  22.4 0.0 collective-permute-done.5.refs_9_.refs_6_.refs_2_
  22.4 0.1 shard_map.88
  22.5 1.0 %collective-permute-start.6 = (f32[184,128]{1,0:T(8,128)S(1)}, f32[184,128]{1,0:T(8,128)S(1)}, u32[]{:S(2)}, u32[]{:S(2)}) collective-permute-start(f32[184,128]{1,0:T(8,128)S(1)} %get-tuple-element.59.refs_13_.refs_2_.refs_3_), channel_id=1, source_target_pairs={{0,6},{2,4},{4,2},{6,0},{1,7},{3,5},{5,3},{7,1},{8,14},{10,12},{12... | collective-permute-start | bytes 282632 | tf_op jit(solution)/shard_map/ppermute | solution.py:762
  23.5 2.9 %shard_map.89 = (f32[4,256,144]{2,1,0:T(8,128)S(1)}, f32[448,88]{1,0:T(8,128)S(1)}, f32[256,128]{1,0:T(8,128)S(1)}, f32[448,88]{1,0:T(8,128)S(1)}) custom-call(f32[13,128]{1,0:T(8,128)S(1)} %select_select_fusion.refs_0_, f32[2,288,128]{2,1,0:T(8,128)S(1)} %get-tuple-element.53.refs_1_, f32[256,128]{1,0:T(8,128)S(1)} %get-tuple-element.40.refs_1_.refs_2_, ...), custom_call_target="tpu_custom_call" | custom-call | tf_op jit(solution)/shard_map/pallas_call | solution.py:747
  26.4 0.6 %collective-permute-done.6.refs_3_.refs_4_ = f32[184,128]{1,0:T(8,128)S(1)} collective-permute-done((f32[184,128]{1,0:T(8,128)S(1)}, f32[184,128]{1,0:T(8,128)S(1)}, u32[]{:S(2)}, u32[]{:S(2)}) %collective-permute-start.6) | collective-permute-done | bytes 94240 | tf_op jit(solution)/shard_map/ppermute | solution.py:762
  27.0 1.0 %shard_map.90.refs_16_ = f32[256,128]{1,0:T(8,128)S(1)} custom-call(f32[256,128]{1,0:T(8,128)S(1)} %get-tuple-element.65.refs_0_, f32[448,88]{1,0:T(8,128)S(1)} %get-tuple-element.66.refs_1_, f32[184,128]{1,0:T(8,128)S(1)} %get-tuple-element.59.refs_13_.refs_2_.refs_3_, f32[184,128]{1,0:T(8,128)S(1)} %collective-permute-done.6.refs_3_.refs_4_, ...), custom_call_target="tpu_custom_call" | custom-call | tf_op jit(solution)/shard_map/pallas_call | solution.py:747
  28.0 0.5 %collective-permute-start.7 = (f32[256,128]{1,0:T(8,128)S(1)}, f32[256,128]{1,0:T(8,128)S(1)}, u32[]{:S(2)}, u32[]{:S(2)}) collective-permute-start(f32[256,128]{1,0:T(8,128)S(1)} %shard_map.90.refs_16_), channel_id=1, source_target_pairs={{0,2},{2,0},{4,6},{6,4},{1,3},{3,1},{5,7},{7,5},{8,10},{10,8},{12,... | collective-permute-start | bytes 393224 | tf_op jit(solution)/shard_map/ppermute | solution.py:762
  28.4 1.6 %shard_map.91.refs_0_ = f32[256,128]{1,0:T(8,128)S(1)} custom-call(f32[4,256,144]{2,1,0:T(8,128)S(1)} %get-tuple-element.60.refs_0_, f32[448,88]{1,0:T(8,128)S(1)} %get-tuple-element.61.refs_1_, f32[160,128]{1,0:T(8,128)S(1)} %collective-permute-done.5.refs_9_.refs_6_.refs_2_, f32[184,128]{1,0:T(8,128)S(1)} %get-tuple-element.59.refs_13_.refs_2_.refs_3_, ...), custom_call_target="tpu_custom_call" | custom-call | tf_op jit(solution)/shard_map/pallas_call | solution.py:747
  30.0 0.0 collective-permute-done.7.refs_1_
  30.0 0.7 %shard_map.92 = f32[16,16,128]{2,1,0:T(8,128)} custom-call(f32[256,128]{1,0:T(8,128)S(1)} %shard_map.91.refs_0_, f32[256,128]{1,0:T(8,128)S(1)} %collective-permute-done.7.refs_1_), custom_call_target="tpu_custom_call" | custom-call | tf_op jit(solution)/shard_map/pallas_call | solution.py:747
  (4 shorter events, 0.0 us)
Async XLA Ops:
  1.4 5.1 %collective-permute-start = (f32[112,128]{1,0:T(8,128)S(1)}, f32[112,128]{1,0:T(8,128)S(1)}, u32[]{:S(2)}, u32[]{:S(2)}) collective-permute-start(f32[112,128]{1,0:T(8,128)S(1)} %get-tuple-element.37.refs_6_.refs_2_), channel_id=1, source_target_pairs={{0,1},{1,0},{2,3},{3,2},{4,5},{5,4},{6,7},{7,6},{8,9},{9,8},{10,11... | collective-permute-start | bytes 172040 | tf_op jit(solution)/shard_map/ppermute | solution.py:762
  6.9 5.1 %collective-permute-start.1 = (f32[256,128]{1,0:T(8,128)S(1)}, f32[256,128]{1,0:T(8,128)S(1)}, u32[]{:S(2)}, u32[]{:S(2)}) collective-permute-start(f32[256,128]{1,0:T(8,128)S(1)} %get-tuple-element.40.refs_1_.refs_2_), channel_id=1, source_target_pairs={{0,8},{8,0},{16,24},{24,16},{1,9},{9,1},{17,25},{25,17},{2,10},{10... | collective-permute-start | bytes 393224 | tf_op jit(solution)/shard_map/ppermute | solution.py:762
  9.1 9.9 %collective-permute-start.4 = (f32[232,128]{1,0:T(8,128)S(1)}, f32[232,128]{1,0:T(8,128)S(1)}, u32[]{:S(2)}, u32[]{:S(2)}) collective-permute-start(f32[232,128]{1,0:T(8,128)S(1)} %get-tuple-element.51), channel_id=1, source_target_pairs={{0,6},{2,4},{4,2},{6,0},{1,7},{3,5},{5,3},{7,1},{8,14},{10,12},{12... | collective-permute-start | bytes 356360 | tf_op jit(solution)/shard_map/ppermute | solution.py:762
  12.2 10.2 %collective-permute-start.5 = (f32[160,128]{1,0:T(8,128)S(1)}, f32[160,128]{1,0:T(8,128)S(1)}, u32[]{:S(2)}, u32[]{:S(2)}) collective-permute-start(f32[160,128]{1,0:T(8,128)S(1)} %get-tuple-element.52), channel_id=1, source_target_pairs={{0,6},{2,4},{4,2},{6,0},{1,7},{3,5},{5,3},{7,1},{8,14},{10,12},{12... | collective-permute-start | bytes 245768 | tf_op jit(solution)/shard_map/ppermute | solution.py:762
  12.3 6.7 %collective-permute-start.2 = (f32[144,128]{1,0:T(8,128)S(1)}, f32[144,128]{1,0:T(8,128)S(1)}, u32[]{:S(2)}, u32[]{:S(2)}) collective-permute-start(f32[144,128]{1,0:T(8,128)S(1)} %get-tuple-element.42), channel_id=1, source_target_pairs={{0,24},{8,16},{16,8},{24,0},{1,25},{9,17},{17,9},{25,1},{2,26},{10... | collective-permute-start | bytes 221192 | tf_op jit(solution)/shard_map/ppermute | solution.py:762
  16.4 6.0 %collective-permute-start.3 = (f32[112,128]{1,0:T(8,128)S(1)}, f32[112,128]{1,0:T(8,128)S(1)}, u32[]{:S(2)}, u32[]{:S(2)}) collective-permute-start(f32[112,128]{1,0:T(8,128)S(1)} %get-tuple-element.41.refs_7_.refs_3_.refs_2_), channel_id=1, source_target_pairs={{0,16},{8,24},{16,0},{24,8},{1,17},{9,25},{17,1},{25,9},{2,18},{10... | collective-permute-start | bytes 172040 | tf_op jit(solution)/shard_map/ppermute | solution.py:762
  22.5 4.5 %collective-permute-start.6 = (f32[184,128]{1,0:T(8,128)S(1)}, f32[184,128]{1,0:T(8,128)S(1)}, u32[]{:S(2)}, u32[]{:S(2)}) collective-permute-start(f32[184,128]{1,0:T(8,128)S(1)} %get-tuple-element.59.refs_13_.refs_2_.refs_3_), channel_id=1, source_target_pairs={{0,6},{2,4},{4,2},{6,0},{1,7},{3,5},{5,3},{7,1},{8,14},{10,12},{12... | collective-permute-start | bytes 282632 | tf_op jit(solution)/shard_map/ppermute | solution.py:762
  28.0 2.0 %collective-permute-start.7 = (f32[256,128]{1,0:T(8,128)S(1)}, f32[256,128]{1,0:T(8,128)S(1)}, u32[]{:S(2)}, u32[]{:S(2)}) collective-permute-start(f32[256,128]{1,0:T(8,128)S(1)} %shard_map.90.refs_16_), channel_id=1, source_target_pairs={{0,2},{2,0},{4,6},{6,4},{1,3},{3,1},{5,7},{7,5},{8,10},{10,8},{12,... | collective-permute-start | bytes 393224 | tf_op jit(solution)/shard_map/ppermute | solution.py:762
